TPU v7x, 128 devices: a whole 4x4x4 slice. The times are simulated.
128 devices in a mesh: depth: 16 (over y, z_lo, core), azim: 8 (over z_hi, x).
Axes of the slice: x: 4, y: 4, z: 4 (z_hi: 2, z_lo: 2; z = z_hi * 2 + z_lo), core: 2. Of those that a mesh axis runs over, the one named last changes fastest.
Arguments:
- fluid_pos: float32 [2, 16, 32, 128], P(None, 'depth', 'azim'), may hold values from 0 to 1
- fluid_vel: float32 [2, 16, 32, 128], P(None, 'depth', 'azim'), may hold values from -4 to 4
- fluid_mass: float32 [16, 32, 128], P('depth', 'azim'), may hold values from 0.015 to 0.04
- cell_count: int32 [16, 32], P('depth', 'azim'), may hold values from 16 to 128
- nb_list: int32 [24, 16, 32, 128], P(None, 'depth', 'azim'), may hold values from 0 to 1151, as said below
- iface_dest: int32 [128, 512, 1], P(('depth', 'azim')), may hold values from 0 to 127; in each aligned block of 512 rows (0 to 511, 512 to 1023, ..., all dimensions but the last counted through in order) at most 10 rows name the same one
- iface_shell: int32 [128, 512], P(('depth', 'azim')), may hold values from 0 to 15
- soil_stress: float32 [4, 2048, 128], P(None, ('depth', 'azim')), may hold values from -6 to 6
- soil_rate: float32 [3, 2048, 128], P(None, ('depth', 'azim')), may hold values from -4 to 4
- soil_couple: float32 [3, 2048, 128], P(None, ('depth', 'azim')), may hold values from -30 to 30
Outputs:
- pos_out: float32 [2, 16, 32, 128], P(None, 'depth', 'azim')
- vel_out: float32 [2, 16, 32, 128], P(None, 'depth', 'azim')
- rho_out: float32 [16, 32, 128], P('depth', 'azim')
- stress_out: float32 [4, 2048, 128], P(None, ('depth', 'azim'))
Inputs may be any that keep to these rules, and one draw needn't show every extreme that they name: A cell's live particles fill its slots 0 to cell_count - 1. `nb_list`: entry nb * 128 + s names slot s of the cell at offset (nb // 3 - 1, nb % 3 - 1) in (depth, azimuth) cells, never the particle itself; entries may repeat or name empty slots. `iface_dest`: among the 512 interface slots of one device at most 10 name the same owner.
All inputs are finite; a program needn't handle non-finite values.
Results may differ from a plain program's by a relative error of at most 0.0003.
Values sent between devices are 32-bit elements; how exact they have to be, the bound alone decides.
No kernel may reach another device: no remote copies, remote signals or barrier semaphores. Data moves between devices by JAX's collectives and lax.ppermute only.
A program may use at most 64 MiB of HBM per device.

v0:
```python
import jax
import jax.numpy as jnp
from jax import lax
from jax.sharding import PartitionSpec as P

FSTEPS = 2


step_dt = 0.05
sound_sq = 1.0
visc_alpha = 0.5
soil_dt = 0.1
shear_mod = 1.0
bulk_mod = 2.0
cohesion = 1.0
friction = 0.3


def padded(cells, sides, width, closed):
    for axis, dim in sides:
        count = lax.axis_size(axis)
        ends = count if closed else count - 1
        head = lax.slice_in_dim(cells, 0, width, axis=dim)
        tail = lax.slice_in_dim(cells, cells.shape[dim] - width, cells.shape[dim], axis=dim)
        cells = jnp.concatenate(
            [
                lax.ppermute(tail, axis, [(i, (i + 1) % count) for i in range(ends)]),
                cells,
                lax.ppermute(head, axis, [((i + 1) % count, i) for i in range(ends)]),
            ],
            axis=dim,
        )
    return cells


def state_rim(field):
    banded = padded(field, (("depth", 1),), 1, False)
    return padded(banded, (("azim", 2),), 1, True)


def press_rim(field):
    banded = padded(field, (("depth", 1),), 1, False)
    return padded(banded, (("azim", 2),), 1, True)


def pair_setup(codes, width_ext, slots):
    cell_code = codes // slots
    slot = codes - cell_code * slots
    row_off = cell_code // 3
    col_off = cell_code - row_off * 3
    rows = jnp.arange(codes.shape[1], dtype=jnp.int32)[None, :, None, None]
    cols = jnp.arange(codes.shape[2], dtype=jnp.int32)[None, None, :, None]
    index = ((rows + row_off) * width_ext + cols + col_off) * slots + slot
    return (index, (row_off - 1).astype(jnp.float32), (col_off - 1).astype(jnp.float32))


def soil_step(stress, rate, couple, loads):
    force_x = loads[0][:, None]
    force_y = loads[1][:, None]
    force_p = loads[2][:, None]
    force_e = loads[3][:, None]
    exx = rate[0] + couple[0] * force_x
    eyy = rate[1] + couple[1] * force_y
    exy = rate[2] + couple[2] * force_p
    ezz = -0.5 * (couple[0] + couple[1]) * force_e
    trace = exx + eyy + ezz
    sxx = stress[0] + soil_dt * (2.0 * shear_mod * (exx - trace / 3.0) + bulk_mod * trace)
    syy = stress[1] + soil_dt * (2.0 * shear_mod * (eyy - trace / 3.0) + bulk_mod * trace)
    szz = stress[2] + soil_dt * (2.0 * shear_mod * (ezz - trace / 3.0) + bulk_mod * trace)
    sxy = stress[3] + soil_dt * 2.0 * shear_mod * exy
    first = sxx + syy + szz
    mean = first / 3.0
    dxx = sxx - mean
    dyy = syy - mean
    dzz = szz - mean
    root = jnp.sqrt(0.5 * (dxx * dxx + dyy * dyy + dzz * dzz) + sxy * sxy)
    radius = jnp.maximum(cohesion - friction * first, 0.2 * cohesion)
    factor = radius / jnp.maximum(root, radius)
    return jnp.stack([mean + factor * dxx, mean + factor * dyy, mean + factor * dzz, factor * sxy])


def slot_numbers(dest, devices, capacity):
    rows = dest.shape[0]
    block = 512
    hot = (dest[:, None] == jnp.arange(devices, dtype=jnp.int32)[None, :]).astype(jnp.bfloat16)
    hot = hot.reshape(rows // block, block, devices)
    lower = (
        jnp.arange(block, dtype=jnp.int32)[:, None] > jnp.arange(block, dtype=jnp.int32)[None, :]
    ).astype(jnp.bfloat16)
    within = jnp.einsum("ij,bjd->bid", lower, hot, preferred_element_type=jnp.float32)
    totals = jnp.sum(hot, axis=1, dtype=jnp.float32)
    before = jnp.cumsum(totals, axis=0) - totals
    rank = jnp.sum((within + before[:, None, :]) * hot, axis=2)
    return dest * capacity + rank.reshape(rows).astype(jnp.int32)


def local(
    fluid_pos,
    fluid_vel,
    fluid_mass,
    cell_count,
    nb_list,
    iface_dest,
    iface_shell,
    soil_stress,
    soil_rate,
    soil_couple,
):
    slots = fluid_pos.shape[3]
    depth_rows = fluid_pos.shape[1]
    width_ext = fluid_pos.shape[2] + 2
    live = (jnp.arange(slots, dtype=jnp.int32)[None, None, :] < cell_count[:, :, None]).astype(
        jnp.float32
    )
    mass = fluid_mass * live
    pos = fluid_pos
    vel = fluid_vel
    rho = mass
    press = mass
    index, off_r, off_c = pair_setup(nb_list, width_ext, slots)
    for step in range(FSTEPS):
        state = jnp.concatenate([pos, mass[None], vel], axis=0)
        state_ext = state_rim(state)
        near = jnp.take(state_ext.reshape(state_ext.shape[0], -1), index, axis=1)
        own = state_ext[:, 1:-1, 1:-1]
        dx = own[0][None] - (off_r + near[0])
        dy = own[1][None] - (off_c + near[1])
        dist = jnp.sqrt(dx * dx + dy * dy)
        tail = jnp.maximum(1.0 - dist, 0.0)
        kern = tail * tail * tail * tail * (4.0 * dist + 1.0)
        own_mass = own[2]
        rho = own_mass + jnp.sum(near[2] * kern, axis=0) + jnp.where(own_mass > 0.0, 0.0, 1.0)
        press = sound_sq * (rho - 1.0)
        qterm = press / (rho * rho)
        press_ext = press_rim(jnp.stack([qterm, rho]))
        near_p = jnp.take(press_ext.reshape(press_ext.shape[0], -1), index, axis=1)
        own_p = press_ext[:, 1:-1, 1:-1]
        vdot = (own[3][None] - near[3]) * dx + (own[4][None] - near[4]) * dy
        visc = (
            visc_alpha
            * jnp.maximum(-vdot, 0.0)
            / (dist * dist + 0.01)
            / (0.5 * (own_p[1][None] + near_p[1]))
        )
        coef = near[2] * (own_p[0][None] + near_p[0] + visc) * (20.0 * tail * tail * tail)
        acc = jnp.stack([jnp.sum(coef * dx, axis=0), jnp.sum(coef * dy, axis=0)])
        vel = vel + step_dt * acc * live[None]
        pos = pos + step_dt * vel * live[None]
    edge = depth_rows - 1
    load = jnp.stack(
        [
            mass[edge] * vel[0, edge],
            mass[edge] * vel[1, edge],
            mass[edge] * press[edge],
            0.5 * mass[edge] * (vel[0, edge] * vel[0, edge] + vel[1, edge] * vel[1, edge]),
        ]
    )
    iface_rows = load.shape[1] * load.shape[2]
    load = load.reshape(4, iface_rows)
    shell_local = iface_shell[0]
    dest = iface_dest[0, :, 0]
    n_depth = lax.axis_size("depth")
    n_azim = lax.axis_size("azim")
    devices = n_depth * n_azim
    capacity = 5 * iface_rows // (2 * devices)
    slot = slot_numbers(dest, devices, capacity)
    packet = jnp.concatenate([load, shell_local.astype(jnp.float32)[None]], axis=0)
    outgoing = jnp.zeros((5, devices * capacity), jnp.float32).at[:, slot].set(packet)
    incoming = lax.all_to_all(outgoing, ("depth", "azim"), split_axis=1, concat_axis=1, tiled=True)
    shells_here = soil_stress.shape[1]
    member = (incoming[4][None, :] == jnp.arange(shells_here, dtype=jnp.float32)[:, None]).astype(
        jnp.float32
    )
    shell_load = jnp.dot(incoming[:4], member.T, precision=lax.Precision.HIGHEST)
    stress_out = soil_step(soil_stress, soil_rate, soil_couple, shell_load)
    return (pos, vel, rho, stress_out)


def solution(mesh):
    return jax.shard_map(
        local,
        mesh=mesh,
        in_specs=(
            P(None, "depth", "azim", None),
            P(None, "depth", "azim", None),
            P("depth", "azim", None),
            P("depth", "azim"),
            P(None, "depth", "azim", None),
            P(("depth", "azim"), None, None),
            P(("depth", "azim"), None),
            P(None, ("depth", "azim"), None),
            P(None, ("depth", "azim"), None),
            P(None, ("depth", "azim"), None),
        ),
        out_specs=(
            P(None, "depth", "azim", None),
            P(None, "depth", "azim", None),
            P("depth", "azim", None),
            P(None, ("depth", "azim"), None),
        ),
        check_vma=False,
    )
```

profile of v0, /device:TPU:1, one launch (start us, length us, event | category | flops | bytes accessed | tf_op | source)
XLA Modules:
  0.0 280.7 jit_solution(9067108489507527756)
XLA Ops:
  0.7 0.8 fusion.89
  1.5 0.7 fusion.77
  2.2 3.3 %collective-permute-start.1 = (f32[5,1,4,128]{3,2,1,0:T(4,128)S(1)}, f32[5,1,4,128]{3,2,1,0:T(4,128)S(1)}, u32[]{:S(2)}, u32[]{:S(2)}) collective-permute-start(f32[5,1,4,128]{3,2,1,0:T(4,128)S(1)} %fusion.77), channel_id=1, source_target_pairs={{8,0},{16,8},{24,16},{32,24},{40,32},{48,40},{56,48},{64,56},{72,6... | collective-permute-start | bytes 30728 | tf_op jit(solution)/shard_map/ppermute | solution.py:29
  5.5 3.5 %collective-permute-start = (f32[5,1,4,128]{3,2,1,0:T(4,128)S(1)}, f32[5,1,4,128]{3,2,1,0:T(4,128)S(1)}, u32[]{:S(2)}, u32[]{:S(2)}) collective-permute-start(f32[5,1,4,128]{3,2,1,0:T(4,128)S(1)} %fusion.77), channel_id=1, source_target_pairs={{0,8},{8,16},{16,24},{24,32},{32,40},{40,48},{48,56},{56,64},{64,7... | collective-permute-start | bytes 30728 | tf_op jit(solution)/shard_map/ppermute | solution.py:27
  9.0 0.9 and_bitcast_fusion
  10.0 0.7 fusion.73
  10.7 5.6 %collective-permute-start.3 = (f32[5,3,1,128]{3,2,1,0:T(1,128)S(1)}, f32[5,3,1,128]{3,2,1,0:T(1,128)S(1)}, u32[]{:S(2)}, u32[]{:S(2)}) collective-permute-start(f32[5,3,1,128]{3,2,1,0:T(1,128)S(1)} %get-tuple-element.39), channel_id=1, source_target_pairs={{1,0},{2,1},{3,2},{4,3},{5,4},{6,5},{7,6},{0,7},{9,8},{10,9},{11,1... | collective-permute-start | bytes 23048 | tf_op jit(solution)/shard_map/ppermute | solution.py:29
  16.3 0.7 slice_bitcast_fusion.22
  17.1 5.7 %collective-permute-done.2 = f32[5,3,1,128]{3,2,1,0:T(1,128)S(1)} collective-permute-done((f32[5,3,1,128]{3,2,1,0:T(1,128)S(1)}, f32[5,3,1,128]{3,2,1,0:T(1,128)S(1)}, u32[]{:S(2)}, u32[]{:S(2)}) %collective-permute-start.2) | collective-permute-done | bytes 7712 | tf_op jit(solution)/shard_map/ppermute | solution.py:27
  22.8 0.7 fusion.15
  23.5 0.4 copy.138
  23.9 41.1 %gather_fusion = f32[12288,5]{1,0:T(8,128)} fusion(f32[5,2304]{0,1:T(8,128)S(1)} %bitcast.259, s32[12288]{0:T(1024)S(1)} %broadcast_clamp_fusion), kind=kCustom, calls=%fused_computation.clone | custom fusion | bytes 540672 | tf_op jit(solution)/shard_map/jit(_take)/gather | solution.py:124
  65.0 4.4 %copy.141 = f32[24,4,128,5]{2,0,1,3:T(8,128)S(1)} copy(f32[24,4,128,5]{3,2,1,0:T(8,128)} %bitcast.261) | data formatting | bytes 491520 | tf_op jit(solution)/shard_map/jit(_take)/gather | solution.py:124
  69.8 2.3 collective-permute-start.5
  72.1 4.1 %collective-permute-start.4 = (f32[2,1,4,128]{3,2,1,0:T(4,128)S(1)}, f32[2,1,4,128]{3,2,1,0:T(4,128)S(1)}, u32[]{:S(2)}, u32[]{:S(2)}) collective-permute-start(f32[2,1,4,128]{3,2,1,0:T(4,128)S(1)} %pad_maximum_fusion.9), channel_id=1, source_target_pairs={{0,8},{8,16},{16,24},{24,32},{32,40},{40,48},{48,56},{56,64},{64,7... | collective-permute-start | bytes 12296 | tf_op jit(solution)/shard_map/ppermute | solution.py:27
  76.3 0.7 collective-permute-done.4
  77.0 0.4 collective-permute-start.7
  77.4 1.1 collective-permute-start.6
  78.6 0.9 collective-permute-done.7
  79.5 3.9 %collective-permute-done.6 = f32[2,3,1,128]{3,2,1,0:T(1,128)S(1)} collective-permute-done((f32[2,3,1,128]{3,2,1,0:T(1,128)S(1)}, f32[2,3,1,128]{3,2,1,0:T(1,128)S(1)}, u32[]{:S(2)}, u32[]{:S(2)}) %collective-permute-start.6) | collective-permute-done | bytes 3104 | tf_op jit(solution)/shard_map/ppermute | solution.py:27
  83.4 0.4 copy.142
  83.8 41.1 %gather_fusion.1 = f32[12288,2]{1,0:T(8,128)} fusion(f32[2,2304]{0,1:T(8,128)S(1)} %bitcast.266, s32[12288]{0:T(1024)S(1)} %broadcast_clamp_fusion), kind=kCustom, calls=%fused_computation.1.clone | custom fusion | bytes 245760 | tf_op jit(solution)/shard_map/jit(_take)/gather | solution.py:136
  125.0 4.4 %copy.145 = f32[24,4,128,2]{2,0,1,3:T(8,128)S(1)} copy(f32[24,4,128,2]{3,2,1,0:T(8,128)} %bitcast.264) | data formatting | bytes 196608 | tf_op jit(solution)/shard_map/jit(_take)/gather | solution.py:136
  129.6 1.9 collective-permute-start.9
  131.5 5.1 %collective-permute-start.8 = (f32[5,1,4,128]{3,2,1,0:T(4,128)S(1)}, f32[5,1,4,128]{3,2,1,0:T(4,128)S(1)}, u32[]{:S(2)}, u32[]{:S(2)}) collective-permute-start(f32[5,1,4,128]{3,2,1,0:T(4,128)S(1)} %fusion.78), channel_id=1, source_target_pairs={{0,8},{8,16},{16,24},{24,32},{32,40},{40,48},{48,56},{56,64},{64,7... | collective-permute-start | bytes 30728 | tf_op jit(solution)/shard_map/ppermute | solution.py:27
  136.7 0.6 collective-permute-done.8
  137.4 0.3 collective-permute-start.11
  137.7 1.2 collective-permute-start.10
  138.9 1.3 collective-permute-done.11
  140.3 3.6 %collective-permute-done.10 = f32[5,3,1,128]{3,2,1,0:T(1,128)S(1)} collective-permute-done((f32[5,3,1,128]{3,2,1,0:T(1,128)S(1)}, f32[5,3,1,128]{3,2,1,0:T(1,128)S(1)}, u32[]{:S(2)}, u32[]{:S(2)}) %collective-permute-start.10) | collective-permute-done | bytes 7712 | tf_op jit(solution)/shard_map/ppermute | solution.py:27
  143.9 0.4 copy.146
  144.3 41.1 %gather_fusion.2 = f32[12288,5]{1,0:T(8,128)} fusion(f32[5,2304]{0,1:T(8,128)S(1)} %bitcast.260, s32[12288]{0:T(1024)S(1)} %broadcast_clamp_fusion), kind=kCustom, calls=%fused_computation.2.clone | custom fusion | bytes 540672 | tf_op jit(solution)/shard_map/jit(_take)/gather | solution.py:124
  185.4 4.4 %copy.149 = f32[24,4,128,5]{2,0,1,3:T(8,128)S(1)} copy(f32[24,4,128,5]{3,2,1,0:T(8,128)} %bitcast.262) | data formatting | bytes 491520 | tf_op jit(solution)/shard_map/jit(_take)/gather | solution.py:124
  190.1 1.9 collective-permute-start.13
  192.1 5.2 %collective-permute-start.12 = (f32[2,1,4,128]{3,2,1,0:T(4,128)S(1)}, f32[2,1,4,128]{3,2,1,0:T(4,128)S(1)}, u32[]{:S(2)}, u32[]{:S(2)}) collective-permute-start(f32[2,1,4,128]{3,2,1,0:T(4,128)S(1)} %pad_maximum_fusion.10), channel_id=1, source_target_pairs={{0,8},{8,16},{16,24},{24,32},{32,40},{40,48},{48,56},{56,64},{64,7... | collective-permute-start | bytes 12296 | tf_op jit(solution)/shard_map/ppermute | solution.py:27
  197.2 0.4 fusion.3
  198.0 0.3 collective-permute-start.15
  198.3 1.2 collective-permute-start.14
  199.5 1.2 collective-permute-done.15
  200.8 3.6 %collective-permute-done.14 = f32[2,3,1,128]{3,2,1,0:T(1,128)S(1)} collective-permute-done((f32[2,3,1,128]{3,2,1,0:T(1,128)S(1)}, f32[2,3,1,128]{3,2,1,0:T(1,128)S(1)}, u32[]{:S(2)}, u32[]{:S(2)}) %collective-permute-start.14) | collective-permute-done | bytes 3104 | tf_op jit(solution)/shard_map/ppermute | solution.py:27
  204.4 0.4 copy.150
  204.8 41.1 %gather_fusion.3 = f32[12288,2]{1,0:T(8,128)} fusion(f32[2,2304]{0,1:T(8,128)S(1)} %bitcast.265, s32[12288]{0:T(1024)S(1)} %broadcast_clamp_fusion), kind=kCustom, calls=%fused_computation.3.clone | custom fusion | bytes 245760 | tf_op jit(solution)/shard_map/jit(_take)/gather | solution.py:136
  245.9 4.4 %copy.153 = f32[24,4,128,2]{2,0,1,3:T(8,128)S(1)} copy(f32[24,4,128,2]{3,2,1,0:T(8,128)} %bitcast.263) | data formatting | bytes 196608 | tf_op jit(solution)/shard_map/jit(_take)/gather | solution.py:136
  250.5 0.6 multiply_add_fusion.9
  251.3 1.9 scatter_custom_fusion
  253.4 0.3 all_to_all.6
  254.0 25.1 %all_to_all.9 = f32[5,128,10]{2,0,1:T(8,128)S(1)} all-to-all(f32[5,128,10]{2,0,1:T(8,128)S(1)} %copy.156), channel_id=1, replica_groups=mesh['depth'=16,'azim'=8] {'depth','azim'}, dimensions={1} | all-to-all | bytes 51200 | tf_op jit(solution)/shard_map/all_to_all | solution.py:169
  280.1 0.6 pad_maximum_fusion.4
  (81 shorter events, 3.2 us)
Async XLA Ops:
  0.6 69.1 %copy-start.9 = (s32[1,4]{1,0:T(1,128)S(1)}, s32[1,4]{1,0:T(1,128)}, u32[]{:S(2)}) copy-start(s32[1,4]{1,0:T(1,128)} %param.17) | copy-start | bytes 52
  0.6 69.1 %copy-start.5 = (f32[1,4,128]{2,1,0:T(4,128)S(1)}, f32[1,4,128]{2,1,0:T(4,128)}, u32[]{:S(2)}) copy-start(f32[1,4,128]{2,1,0:T(4,128)} %param.16) | copy-start | bytes 6148
  0.7 75.6 %copy-start.2 = (f32[2,1,4,128]{3,2,1,0:T(4,128)S(1)}, f32[2,1,4,128]{3,2,1,0:T(4,128)}, u32[]{:S(2)}) copy-start(f32[2,1,4,128]{3,2,1,0:T(4,128)} %param.15) | copy-start | bytes 12292
  0.7 68.9 %copy-start = (s32[24,1,4,128]{3,2,1,0:T(4,128)S(1)}, s32[24,1,4,128]{3,2,1,0:T(4,128)}, u32[]{:S(2)}) copy-start(s32[24,1,4,128]{3,2,1,0:T(4,128)} %param.18) | copy-start | bytes 147460
  2.2 7.8 %collective-permute-start.1 = (f32[5,1,4,128]{3,2,1,0:T(4,128)S(1)}, f32[5,1,4,128]{3,2,1,0:T(4,128)S(1)}, u32[]{:S(2)}, u32[]{:S(2)}) collective-permute-start(f32[5,1,4,128]{3,2,1,0:T(4,128)S(1)} %fusion.77), channel_id=1, source_target_pairs={{8,0},{16,8},{24,16},{32,24},{40,32},{48,40},{56,48},{64,56},{72,6... | collective-permute-start | bytes 30728 | tf_op jit(solution)/shard_map/ppermute | solution.py:29
  5.5 4.5 %collective-permute-start = (f32[5,1,4,128]{3,2,1,0:T(4,128)S(1)}, f32[5,1,4,128]{3,2,1,0:T(4,128)S(1)}, u32[]{:S(2)}, u32[]{:S(2)}) collective-permute-start(f32[5,1,4,128]{3,2,1,0:T(4,128)S(1)} %fusion.77), channel_id=1, source_target_pairs={{0,8},{8,16},{16,24},{24,32},{32,40},{40,48},{48,56},{56,64},{64,7... | collective-permute-start | bytes 30728 | tf_op jit(solution)/shard_map/ppermute | solution.py:27
  10.7 6.4 %collective-permute-start.3 = (f32[5,3,1,128]{3,2,1,0:T(1,128)S(1)}, f32[5,3,1,128]{3,2,1,0:T(1,128)S(1)}, u32[]{:S(2)}, u32[]{:S(2)}) collective-permute-start(f32[5,3,1,128]{3,2,1,0:T(1,128)S(1)} %get-tuple-element.39), channel_id=1, source_target_pairs={{1,0},{2,1},{3,2},{4,3},{5,4},{6,5},{7,6},{0,7},{9,8},{10,9},{11,1... | collective-permute-start | bytes 23048 | tf_op jit(solution)/shard_map/ppermute | solution.py:29
  16.3 6.5 %collective-permute-start.2 = (f32[5,3,1,128]{3,2,1,0:T(1,128)S(1)}, f32[5,3,1,128]{3,2,1,0:T(1,128)S(1)}, u32[]{:S(2)}, u32[]{:S(2)}) collective-permute-start(f32[5,3,1,128]{3,2,1,0:T(1,128)S(1)} %get-tuple-element.38), channel_id=1, source_target_pairs={{0,1},{1,2},{2,3},{3,4},{4,5},{5,6},{6,7},{7,0},{8,9},{9,10},{10,1... | collective-permute-start | bytes 23048 | tf_op jit(solution)/shard_map/ppermute | solution.py:27
  69.5 60.0 %copy-start.1 = (f32[2,1,4,128]{3,2,1,0:T(4,128)S(1)}, f32[2,1,4,128]{3,2,1,0:T(4,128)}, u32[]{:S(2)}) copy-start(f32[2,1,4,128]{3,2,1,0:T(4,128)} %param.14) | copy-start | bytes 12292
  69.5 67.1 %copy-start.10 = (s32[1,512,1]{1,2,0:T(1,128)S(1)}, s32[1,512,1]{1,2,0:T(1,128)}, u32[]{:S(2)}) copy-start(s32[1,512,1]{1,2,0:T(1,128)} %param.19) | copy-start | bytes 6148
  69.8 6.4 %collective-permute-start.5 = (f32[2,1,4,128]{3,2,1,0:T(4,128)S(1)}, f32[2,1,4,128]{3,2,1,0:T(4,128)S(1)}, u32[]{:S(2)}, u32[]{:S(2)}) collective-permute-start(f32[2,1,4,128]{3,2,1,0:T(4,128)S(1)} %pad_maximum_fusion.9), channel_id=1, source_target_pairs={{8,0},{16,8},{24,16},{32,24},{40,32},{48,40},{56,48},{64,56},{72,6... | collective-permute-start | bytes 12296 | tf_op jit(solution)/shard_map/ppermute | solution.py:29
  72.1 4.8 %collective-permute-start.4 = (f32[2,1,4,128]{3,2,1,0:T(4,128)S(1)}, f32[2,1,4,128]{3,2,1,0:T(4,128)S(1)}, u32[]{:S(2)}, u32[]{:S(2)}) collective-permute-start(f32[2,1,4,128]{3,2,1,0:T(4,128)S(1)} %pad_maximum_fusion.9), channel_id=1, source_target_pairs={{0,8},{8,16},{16,24},{24,32},{32,40},{40,48},{48,56},{56,64},{64,7... | collective-permute-start | bytes 12296 | tf_op jit(solution)/shard_map/ppermute | solution.py:27
  77.0 2.5 collective-permute-start.7
  77.4 6.1 %collective-permute-start.6 = (f32[2,3,1,128]{3,2,1,0:T(1,128)S(1)}, f32[2,3,1,128]{3,2,1,0:T(1,128)S(1)}, u32[]{:S(2)}, u32[]{:S(2)}) collective-permute-start(f32[2,3,1,128]{3,2,1,0:T(1,128)S(1)} %get-tuple-element.43), channel_id=1, source_target_pairs={{0,1},{1,2},{2,3},{3,4},{4,5},{5,6},{6,7},{7,0},{8,9},{9,10},{10,1... | collective-permute-start | bytes 9224 | tf_op jit(solution)/shard_map/ppermute | solution.py:27
  129.4 70.1 %copy-start.11 = (s32[1,512]{1,0:T(1,128)S(1)}, s32[1,512]{1,0:T(1,128)}, u32[]{:S(2)}) copy-start(s32[1,512]{1,0:T(1,128)} %param.20) | copy-start | bytes 6148
  129.6 7.2 %collective-permute-start.9 = (f32[5,1,4,128]{3,2,1,0:T(4,128)S(1)}, f32[5,1,4,128]{3,2,1,0:T(4,128)S(1)}, u32[]{:S(2)}, u32[]{:S(2)}) collective-permute-start(f32[5,1,4,128]{3,2,1,0:T(4,128)S(1)} %fusion.78), channel_id=1, source_target_pairs={{8,0},{16,8},{24,16},{32,24},{40,32},{48,40},{56,48},{64,56},{72,6... | collective-permute-start | bytes 30728 | tf_op jit(solution)/shard_map/ppermute | solution.py:29
  131.5 5.9 %collective-permute-start.8 = (f32[5,1,4,128]{3,2,1,0:T(4,128)S(1)}, f32[5,1,4,128]{3,2,1,0:T(4,128)S(1)}, u32[]{:S(2)}, u32[]{:S(2)}) collective-permute-start(f32[5,1,4,128]{3,2,1,0:T(4,128)S(1)} %fusion.78), channel_id=1, source_target_pairs={{0,8},{8,16},{16,24},{24,32},{32,40},{40,48},{48,56},{56,64},{64,7... | collective-permute-start | bytes 30728 | tf_op jit(solution)/shard_map/ppermute | solution.py:27
  137.4 2.9 %collective-permute-start.11 = (f32[5,3,1,128]{3,2,1,0:T(1,128)S(1)}, f32[5,3,1,128]{3,2,1,0:T(1,128)S(1)}, u32[]{:S(2)}, u32[]{:S(2)}) collective-permute-start(f32[5,3,1,128]{3,2,1,0:T(1,128)S(1)} %get-tuple-element.37), channel_id=1, source_target_pairs={{1,0},{2,1},{3,2},{4,3},{5,4},{6,5},{7,6},{0,7},{9,8},{10,9},{11,1... | collective-permute-start | bytes 23048 | tf_op jit(solution)/shard_map/ppermute | solution.py:29
  137.7 6.1 %collective-permute-start.10 = (f32[5,3,1,128]{3,2,1,0:T(1,128)S(1)}, f32[5,3,1,128]{3,2,1,0:T(1,128)S(1)}, u32[]{:S(2)}, u32[]{:S(2)}) collective-permute-start(f32[5,3,1,128]{3,2,1,0:T(1,128)S(1)} %get-tuple-element.36), channel_id=1, source_target_pairs={{0,1},{1,2},{2,3},{3,4},{4,5},{5,6},{6,7},{7,0},{8,9},{9,10},{10,1... | collective-permute-start | bytes 23048 | tf_op jit(solution)/shard_map/ppermute | solution.py:27
  190.1 63.9 %copy-start.3 = (f32[1,4,128]{2,1,0:T(4,128)}, f32[1,4,128]{2,1,0:T(4,128)S(1)}, u32[]{:S(2)}) copy-start(f32[1,4,128]{2,1,0:T(4,128)S(1)} %get-tuple-element.16) | copy-start | bytes 6148
  190.1 7.5 %collective-permute-start.13 = (f32[2,1,4,128]{3,2,1,0:T(4,128)S(1)}, f32[2,1,4,128]{3,2,1,0:T(4,128)S(1)}, u32[]{:S(2)}, u32[]{:S(2)}) collective-permute-start(f32[2,1,4,128]{3,2,1,0:T(4,128)S(1)} %pad_maximum_fusion.10), channel_id=1, source_target_pairs={{8,0},{16,8},{24,16},{32,24},{40,32},{48,40},{56,48},{64,56},{72,6... | collective-permute-start | bytes 12296 | tf_op jit(solution)/shard_map/ppermute | solution.py:29
  192.1 5.9 %collective-permute-start.12 = (f32[2,1,4,128]{3,2,1,0:T(4,128)S(1)}, f32[2,1,4,128]{3,2,1,0:T(4,128)S(1)}, u32[]{:S(2)}, u32[]{:S(2)}) collective-permute-start(f32[2,1,4,128]{3,2,1,0:T(4,128)S(1)} %pad_maximum_fusion.10), channel_id=1, source_target_pairs={{0,8},{8,16},{16,24},{24,32},{32,40},{40,48},{48,56},{56,64},{64,7... | collective-permute-start | bytes 12296 | tf_op jit(solution)/shard_map/ppermute | solution.py:27
  198.0 2.8 collective-permute-start.15
  198.3 6.1 %collective-permute-start.14 = (f32[2,3,1,128]{3,2,1,0:T(1,128)S(1)}, f32[2,3,1,128]{3,2,1,0:T(1,128)S(1)}, u32[]{:S(2)}, u32[]{:S(2)}) collective-permute-start(f32[2,3,1,128]{3,2,1,0:T(1,128)S(1)} %get-tuple-element.41), channel_id=1, source_target_pairs={{0,1},{1,2},{2,3},{3,4},{4,5},{5,6},{6,7},{7,0},{8,9},{9,10},{10,1... | collective-permute-start | bytes 9224 | tf_op jit(solution)/shard_map/ppermute | solution.py:27
  245.9 33.9 %copy-start.6 = (f32[3,16,128]{2,1,0:T(8,128)S(1)}, f32[3,16,128]{2,1,0:T(8,128)}, u32[]{:S(2)}) copy-start(f32[3,16,128]{2,1,0:T(8,128)} %param.22) | copy-start | bytes 73732
  245.9 34.0 %copy-start.7 = (f32[3,16,128]{2,1,0:T(8,128)S(1)}, f32[3,16,128]{2,1,0:T(8,128)}, u32[]{:S(2)}) copy-start(f32[3,16,128]{2,1,0:T(8,128)} %param.23) | copy-start | bytes 73732
  245.9 34.0 %copy-start.4 = (f32[4,16,128]{2,1,0:T(8,128)S(1)}, f32[4,16,128]{2,1,0:T(8,128)}, u32[]{:S(2)}) copy-start(f32[4,16,128]{2,1,0:T(8,128)} %param.21) | copy-start | bytes 98308
  251.1 29.6 %copy-start.8 = (f32[2,1,4,128]{3,2,1,0:T(4,128)}, f32[2,1,4,128]{3,2,1,0:T(4,128)S(1)}, u32[]{:S(2)}) copy-start(f32[2,1,4,128]{3,2,1,0:T(4,128)S(1)} %get-tuple-element.18) | copy-start | bytes 12292
where the time goes:
time: 281 us
  local copies, waits for them, and re-layouts  188 us (67%)
  starting transfers between devices  37.5 us (13%)
  blocking collectives  25.1 us (9%)
  waiting for transfers between devices  22 us (8%)
  other arithmetic  6.4 us (2%)
    gather x4, local copies, waits for them, and re-layouts, local(): near = jnp.take(state_ext.reshape(state_ext.shape[0], -1), index, axis=1)  91.1 us
    gather x4, local copies, waits for them, and re-layouts, local(): near_p = jnp.take(press_ext.reshape(press_ext.shape[0], -1), index, axis=1)  91.1 us
    all_to_all x1, blocking collectives, local(): lax.all_to_all(outgoing, ('depth', 'azim'), split_axis=1, concat_axis=1,...  25.1 us
    ppermute x8, starting transfers between devices, padded(): lax.ppermute(tail, axis, [(i, (i + 1) % count) for i in range(ends)])  21.4 us
    ppermute x8, waiting for transfers between devices, padded(): lax.ppermute(tail, axis, [(i, (i + 1) % count) for i in range(ends)])  18.4 us
    ppermute x8, starting transfers between devices, padded(): lax.ppermute(head, axis, [((i + 1) % count, i) for i in range(ends)])  16.1 us
  transfers between devices with their start and end apart: 16, of which 11 were waited for; matrix products, arithmetic and copies ran while one was open for 1% of the time, Pallas kernels for 0%

commit v1 on v0

v1 whole, which is shorter than its diff:
```python
import jax
import jax.numpy as jnp
from jax import lax
from jax.experimental import pallas as pl
from jax.experimental.pallas import tpu as pltpu
from jax.sharding import PartitionSpec as P

step_dt = 0.05
sound_sq = 1.0
visc_alpha = 0.5
soil_dt = 0.1
shear_mod = 1.0
bulk_mod = 2.0
cohesion = 1.0
friction = 0.3

CELLS = 4
NB = 24
NT = 3
WIDE = 8
RING = 6
S = 128
PX, PY, PM, PVX, PVY, PL = range(6)


def pack_kernel(count, pos, vel, mass, nb, out):
    lane = lax.broadcasted_iota(jnp.int32, (1, S), 1)
    for c in range(CELLS):
        live = (lane < count[0, c]).astype(jnp.float32)
        out[8 * c + PX : 8 * c + PX + 1, :] = pos[c : c + 1, :]
        out[8 * c + PY : 8 * c + PY + 1, :] = pos[CELLS + c : CELLS + c + 1, :]
        out[8 * c + PM : 8 * c + PM + 1, :] = mass[c : c + 1, :] * live
        out[8 * c + PVX : 8 * c + PVX + 1, :] = vel[c : c + 1, :]
        out[8 * c + PVY : 8 * c + PVY + 1, :] = vel[CELLS + c : CELLS + c + 1, :]
        out[8 * c + PL : 8 * c + PL + 1, :] = live
        out[8 * c + PL + 1 : 8 * c + 8, :] = jnp.zeros((2, S), jnp.float32)
        base = 8 * CELLS + NB * c
        out[base : base + NB, :] = nb[pl.ds(c, NB, stride=CELLS), :].astype(jnp.float32)


def spread(row):
    return jnp.broadcast_to(row, (8, S))


def pick(tables, slot, masks):
    out = None
    for table, mask in zip(tables, masks):
        got = jnp.take_along_axis(table, slot, axis=1)
        out = got if out is None else jnp.where(mask, got, out)
    return out


def step_body(sign, frame, lists, pair, press):
    def number(dr, dc):
        return 3 * (1 + sign * dr) + dc + 1

    near = [(dr, dc) for dr in (-1, 0, 1) for dc in (-1, 0, 1)]

    def density(cell, carry):
        row = cell // RING
        col = cell - row * RING
        centre = ((row + 1) * WIDE + col + 1) * 8
        own = frame[pl.ds(pl.multiple_of(centre, 8), 8), :]
        own_x, own_y = spread(own[PX : PX + 1]), spread(own[PY : PY + 1])
        own_m = own[PM : PM + 1]
        xs, ys, ms = [], [], []
        for dr, dc in near:
            tile = frame[pl.ds(pl.multiple_of(centre + (dr * WIDE + dc) * 8, 8), 8), :]
            xs.append(spread(tile[PX : PX + 1] + (sign * dr).astype(jnp.float32)))
            ys.append(spread(tile[PY : PY + 1] + float(dc)))
            ms.append(spread(tile[PM : PM + 1]))
        total = jnp.zeros((8, S), jnp.float32)
        for t in range(NT):
            code = lists[pl.ds(pl.multiple_of(cell * NB + 8 * t, 8), 8), :].astype(jnp.int32)
            slot = code & (S - 1)
            which = code >> 7
            masks = [which == number(dr, dc) for dr, dc in near]
            dx = own_x - pick(xs, slot, masks)
            dy = own_y - pick(ys, slot, masks)
            mass = pick(ms, slot, masks)
            dist = jnp.sqrt(dx * dx + dy * dy)
            tail = jnp.maximum(1.0 - dist, 0.0)
            cube = tail * tail * tail
            total = total + mass * (cube * tail * (4.0 * dist + 1.0))
            base = pl.multiple_of((cell * NT + t) * 40, 8)
            pair[pl.ds(base, 8), :] = dx
            pair[pl.ds(base + 8, 8), :] = dy
            pair[pl.ds(base + 16, 8), :] = mass
            pair[pl.ds(base + 24, 8), :] = dist * dist + 0.01
            pair[pl.ds(base + 32, 8), :] = 20.0 * cube
        rho = own_m + jnp.sum(total, axis=0, keepdims=True) + jnp.where(own_m > 0.0, 0.0, 1.0)
        q = sound_sq * (rho - 1.0) / (rho * rho)
        base = pl.multiple_of(cell * 8, 8)
        press[pl.ds(base, 1), :] = q
        press[pl.ds(base + 1, 1), :] = rho
        return carry

    lax.fori_loop(0, 3 * RING, density, 0)

    def force(c, carry):
        cell = RING + 1 + c
        centre = (2 * WIDE + 2 + c) * 8
        own = frame[pl.ds(pl.multiple_of(centre, 8), 8), :]
        own_p = press[pl.ds(pl.multiple_of(cell * 8, 8), 8), :]
        own_vx, own_vy = spread(own[PVX : PVX + 1]), spread(own[PVY : PVY + 1])
        own_q, own_rho = spread(own_p[0:1]), spread(own_p[1:2])
        vxs, vys, qs, rhos = [], [], [], []
        for dr, dc in near:
            tile = frame[pl.ds(pl.multiple_of(centre + (dr * WIDE + dc) * 8, 8), 8), :]
            ptile = press[pl.ds(pl.multiple_of((cell + dr * RING + dc) * 8, 8), 8), :]
            vxs.append(spread(tile[PVX : PVX + 1]))
            vys.append(spread(tile[PVY : PVY + 1]))
            qs.append(spread(ptile[0:1]))
            rhos.append(spread(ptile[1:2]))
        ax = jnp.zeros((8, S), jnp.float32)
        ay = jnp.zeros((8, S), jnp.float32)
        for t in range(NT):
            code = lists[pl.ds(pl.multiple_of(cell * NB + 8 * t, 8), 8), :].astype(jnp.int32)
            slot = code & (S - 1)
            which = code >> 7
            masks = [which == number(dr, dc) for dr, dc in near]
            base = pl.multiple_of((cell * NT + t) * 40, 8)
            dx = pair[pl.ds(base, 8), :]
            dy = pair[pl.ds(base + 8, 8), :]
            mass = pair[pl.ds(base + 16, 8), :]
            soft = pair[pl.ds(base + 24, 8), :]
            slope = pair[pl.ds(base + 32, 8), :]
            vdot = (own_vx - pick(vxs, slot, masks)) * dx + (own_vy - pick(vys, slot, masks)) * dy
            visc = visc_alpha * jnp.maximum(-vdot, 0.0) / (soft * (0.5 * (own_rho + pick(rhos, slot, masks))))
            coef = mass * (own_q + pick(qs, slot, masks) + visc) * slope
            ax = ax + coef * dx
            ay = ay + coef * dy
        live = own[PL : PL + 1]
        vx = own[PVX : PVX + 1] + step_dt * jnp.sum(ax, axis=0, keepdims=True) * live
        vy = own[PVY : PVY + 1] + step_dt * jnp.sum(ay, axis=0, keepdims=True) * live
        x = own[PX : PX + 1] + step_dt * vx * live
        y = own[PY : PY + 1] + step_dt * vy * live
        return x, y, own[PM : PM + 1], vx, vy, live, own_p[1:2]

    return force


def first_kernel(parity, q0, q1, q2, q3, q4, out, frame, lists, pair, press):
    sign = 1 - 2 * parity[0]
    half = 8 * CELLS
    rows = {0: q0, 1: q3, -1: q4, 2: q1}
    right = half + CELLS * NB
    for r, ref in rows.items():
        base = (r + 2) * WIDE * 8
        frame[base : base + half, :] = ref[0:half, :]
        frame[base + half : base + 2 * half, :] = ref[right : right + half, :]
    frame[0 : 2 * half, :] = q2[...]
    for r in (-1, 0, 1):
        ref = rows[r]
        base = (r + 1) * RING * NB
        lists[base : base + 3 * NB, :] = ref[half + NB : half + 4 * NB, :]
        lists[base + 3 * NB : base + 6 * NB, :] = ref[right + half : right + half + 3 * NB, :]
        out[half + (r + 1) * NB : half + (r + 2) * NB, :] = ref[half + 3 * NB : half + 4 * NB, :]
    force = step_body(sign, frame, lists, pair, press)
    for c in range(CELLS):
        x, y, m, vx, vy, live, _ = force(c, 0)
        for k, v in enumerate((x, y, m, vx, vy, live)):
            out[8 * c + k : 8 * c + k + 1, :] = v
        out[8 * c + 6 : 8 * c + 8, :] = jnp.zeros((2, S), jnp.float32)


def second_kernel(parity, dest, shell, left, r0, r1, r2, r3, r4, q0, q3, q4, pos_out, vel_out, rho_out, part, frame, lists, pair, press):
    sign = 1 - 2 * parity[0]
    half = 8 * CELLS
    right = half + CELLS * NB
    for r, ref in {0: r0, 2: r1, -2: r2, 1: r3, -1: r4}.items():
        base = (r + 2) * WIDE * 8
        frame[base : base + 2 * half, :] = ref[...]
    for r, ref in {-1: q4, 0: q0, 1: q3}.items():
        base = (r + 1) * RING * NB
        lists[base : base + NB, :] = left[half + (r + 1) * NB : half + (r + 2) * NB, :]
        lists[base + NB : base + 5 * NB, :] = ref[half : half + 4 * NB, :]
        lists[base + 5 * NB : base + 6 * NB, :] = ref[right + half : right + half + NB, :]
    force = step_body(sign, frame, lists, pair, press)
    total = jnp.zeros((S, S), jnp.float32)
    devices = lax.broadcasted_iota(jnp.int32, (S, S), 0)
    shells = lax.broadcasted_iota(jnp.int32, (16, S), 0)
    for c in range(CELLS):
        x, y, m, vx, vy, live, rho = force(c, 0)
        pos_out[c : c + 1, :] = x
        pos_out[CELLS + c : CELLS + c + 1, :] = y
        vel_out[c : c + 1, :] = vx
        vel_out[CELLS + c : CELLS + c + 1, :] = vy
        rho_out[c : c + 1, :] = rho
        loads = (m * vx, m * vy, m * (sound_sq * (rho - 1.0)), 0.5 * m * (vx * vx + vy * vy))
        owner = (devices == dest[c : c + 1, :]).astype(jnp.float32)
        member = shells == shell[c : c + 1, :]
        spreads = [jnp.where(member, load, 0.0) for load in loads]
        spreads.append(jnp.zeros((S - 64, S), jnp.float32))
        total = total + lax.dot_general(
            owner,
            jnp.concatenate(spreads, axis=0),
            (((1,), (1,)), ((), ())),
            precision=lax.Precision.HIGHEST,
            preferred_element_type=jnp.float32,
        )
    part[...] = total


def soil_kernel(arrived, stress, rate, couple, out):
    total = jnp.sum(arrived[...], axis=0, keepdims=True)
    lane = lax.broadcasted_iota(jnp.int32, (16, S), 1)
    row = lax.broadcasted_iota(jnp.int32, (16, S), 0)
    force_x, force_y, force_p, force_e = [
        jnp.sum(jnp.where(lane == row + 16 * k, total, 0.0), axis=1, keepdims=True) for k in range(4)
    ]
    exx = rate[0] + couple[0] * force_x
    eyy = rate[1] + couple[1] * force_y
    exy = rate[2] + couple[2] * force_p
    ezz = -0.5 * (couple[0] + couple[1]) * force_e
    trace = exx + eyy + ezz
    sxx = stress[0] + soil_dt * (2.0 * shear_mod * (exx - trace / 3.0) + bulk_mod * trace)
    syy = stress[1] + soil_dt * (2.0 * shear_mod * (eyy - trace / 3.0) + bulk_mod * trace)
    szz = stress[2] + soil_dt * (2.0 * shear_mod * (ezz - trace / 3.0) + bulk_mod * trace)
    sxy = stress[3] + soil_dt * 2.0 * shear_mod * exy
    first = sxx + syy + szz
    mean = first / 3.0
    dxx = sxx - mean
    dyy = syy - mean
    dzz = szz - mean
    root = jnp.sqrt(0.5 * (dxx * dxx + dyy * dyy + dzz * dzz) + sxy * sxy)
    radius = jnp.maximum(cohesion - friction * first, 0.2 * cohesion)
    factor = radius / jnp.maximum(root, radius)
    out[0] = mean + factor * dxx
    out[1] = mean + factor * dyy
    out[2] = mean + factor * dzz
    out[3] = factor * sxy


def rows_of(n):
    return jax.ShapeDtypeStruct((n, S), jnp.float32)


VM = pl.BlockSpec(memory_space=pltpu.MemorySpace.VMEM)
SM = pl.BlockSpec(memory_space=pltpu.MemorySpace.SMEM)
WORK = [
    pltpu.VMEM((5 * WIDE * 8, S), jnp.float32),
    pltpu.VMEM((3 * RING * NB, S), jnp.float32),
    pltpu.VMEM((3 * RING * NT * 40, S), jnp.float32),
    pltpu.VMEM((3 * RING * 8, S), jnp.float32),
]


def local(
    fluid_pos,
    fluid_vel,
    fluid_mass,
    cell_count,
    nb_list,
    iface_dest,
    iface_shell,
    soil_stress,
    soil_rate,
    soil_couple,
):
    n_depth = lax.axis_size("depth")
    n_azim = lax.axis_size("azim")
    parity = (lax.axis_index("depth") % 2).astype(jnp.int32).reshape(1)
    toward_left = [(i, (i - 1) % n_azim) for i in range(n_azim)]
    toward_right = [(i, (i + 1) % n_azim) for i in range(n_azim)]
    pairs = [(i, i ^ 1) for i in range(n_depth)]
    far = [(i, i + 2 if i % 2 else i - 2) for i in range(n_depth)]
    far = [(i, j) for i, j in far if 0 <= j < n_depth]
    back = [(j, i) for i, j in far]
    half = 8 * CELLS

    own = pl.pallas_call(
        pack_kernel,
        out_shape=rows_of(half + CELLS * NB),
        in_specs=[SM, VM, VM, VM, VM],
        out_specs=VM,
        name="pack",
    )(
        cell_count,
        fluid_pos.reshape(2 * CELLS, S),
        fluid_vel.reshape(2 * CELLS, S),
        fluid_mass.reshape(CELLS, S),
        nb_list.reshape(NB * CELLS, S),
    )
    right = lax.ppermute(own, "azim", toward_left)
    q0 = jnp.concatenate([own, right[: half + 3 * NB]], axis=0)
    state = jnp.concatenate([own[:half], right[:half]], axis=0)
    q1 = lax.ppermute(q0, "depth", far)
    q2 = lax.ppermute(state, "depth", back)
    q3 = lax.ppermute(q0, "depth", pairs)
    q4 = lax.ppermute(q1, "depth", pairs)
    mid = pl.pallas_call(
        first_kernel,
        out_shape=rows_of(half + 3 * NB),
        in_specs=[SM] + [VM] * 5,
        out_specs=VM,
        scratch_shapes=WORK,
        name="first_step",
    )(parity, q0, q1, q2, q3, q4)

    left = lax.ppermute(mid, "azim", toward_right)
    r0 = jnp.concatenate([left[:half], mid[:half]], axis=0)
    r1 = lax.ppermute(r0, "depth", far)
    r2 = lax.ppermute(r0, "depth", back)
    r3 = lax.ppermute(r0, "depth", pairs)
    r4 = lax.ppermute(r1, "depth", pairs)
    pos, vel, rho, part = pl.pallas_call(
        second_kernel,
        out_shape=(rows_of(2 * CELLS), rows_of(2 * CELLS), rows_of(CELLS), rows_of(S)),
        in_specs=[SM] + [VM] * 11,
        out_specs=(VM, VM, VM, VM),
        scratch_shapes=WORK,
        name="second_step",
    )(parity, iface_dest.reshape(CELLS, S), iface_shell.reshape(CELLS, S), left, r0, r1, r2, r3, r4, q0, q3, q4)

    arrived = lax.all_to_all(part, ("depth", "azim"), split_axis=0, concat_axis=0, tiled=True)
    stress_out = pl.pallas_call(
        soil_kernel,
        out_shape=jax.ShapeDtypeStruct(soil_stress.shape, jnp.float32),
        in_specs=[VM] * 4,
        out_specs=VM,
        name="soil",
    )(arrived, soil_stress, soil_rate, soil_couple)
    return (
        pos.reshape(fluid_pos.shape),
        vel.reshape(fluid_vel.shape),
        rho.reshape(fluid_mass.shape),
        stress_out,
    )


def solution(mesh):
    return jax.shard_map(
        local,
        mesh=mesh,
        in_specs=(
            P(None, "depth", "azim", None),
            P(None, "depth", "azim", None),
            P("depth", "azim", None),
            P("depth", "azim"),
            P(None, "depth", "azim", None),
            P(("depth", "azim"), None, None),
            P(("depth", "azim"), None),
            P(None, ("depth", "azim"), None),
            P(None, ("depth", "azim"), None),
            P(None, ("depth", "azim"), None),
        ),
        out_specs=(
            P(None, "depth", "azim", None),
            P(None, "depth", "azim", None),
            P("depth", "azim", None),
            P(None, ("depth", "azim"), None),
        ),
        check_vma=False,
    )
```

time: 281 us -> 75.1 us (0.27)
  local copies, waits for them, and re-layouts: 188 us -> 2.03 us
  starting transfers between devices: 37.5 us -> 22.1 us
  Pallas kernels: 0 us -> 15.2 us
  waiting for transfers between devices: 22 us -> 15.3 us
  other arithmetic: 6.4 us -> 0.02 us
  blocking collectives: 25.1 us -> 19.2 us
    gather x8 -> x0, local copies, waits for them, and re-layouts: 182 us -> none  [the longest x4 91.1 us: local(): near = jnp.take(state_ext.reshape(state_ext.shape[0], -1), index, axis=1)]
    ppermute x16 -> x10, starting transfers between devices: 37.5 us -> 22.1 us  [the longest x1 6.62 us: local(): right = lax.ppermute(own, 'azim', toward_left)]
    pallas_call x0 -> x4, Pallas kernels: none -> 15.2 us  [the longest x1 6.3 us: local(): pl.pallas_call(second_kernel, out_shape=(rows_of(2 * CELLS), rows_of(2 *...]
    ppermute x16 -> x10, waiting for transfers between devices: 22 us -> 15.3 us  [the longest x1 7.18 us: local(): left = lax.ppermute(mid, 'azim', toward_right)]
    all_to_all x1, blocking collectives: 25.1 us -> 19.2 us  [local(): lax.all_to_all(part, ('depth', 'azim'), split_axis=0, concat_axis=0, tile...]
  transfers between devices with their start and end apart: 16 -> 10, of which waited for: 11 -> 5; matrix products, arithmetic and copies ran while one was open for 1% -> 1% of each run, Pallas kernels for 0% -> 0%
where the time goes in v1:
time: 75.1 us; the launch traced here: 74.6 us
  starting transfers between devices  22.1 us (29%)
  blocking collectives  19.2 us (26%)
  waiting for transfers between devices  15.3 us (20%)
  Pallas kernels  15.2 us (20%)
  local copies, waits for them, and re-layouts  2.03 us (3%)
  between operations  0.8 us (1%)
    all_to_all x1, blocking collectives, local(): lax.all_to_all(part, ('depth', 'azim'), split_axis=0, concat_axis=0, tile...  19.2 us
    ppermute x1, waiting for transfers between devices, local(): left = lax.ppermute(mid, 'azim', toward_right)  7.18 us
    ppermute x1, starting transfers between devices, local(): right = lax.ppermute(own, 'azim', toward_left)  6.62 us
    pallas_call x1, Pallas kernels, local(): pl.pallas_call(second_kernel, out_shape=(rows_of(2 * CELLS), rows_of(2 *...  6.3 us
    pallas_call x1, Pallas kernels, local(): pl.pallas_call(first_kernel, out_shape=rows_of(half + 3 * NB), in_specs=[...  5.78 us
    ppermute x1, starting transfers between devices, local(): r1 = lax.ppermute(r0, 'depth', far)  4.15 us
    ppermute x1, starting transfers between devices, local(): q4 = lax.ppermute(q1, 'depth', pairs)  3.79 us
    ppermute x1, waiting for transfers between devices, local(): q2 = lax.ppermute(state, 'depth', back)  3.53 us
  transfers between devices with their start and end apart: 10, of which 5 were waited for; matrix products, arithmetic and copies ran while one was open for 1% of the time, Pallas kernels for 0%

profile of v1, /device:TPU:1, one launch (start us, length us, event | category | flops | bytes accessed | tf_op | source)
XLA Modules:
  0.0 74.6 jit_solution(434860460075023368)
XLA Ops:
  0.6 1.5 %pack.1 = f32[128,128]{1,0:T(8,128)} custom-call(s32[1,4]{1,0:T(1,128)} %count.1, f32[8,128]{1,0:T(8,128)} %bitcast.21, f32[8,128]{1,0:T(8,128)} %bitcast.22, f32[4,128]{1,0:T(4,128)} %bitcast.23, s32[96,128]{1,0:T(8,128)} %bitcast.20), custom_call_target="tpu_custom_call" | custom-call | tf_op jit(solution)/shard_map/pack/pallas_call | solution.py:272
  2.1 0.0 copy-start.3
  2.1 6.6 %collective-permute-start = (f32[128,128]{1,0:T(8,128)}, f32[128,128]{1,0:T(8,128)S(1)}, u32[]{:S(2)}, u32[]{:S(2)}) collective-permute-start(f32[128,128]{1,0:T(8,128)} %pack.1), channel_id=1, source_target_pairs={{0,7},{1,0},{2,1},{3,2},{4,3},{5,4},{6,5},{7,6},{8,15},{9,8},{10,9... | collective-permute-start | bytes 196616 | tf_op jit(solution)/shard_map/ppermute | solution.py:285
  8.7 1.6 %collective-permute-done = f32[128,128]{1,0:T(8,128)S(1)} collective-permute-done((f32[128,128]{1,0:T(8,128)}, f32[128,128]{1,0:T(8,128)S(1)}, u32[]{:S(2)}, u32[]{:S(2)}) %collective-permute-start) | collective-permute-done | bytes 65568 | tf_op jit(solution)/shard_map/ppermute | solution.py:285
  10.4 0.0 copy-done.3
  10.4 0.0 copy-start
  10.4 2.6 %collective-permute-start.1 = (f32[232,128]{1,0:T(8,128)S(1)}, f32[232,128]{1,0:T(8,128)S(1)}, u32[]{:S(2)}, u32[]{:S(2)}) collective-permute-start(f32[232,128]{1,0:T(8,128)S(1)} %pad_maximum_fusion.q0), channel_id=1, source_target_pairs={{8,24},{16,0},{24,40},{32,16},{40,56},{48,32},{56,72},{64,48},{72,... | collective-permute-start | bytes 356360 | tf_op jit(solution)/shard_map/ppermute | solution.py:288
  13.1 0.3 collective-permute-start.3
  13.4 1.5 %collective-permute-done.1.q1 = f32[232,128]{1,0:T(8,128)S(1)} collective-permute-done((f32[232,128]{1,0:T(8,128)S(1)}, f32[232,128]{1,0:T(8,128)S(1)}, u32[]{:S(2)}, u32[]{:S(2)}) %collective-permute-start.1) | collective-permute-done | bytes 118816 | tf_op jit(solution)/shard_map/ppermute | solution.py:288
  14.9 0.0 copy-start.5
  14.9 3.8 %collective-permute-start.4 = (f32[232,128]{1,0:T(8,128)S(1)}, f32[232,128]{1,0:T(8,128)S(1)}, u32[]{:S(2)}, u32[]{:S(2)}) collective-permute-start(f32[232,128]{1,0:T(8,128)S(1)} %collective-permute-done.1.q1), channel_id=1, source_target_pairs={{0,8},{8,0},{16,24},{24,16},{32,40},{40,32},{48,56},{56,48},{64,72... | collective-permute-start | bytes 356360 | tf_op jit(solution)/shard_map/ppermute | solution.py:291
  18.7 1.3 %collective-permute-start.2 = (f32[64,128]{1,0:T(8,128)S(1)}, f32[64,128]{1,0:T(8,128)S(1)}, u32[]{:S(2)}, u32[]{:S(2)}) collective-permute-start(f32[64,128]{1,0:T(8,128)S(1)} %pad_maximum_fusion.1), channel_id=1, source_target_pairs={{24,8},{0,16},{40,24},{16,32},{56,40},{32,48},{72,56},{48,64},{88,... | collective-permute-start | bytes 98312 | tf_op jit(solution)/shard_map/ppermute | solution.py:289
  20.0 3.5 %collective-permute-done.2.q2 = f32[64,128]{1,0:T(8,128)S(1)} collective-permute-done((f32[64,128]{1,0:T(8,128)S(1)}, f32[64,128]{1,0:T(8,128)S(1)}, u32[]{:S(2)}, u32[]{:S(2)}) %collective-permute-start.2) | collective-permute-done | bytes 32800 | tf_op jit(solution)/shard_map/ppermute | solution.py:289
  23.5 0.0 copy-start.7
  23.5 0.0 collective-permute-done.3.q3
  23.5 0.0 copy-start.1
  23.5 0.0 collective-permute-done.4.q4
  23.5 0.0 copy-start.2
  23.5 0.0 copy-done
  23.6 0.0 copy-done.5
  23.6 0.6 copy-done.7
  24.1 0.0 copy-done.1
  24.2 0.0 copy-done.2
  24.2 5.8 %first_step.1 = f32[104,128]{1,0:T(8,128)} custom-call(s32[1]{0:T(128)} %bitcast.parity, f32[232,128]{1,0:T(8,128)} %copy-done, f32[232,128]{1,0:T(8,128)} %copy-done.5, f32[64,128]{1,0:T(8,128)} %copy-done.7, f32[232,128]{1,0:T(8,128)} %copy-done.1, f32[232,128]{1,0:T(8,128)} %copy-done.2), custom_call_target="tpu_custom_call" | custom-call | tf_op jit(solution)/shard_map/first_step/pallas_call | solution.py:292
  30.0 0.0 collective-permute-start.5
  30.0 0.8 %slice.24 = f32[32,128]{1,0:T(8,128)S(1)} slice(f32[104,128]{1,0:T(8,128)} %first_step.1), slice={[0:32], [0:128]} | slice | bytes 32768 | tf_op jit(solution)/shard_map/slice | solution.py:302
  30.8 7.2 %collective-permute-done.5.left = f32[104,128]{1,0:T(8,128)S(1)} collective-permute-done((f32[104,128]{1,0:T(8,128)}, f32[104,128]{1,0:T(8,128)S(1)}, u32[]{:S(2)}, u32[]{:S(2)}) %collective-permute-start.5) | collective-permute-done | bytes 53280 | tf_op jit(solution)/shard_map/ppermute | solution.py:301
  37.9 0.0 copy-start.6
  37.9 0.0 copy-start.4
  38.0 4.1 %collective-permute-start.6 = (f32[64,128]{1,0:T(8,128)S(1)}, f32[64,128]{1,0:T(8,128)S(1)}, u32[]{:S(2)}, u32[]{:S(2)}) collective-permute-start(f32[64,128]{1,0:T(8,128)S(1)} %pad_maximum_fusion.2.r0), channel_id=1, source_target_pairs={{8,24},{16,0},{24,40},{32,16},{40,56},{48,32},{56,72},{64,48},{72,... | collective-permute-start | bytes 98312 | tf_op jit(solution)/shard_map/ppermute | solution.py:303
  42.1 0.1 collective-permute-start.8
  42.2 1.3 %collective-permute-start.7 = (f32[64,128]{1,0:T(8,128)S(1)}, f32[64,128]{1,0:T(8,128)S(1)}, u32[]{:S(2)}, u32[]{:S(2)}) collective-permute-start(f32[64,128]{1,0:T(8,128)S(1)} %pad_maximum_fusion.2.r0), channel_id=1, source_target_pairs={{24,8},{0,16},{40,24},{16,32},{56,40},{32,48},{72,56},{48,64},{88,... | collective-permute-start | bytes 98312 | tf_op jit(solution)/shard_map/ppermute | solution.py:304
  43.5 0.0 collective-permute-done.6.r1
  43.5 0.0 copy-start.8
  43.5 1.9 %collective-permute-start.9 = (f32[64,128]{1,0:T(8,128)S(1)}, f32[64,128]{1,0:T(8,128)S(1)}, u32[]{:S(2)}, u32[]{:S(2)}) collective-permute-start(f32[64,128]{1,0:T(8,128)S(1)} %collective-permute-done.6.r1), channel_id=1, source_target_pairs={{0,8},{8,0},{16,24},{24,16},{32,40},{40,32},{48,56},{56,48},{64,72... | collective-permute-start | bytes 98312 | tf_op jit(solution)/shard_map/ppermute | solution.py:306
  45.5 0.0 collective-permute-done.8.r3
  45.5 0.0 copy-start.9
  45.5 1.4 %collective-permute-done.7.r2 = f32[64,128]{1,0:T(8,128)S(1)} collective-permute-done((f32[64,128]{1,0:T(8,128)S(1)}, f32[64,128]{1,0:T(8,128)S(1)}, u32[]{:S(2)}, u32[]{:S(2)}) %collective-permute-start.7) | collective-permute-done | bytes 32800 | tf_op jit(solution)/shard_map/ppermute | solution.py:304
  46.9 0.0 collective-permute-done.9.r4
  46.9 0.0 copy-done.6
  46.9 0.0 copy-done.4
  46.9 0.0 copy-done.8
  46.9 0.0 copy-done.9
  46.9 0.6 copy-done.10
  47.5 0.0 copy-done.11
  47.5 6.3 %second_step.1 = (f32[8,128]{1,0:T(8,128)}, f32[8,128]{1,0:T(8,128)}, f32[4,128]{1,0:T(4,128)}, f32[128,128]{1,0:T(8,128)}) custom-call(s32[1]{0:T(128)} %bitcast.parity, s32[4,128]{1,0:T(4,128)} %bitcast.24, s32[4,128]{1,0:T(4,128)} %bitcast.25, f32[104,128]{1,0:T(8,128)} %copy-done.6, f32[64,128]{1,0:T(8,128)} %copy-done.4, f32[64,128]{1,0:T(8,128)} %copy-done.8, ...), custom_call_target="tpu_custom_call" | custom-call | tf_op jit(solution)/shard_map/second_step/pallas_call | solution.py:307
  53.8 19.2 %all_to_all.11 = f32[128,1,128]{2,1,0:T(1,128)} all-to-all(f32[128,1,128]{2,1,0:T(1,128)} %bitcast.19), channel_id=1, replica_groups=mesh['depth'=16,'azim'=8] {'depth','azim'}, dimensions={0} | all-to-all | bytes 131072 | tf_op jit(solution)/shard_map/all_to_all | solution.py:316
  73.0 1.6 %soil.1 = f32[4,16,128]{2,1,0:T(8,128)} custom-call(f32[128,128]{1,0:T(8,128)} %bitcast.18, f32[4,16,128]{2,1,0:T(8,128)} %stress.1, f32[3,16,128]{2,1,0:T(8,128)} %rate.1, f32[3,16,128]{2,1,0:T(8,128)} %couple.1), custom_call_target="tpu_custom_call" | custom-call | tf_op jit(solution)/shard_map/soil/pallas_call | solution.py:317
  (9 shorter events, 0.0 us)
Async XLA Ops:
  2.1 8.3 %copy-start.3 = (f32[128,128]{1,0:T(8,128)S(1)}, f32[128,128]{1,0:T(8,128)}, u32[]{:S(2)}) copy-start(f32[128,128]{1,0:T(8,128)} %pack.1) | copy-start | bytes 196612
  2.1 8.3 %collective-permute-start = (f32[128,128]{1,0:T(8,128)}, f32[128,128]{1,0:T(8,128)S(1)}, u32[]{:S(2)}, u32[]{:S(2)}) collective-permute-start(f32[128,128]{1,0:T(8,128)} %pack.1), channel_id=1, source_target_pairs={{0,7},{1,0},{2,1},{3,2},{4,3},{5,4},{6,5},{7,6},{8,15},{9,8},{10,9... | collective-permute-start | bytes 196616 | tf_op jit(solution)/shard_map/ppermute | solution.py:285
  10.4 13.1 %copy-start = (f32[232,128]{1,0:T(8,128)}, f32[232,128]{1,0:T(8,128)S(1)}, u32[]{:S(2)}) copy-start(f32[232,128]{1,0:T(8,128)S(1)} %pad_maximum_fusion.q0) | copy-start | bytes 356356
  10.4 4.5 %collective-permute-start.1 = (f32[232,128]{1,0:T(8,128)S(1)}, f32[232,128]{1,0:T(8,128)S(1)}, u32[]{:S(2)}, u32[]{:S(2)}) collective-permute-start(f32[232,128]{1,0:T(8,128)S(1)} %pad_maximum_fusion.q0), channel_id=1, source_target_pairs={{8,24},{16,0},{24,40},{32,16},{40,56},{48,32},{56,72},{64,48},{72,... | collective-permute-start | bytes 356360 | tf_op jit(solution)/shard_map/ppermute | solution.py:288
  13.1 10.4 %collective-permute-start.3 = (f32[232,128]{1,0:T(8,128)S(1)}, f32[232,128]{1,0:T(8,128)S(1)}, u32[]{:S(2)}, u32[]{:S(2)}) collective-permute-start(f32[232,128]{1,0:T(8,128)S(1)} %pad_maximum_fusion.q0), channel_id=1, source_target_pairs={{0,8},{8,0},{16,24},{24,16},{32,40},{40,32},{48,56},{56,48},{64,72... | collective-permute-start | bytes 356360 | tf_op jit(solution)/shard_map/ppermute | solution.py:290
  14.9 8.7 %copy-start.5 = (f32[232,128]{1,0:T(8,128)}, f32[232,128]{1,0:T(8,128)S(1)}, u32[]{:S(2)}) copy-start(f32[232,128]{1,0:T(8,128)S(1)} %collective-permute-done.1.q1) | copy-start | bytes 356356
  14.9 8.6 %collective-permute-start.4 = (f32[232,128]{1,0:T(8,128)S(1)}, f32[232,128]{1,0:T(8,128)S(1)}, u32[]{:S(2)}, u32[]{:S(2)}) collective-permute-start(f32[232,128]{1,0:T(8,128)S(1)} %collective-permute-done.1.q1), channel_id=1, source_target_pairs={{0,8},{8,0},{16,24},{24,16},{32,40},{40,32},{48,56},{56,48},{64,72... | collective-permute-start | bytes 356360 | tf_op jit(solution)/shard_map/ppermute | solution.py:291
  18.7 4.8 %collective-permute-start.2 = (f32[64,128]{1,0:T(8,128)S(1)}, f32[64,128]{1,0:T(8,128)S(1)}, u32[]{:S(2)}, u32[]{:S(2)}) collective-permute-start(f32[64,128]{1,0:T(8,128)S(1)} %pad_maximum_fusion.1), channel_id=1, source_target_pairs={{24,8},{0,16},{40,24},{16,32},{56,40},{32,48},{72,56},{48,64},{88,... | collective-permute-start | bytes 98312 | tf_op jit(solution)/shard_map/ppermute | solution.py:289
  23.5 0.6 copy-start.7
  23.5 0.7 copy-start.1
  23.5 0.7 copy-start.2
  30.0 7.9 %collective-permute-start.5 = (f32[104,128]{1,0:T(8,128)}, f32[104,128]{1,0:T(8,128)S(1)}, u32[]{:S(2)}, u32[]{:S(2)}) collective-permute-start(f32[104,128]{1,0:T(8,128)} %first_step.1), channel_id=1, source_target_pairs={{0,1},{1,2},{2,3},{3,4},{4,5},{5,6},{6,7},{7,0},{8,9},{9,10},{10,1... | collective-permute-start | bytes 159752 | tf_op jit(solution)/shard_map/ppermute | solution.py:301
  37.9 8.9 %copy-start.6 = (f32[104,128]{1,0:T(8,128)}, f32[104,128]{1,0:T(8,128)S(1)}, u32[]{:S(2)}) copy-start(f32[104,128]{1,0:T(8,128)S(1)} %collective-permute-done.5.left) | copy-start | bytes 159748
  37.9 8.9 %copy-start.4 = (f32[64,128]{1,0:T(8,128)}, f32[64,128]{1,0:T(8,128)S(1)}, u32[]{:S(2)}) copy-start(f32[64,128]{1,0:T(8,128)S(1)} %pad_maximum_fusion.2.r0) | copy-start | bytes 98308
  38.0 5.5 %collective-permute-start.6 = (f32[64,128]{1,0:T(8,128)S(1)}, f32[64,128]{1,0:T(8,128)S(1)}, u32[]{:S(2)}, u32[]{:S(2)}) collective-permute-start(f32[64,128]{1,0:T(8,128)S(1)} %pad_maximum_fusion.2.r0), channel_id=1, source_target_pairs={{8,24},{16,0},{24,40},{32,16},{40,56},{48,32},{56,72},{64,48},{72,... | collective-permute-start | bytes 98312 | tf_op jit(solution)/shard_map/ppermute | solution.py:303
  42.1 3.4 %collective-permute-start.8 = (f32[64,128]{1,0:T(8,128)S(1)}, f32[64,128]{1,0:T(8,128)S(1)}, u32[]{:S(2)}, u32[]{:S(2)}) collective-permute-start(f32[64,128]{1,0:T(8,128)S(1)} %pad_maximum_fusion.2.r0), channel_id=1, source_target_pairs={{0,8},{8,0},{16,24},{24,16},{32,40},{40,32},{48,56},{56,48},{64,72... | collective-permute-start | bytes 98312 | tf_op jit(solution)/shard_map/ppermute | solution.py:305
  42.2 4.7 %collective-permute-start.7 = (f32[64,128]{1,0:T(8,128)S(1)}, f32[64,128]{1,0:T(8,128)S(1)}, u32[]{:S(2)}, u32[]{:S(2)}) collective-permute-start(f32[64,128]{1,0:T(8,128)S(1)} %pad_maximum_fusion.2.r0), channel_id=1, source_target_pairs={{24,8},{0,16},{40,24},{16,32},{56,40},{32,48},{72,56},{48,64},{88,... | collective-permute-start | bytes 98312 | tf_op jit(solution)/shard_map/ppermute | solution.py:304
  43.5 3.4 %copy-start.8 = (f32[64,128]{1,0:T(8,128)}, f32[64,128]{1,0:T(8,128)S(1)}, u32[]{:S(2)}) copy-start(f32[64,128]{1,0:T(8,128)S(1)} %collective-permute-done.6.r1) | copy-start | bytes 98308
  43.5 3.3 %collective-permute-start.9 = (f32[64,128]{1,0:T(8,128)S(1)}, f32[64,128]{1,0:T(8,128)S(1)}, u32[]{:S(2)}, u32[]{:S(2)}) collective-permute-start(f32[64,128]{1,0:T(8,128)S(1)} %collective-permute-done.6.r1), channel_id=1, source_target_pairs={{0,8},{8,0},{16,24},{24,16},{32,40},{40,32},{48,56},{56,48},{64,72... | collective-permute-start | bytes 98312 | tf_op jit(solution)/shard_map/ppermute | solution.py:306
  45.5 1.4 %copy-start.9 = (f32[64,128]{1,0:T(8,128)}, f32[64,128]{1,0:T(8,128)S(1)}, u32[]{:S(2)}) copy-start(f32[64,128]{1,0:T(8,128)S(1)} %collective-permute-done.8.r3) | copy-start | bytes 98308
  46.9 0.6 copy-start.10
  46.9 0.6 copy-start.11

commit v2 on v1

v2 whole, which is shorter than its diff:
```python
import jax
import jax.numpy as jnp
from jax import lax
from jax.experimental import pallas as pl
from jax.experimental.pallas import tpu as pltpu
from jax.sharding import PartitionSpec as P

step_dt = 0.05
sound_sq = 1.0
visc_alpha = 0.5
soil_dt = 0.1
shear_mod = 1.0
bulk_mod = 2.0
cohesion = 1.0
friction = 0.3

CELLS = 4
NB = 24
NT = 3
WIDE = 8
RING = 6
S = 128
PX, PY, PM, PVX, PVY, PL = range(6)


def pack_kernel(count, pos, vel, mass, nb, out):
    lane = lax.broadcasted_iota(jnp.int32, (1, S), 1)
    for c in range(CELLS):
        live = (lane < count[0, c]).astype(jnp.float32)
        out[NB * c : NB * c + NB, :] = nb[pl.ds(c, NB, stride=CELLS), :].astype(jnp.float32)
        base = NB * CELLS + 8 * c
        out[base + PX : base + PX + 1, :] = pos[c : c + 1, :]
        out[base + PY : base + PY + 1, :] = pos[CELLS + c : CELLS + c + 1, :]
        out[base + PM : base + PM + 1, :] = mass[c : c + 1, :] * live
        out[base + PVX : base + PVX + 1, :] = vel[c : c + 1, :]
        out[base + PVY : base + PVY + 1, :] = vel[CELLS + c : CELLS + c + 1, :]
        out[base + PL : base + PL + 1, :] = live
        out[base + PL + 1 : base + 8, :] = jnp.zeros((2, S), jnp.float32)


def spread(row):
    return jnp.broadcast_to(row, (8, S))


def pick(tables, slot, masks):
    out = None
    for table, mask in zip(tables, masks):
        got = jnp.take_along_axis(table, slot, axis=1)
        out = got if out is None else jnp.where(mask, got, out)
    return out


def step_body(sign, frame, lists, pair, press):
    near = [(dr, dc) for dr in (-1, 0, 1) for dc in (-1, 0, 1)]
    numbers = [3 * (1 + sign * dr) + dc + 1 for dr, dc in near]

    def codes(start):
        code = lists[pl.ds(start, 8), :].astype(jnp.int32)
        which = code >> 7
        return code & (S - 1), which, [which == n for n in numbers]

    def density(row, carry):
        for col in range(RING):
            centre = pl.multiple_of(row * (WIDE * 8), 8) + (WIDE + col + 1) * 8
            own_x = spread(frame[pl.ds(centre + PX, 1), :])
            own_y = spread(frame[pl.ds(centre + PY, 1), :])
            own_m = frame[pl.ds(centre + PM, 1), :]

            def table(k):
                return [spread(frame[pl.ds(centre + (dr * WIDE + dc) * 8 + k, 1), :]) for dr, dc in near]

            xs, ys, ms = table(PX), table(PY), table(PM)
            total = jnp.zeros((8, S), jnp.float32)
            for t in range(NT):
                slot, which, masks = codes(pl.multiple_of(row * (RING * NB), 8) + col * NB + 8 * t)
                third = (which * 11) >> 5
                dx = own_x - ((third - 1).astype(jnp.float32) + pick(xs, slot, masks))
                dy = own_y - ((which - 3 * third - 1).astype(jnp.float32) + pick(ys, slot, masks))
                mass = pick(ms, slot, masks)
                dist = jnp.sqrt(dx * dx + dy * dy)
                tail = jnp.maximum(1.0 - dist, 0.0)
                cube = tail * tail * tail
                total = total + mass * (cube * tail * (4.0 * dist + 1.0))
                base = pl.multiple_of(row * (RING * NT * 40), 8) + (col * NT + t) * 40
                pair[pl.ds(base, 8), :] = dx
                pair[pl.ds(base + 8, 8), :] = dy
                pair[pl.ds(base + 16, 8), :] = mass
                pair[pl.ds(base + 24, 8), :] = dist * dist + 0.01
                pair[pl.ds(base + 32, 8), :] = 20.0 * cube
            rho = own_m + jnp.sum(total, axis=0, keepdims=True) + jnp.where(own_m > 0.0, 0.0, 1.0)
            press[pl.ds(pl.multiple_of(row * (RING * 8), 8) + col * 8, 1), :] = rho
        return carry

    lax.fori_loop(0, 3, density, 0)

    def term(rho):
        return sound_sq * (rho - 1.0) / (rho * rho)

    def force(c):
        cell = RING + 1 + c
        centre = (2 * WIDE + 2 + c) * 8
        own = frame[centre : centre + 8, :]
        own_rho = press[cell * 8 : cell * 8 + 1, :]
        own_vx, own_vy = spread(own[PVX : PVX + 1]), spread(own[PVY : PVY + 1])
        own_q, own_r = spread(term(own_rho)), spread(own_rho)
        vxs, vys, rhos = [], [], []
        for dr, dc in near:
            tile = centre + (dr * WIDE + dc) * 8
            vxs.append(spread(frame[tile + PVX : tile + PVX + 1, :]))
            vys.append(spread(frame[tile + PVY : tile + PVY + 1, :]))
            tile = (cell + dr * RING + dc) * 8
            rhos.append(spread(press[tile : tile + 1, :]))
        ax = jnp.zeros((8, S), jnp.float32)
        ay = jnp.zeros((8, S), jnp.float32)
        for t in range(NT):
            slot, _, masks = codes(cell * NB + 8 * t)
            base = (cell * NT + t) * 40
            dx = pair[base : base + 8, :]
            dy = pair[base + 8 : base + 16, :]
            mass = pair[base + 16 : base + 24, :]
            soft = pair[base + 24 : base + 32, :]
            slope = pair[base + 32 : base + 40, :]
            rho = pick(rhos, slot, masks)
            vdot = (own_vx - pick(vxs, slot, masks)) * dx + (own_vy - pick(vys, slot, masks)) * dy
            visc = visc_alpha * jnp.maximum(-vdot, 0.0) / (soft * (0.5 * (own_r + rho)))
            coef = mass * (own_q + term(rho) + visc) * slope
            ax = ax + coef * dx
            ay = ay + coef * dy
        live = own[PL : PL + 1]
        vx = own[PVX : PVX + 1] + step_dt * jnp.sum(ax, axis=0, keepdims=True) * live
        vy = own[PVY : PVY + 1] + step_dt * jnp.sum(ay, axis=0, keepdims=True) * live
        x = own[PX : PX + 1] + step_dt * vx * live
        y = own[PY : PY + 1] + step_dt * vy * live
        return x, y, own[PM : PM + 1], vx, vy, live, own_rho

    return force


LISTS = NB * CELLS
STATE = 8 * CELLS
HEAD = LISTS
MORE = LISTS + 2 * STATE
BUNDLE = MORE + 3 * NB


def first_kernel(parity, q0, q1, outer, q3, out, frame, lists, pair, press):
    sign = 1 - 2 * parity[0]
    two = 2 * STATE
    frame[0:two, :] = outer[BUNDLE : BUNDLE + two, :]
    frame[two : 2 * two, :] = outer[HEAD:MORE, :]
    frame[2 * two : 3 * two, :] = q0[HEAD:MORE, :]
    frame[3 * two : 4 * two, :] = q3[HEAD:MORE, :]
    frame[4 * two : 5 * two, :] = q1[...]
    for r, ref in enumerate((outer, q0, q3)):
        base = r * RING * NB
        lists[base : base + 3 * NB, :] = ref[NB:LISTS, :]
        lists[base + 3 * NB : base + 6 * NB, :] = ref[MORE:BUNDLE, :]
        out[STATE + r * NB : STATE + (r + 1) * NB, :] = ref[LISTS - NB : LISTS, :]
    force = step_body(sign, frame, lists, pair, press)
    for c in range(CELLS):
        x, y, m, vx, vy, live, _ = force(c)
        for k, v in enumerate((x, y, m, vx, vy, live)):
            out[8 * c + k : 8 * c + k + 1, :] = v
        out[8 * c + 6 : 8 * c + 8, :] = jnp.zeros((2, S), jnp.float32)


def second_kernel(parity, dest, shell, left, r0, r1, outer, r3, q0, before, q3, pos_out, vel_out, rho_out, part, frame, lists, pair, press):
    sign = 1 - 2 * parity[0]
    two = 2 * STATE
    frame[0:two, :] = outer[two : 2 * two, :]
    frame[two : 2 * two, :] = outer[0:two, :]
    frame[2 * two : 3 * two, :] = r0[...]
    frame[3 * two : 4 * two, :] = r3[...]
    frame[4 * two : 5 * two, :] = r1[...]
    for r, ref in enumerate((before, q0, q3)):
        base = r * RING * NB
        lists[base : base + NB, :] = left[STATE + r * NB : STATE + (r + 1) * NB, :]
        lists[base + NB : base + 5 * NB, :] = ref[0:LISTS, :]
        lists[base + 5 * NB : base + 6 * NB, :] = ref[MORE : MORE + NB, :]
    force = step_body(sign, frame, lists, pair, press)
    total = jnp.zeros((S, S), jnp.float32)
    devices = lax.broadcasted_iota(jnp.int32, (S, S), 0)
    shells = lax.broadcasted_iota(jnp.int32, (16, S), 0)
    for c in range(CELLS):
        x, y, m, vx, vy, live, rho = force(c)
        pos_out[c : c + 1, :] = x
        pos_out[CELLS + c : CELLS + c + 1, :] = y
        vel_out[c : c + 1, :] = vx
        vel_out[CELLS + c : CELLS + c + 1, :] = vy
        rho_out[c : c + 1, :] = rho
        loads = (m * vx, m * vy, m * (sound_sq * (rho - 1.0)), 0.5 * m * (vx * vx + vy * vy))
        owner = (devices == dest[c : c + 1, :]).astype(jnp.float32)
        member = shells == shell[c : c + 1, :]
        spreads = [jnp.where(member, load, 0.0) for load in loads]
        spreads.append(jnp.zeros((S - 64, S), jnp.float32))
        total = total + lax.dot_general(
            owner,
            jnp.concatenate(spreads, axis=0),
            (((1,), (1,)), ((), ())),
            precision=lax.Precision.HIGHEST,
            preferred_element_type=jnp.float32,
        )
    part[...] = total


def soil_kernel(arrived, stress, rate, couple, out):
    total = jnp.sum(arrived[...], axis=0, keepdims=True)
    lane = lax.broadcasted_iota(jnp.int32, (16, S), 1)
    row = lax.broadcasted_iota(jnp.int32, (16, S), 0)
    force_x, force_y, force_p, force_e = [
        jnp.sum(jnp.where(lane == row + 16 * k, total, 0.0), axis=1, keepdims=True) for k in range(4)
    ]
    exx = rate[0] + couple[0] * force_x
    eyy = rate[1] + couple[1] * force_y
    exy = rate[2] + couple[2] * force_p
    ezz = -0.5 * (couple[0] + couple[1]) * force_e
    trace = exx + eyy + ezz
    sxx = stress[0] + soil_dt * (2.0 * shear_mod * (exx - trace / 3.0) + bulk_mod * trace)
    syy = stress[1] + soil_dt * (2.0 * shear_mod * (eyy - trace / 3.0) + bulk_mod * trace)
    szz = stress[2] + soil_dt * (2.0 * shear_mod * (ezz - trace / 3.0) + bulk_mod * trace)
    sxy = stress[3] + soil_dt * 2.0 * shear_mod * exy
    first = sxx + syy + szz
    mean = first / 3.0
    dxx = sxx - mean
    dyy = syy - mean
    dzz = szz - mean
    root = jnp.sqrt(0.5 * (dxx * dxx + dyy * dyy + dzz * dzz) + sxy * sxy)
    radius = jnp.maximum(cohesion - friction * first, 0.2 * cohesion)
    factor = radius / jnp.maximum(root, radius)
    out[0] = mean + factor * dxx
    out[1] = mean + factor * dyy
    out[2] = mean + factor * dzz
    out[3] = factor * sxy


def rows_of(n):
    return jax.ShapeDtypeStruct((n, S), jnp.float32)


VM = pl.BlockSpec(memory_space=pltpu.MemorySpace.VMEM)
SM = pl.BlockSpec(memory_space=pltpu.MemorySpace.SMEM)
WORK = [
    pltpu.VMEM((5 * WIDE * 8, S), jnp.float32),
    pltpu.VMEM((3 * RING * NB, S), jnp.float32),
    pltpu.VMEM((3 * RING * NT * 40, S), jnp.float32),
    pltpu.VMEM((3 * RING * 8, S), jnp.float32),
]


def local(
    fluid_pos,
    fluid_vel,
    fluid_mass,
    cell_count,
    nb_list,
    iface_dest,
    iface_shell,
    soil_stress,
    soil_rate,
    soil_couple,
):
    n_depth = lax.axis_size("depth")
    n_azim = lax.axis_size("azim")
    parity = (lax.axis_index("depth") % 2).astype(jnp.int32).reshape(1)
    toward_left = [(i, (i - 1) % n_azim) for i in range(n_azim)]
    toward_right = [(i, (i + 1) % n_azim) for i in range(n_azim)]
    pairs = [(i, i ^ 1) for i in range(n_depth)]
    facing = [(i, i + 1 if i % 2 else i - 1) for i in range(n_depth)]
    facing = [(i, j) for i, j in facing if 0 <= j < n_depth]

    own = pl.pallas_call(
        pack_kernel,
        out_shape=rows_of(LISTS + STATE),
        in_specs=[SM, VM, VM, VM, VM],
        out_specs=VM,
        name="pack",
    )(
        cell_count,
        fluid_pos.reshape(2 * CELLS, S),
        fluid_vel.reshape(2 * CELLS, S),
        fluid_mass.reshape(CELLS, S),
        nb_list.reshape(NB * CELLS, S),
    )
    right = lax.ppermute(own, "azim", toward_left)
    q0 = jnp.concatenate([own, right[HEAD:], right[: 3 * NB]], axis=0)
    q3 = lax.ppermute(q0, "depth", pairs)
    outer = lax.ppermute(jnp.concatenate([q0, q3[HEAD:MORE]], axis=0), "depth", facing)
    q1 = lax.ppermute(outer[HEAD:MORE], "depth", pairs)
    mid = pl.pallas_call(
        first_kernel,
        out_shape=rows_of(STATE + 3 * NB),
        in_specs=[SM] + [VM] * 4,
        out_specs=VM,
        scratch_shapes=WORK,
        name="first_step",
    )(parity, q0, q1, outer, q3)

    left = lax.ppermute(mid, "azim", toward_right)
    r0 = jnp.concatenate([left[:STATE], mid[:STATE]], axis=0)
    r3 = lax.ppermute(r0, "depth", pairs)
    beyond = lax.ppermute(jnp.concatenate([r0, r3], axis=0), "depth", facing)
    r1 = lax.ppermute(beyond[: 2 * STATE], "depth", pairs)
    pos, vel, rho, part = pl.pallas_call(
        second_kernel,
        out_shape=(rows_of(2 * CELLS), rows_of(2 * CELLS), rows_of(CELLS), rows_of(S)),
        in_specs=[SM] + [VM] * 10,
        out_specs=(VM, VM, VM, VM),
        scratch_shapes=WORK,
        name="second_step",
    )(parity, iface_dest.reshape(CELLS, S), iface_shell.reshape(CELLS, S), left, r0, r1, beyond, r3, q0, outer, q3)

    arrived = lax.all_to_all(part, ("depth", "azim"), split_axis=0, concat_axis=0, tiled=True)
    stress_out = pl.pallas_call(
        soil_kernel,
        out_shape=jax.ShapeDtypeStruct(soil_stress.shape, jnp.float32),
        in_specs=[VM] * 4,
        out_specs=VM,
        name="soil",
    )(arrived, soil_stress, soil_rate, soil_couple)
    return (
        pos.reshape(fluid_pos.shape),
        vel.reshape(fluid_vel.shape),
        rho.reshape(fluid_mass.shape),
        stress_out,
    )


def solution(mesh):
    return jax.shard_map(
        local,
        mesh=mesh,
        in_specs=(
            P(None, "depth", "azim", None),
            P(None, "depth", "azim", None),
            P("depth", "azim", None),
            P("depth", "azim"),
            P(None, "depth", "azim", None),
            P(("depth", "azim"), None, None),
            P(("depth", "azim"), None),
            P(None, ("depth", "azim"), None),
            P(None, ("depth", "azim"), None),
            P(None, ("depth", "azim"), None),
        ),
        out_specs=(
            P(None, "depth", "azim", None),
            P(None, "depth", "azim", None),
            P("depth", "azim", None),
            P(None, ("depth", "azim"), None),
        ),
        check_vma=False,
    )
```

time: 75.1 us -> 68.9 us (0.917)
  starting transfers between devices: 22.1 us -> 15.7 us
  waiting for transfers between devices: 15.3 us -> 19.2 us
  Pallas kernels: 15.2 us -> 12 us
  blocking collectives: 19.2 us -> 17.6 us
  local copies, waits for them, and re-layouts: 2.03 us -> 3.21 us
    ppermute x6 -> x4, starting transfers between devices: 15.1 us -> 6.66 us  [the longest x1 3.77 us: local(): beyond = lax.ppermute(jnp.concatenate([r0, r3], axis=0), 'depth', facing)]
    pallas_call x2, Pallas kernels: 7.28 us -> 5.65 us  [the longest x1 4.14 us: local(): pl.pallas_call(first_kernel, out_shape=rows_of(STATE + 3 * NB), in_specs=...]
    all_to_all x1, blocking collectives: 19.2 us -> 17.6 us  [local(): lax.all_to_all(part, ('depth', 'azim'), split_axis=0, concat_axis=0, tile...]
    ppermute x6 -> x4, waiting for transfers between devices: 6.48 us -> 8.06 us  [the longest x1 3.73 us: local(): lax.ppermute(jnp.concatenate([q0, q3[HEAD:MORE]], axis=0), 'depth', facing)]
    pallas_call x1, Pallas kernels: 6.3 us -> 4.74 us  [local(): pl.pallas_call(second_kernel, out_shape=(rows_of(2 * CELLS), rows_of(2 *...]
    ppermute x1, starting transfers between devices: 0.25 us -> 1.61 us  [local(): q3 = lax.ppermute(q0, 'depth', pairs)]
    unnamed x24 -> x20, local copies, waits for them, and re-layouts: 1.27 us -> 2.44 us
    ppermute x1, waiting for transfers between devices: 0.01 us -> 0.97 us  [local(): q3 = lax.ppermute(q0, 'depth', pairs)]
  transfers between devices with their start and end apart: 10 -> 8, of which waited for: 5 -> 8; matrix products, arithmetic and copies ran while one was open for 1% -> 1% of each run, Pallas kernels for 0% -> 0%
where the time goes in v2:
time: 68.9 us; the launch traced here: 68.5 us
  waiting for transfers between devices  19.2 us (28%)
  blocking collectives  17.6 us (26%)
  starting transfers between devices  15.7 us (23%)
  Pallas kernels  12 us (17%)
  local copies, waits for them, and re-layouts  3.21 us (5%)
  between operations  0.74 us (1%)
    all_to_all x1, blocking collectives, local(): lax.all_to_all(part, ('depth', 'azim'), split_axis=0, concat_axis=0, tile...  17.6 us
    ppermute x1, waiting for transfers between devices, local(): left = lax.ppermute(mid, 'azim', toward_right)  7.69 us
    ppermute x1, starting transfers between devices, local(): right = lax.ppermute(own, 'azim', toward_left)  6.62 us
    pallas_call x1, Pallas kernels, local(): pl.pallas_call(second_kernel, out_shape=(rows_of(2 * CELLS), rows_of(2 *...  4.74 us
    pallas_call x1, Pallas kernels, local(): pl.pallas_call(first_kernel, out_shape=rows_of(STATE + 3 * NB), in_specs=...  4.14 us
    ppermute x1, starting transfers between devices, local(): beyond = lax.ppermute(jnp.concatenate([r0, r3], axis=0), 'depth', facing)  3.77 us
    ppermute x1, waiting for transfers between devices, local(): lax.ppermute(jnp.concatenate([q0, q3[HEAD:MORE]], axis=0), 'depth', facing)  3.73 us
    ppermute x1, starting transfers between devices, local(): lax.ppermute(jnp.concatenate([q0, q3[HEAD:MORE]], axis=0), 'depth', facing)  2.88 us
  transfers between devices with their start and end apart: 8, of which 8 were waited for; matrix products, arithmetic and copies ran while one was open for 1% of the time, Pallas kernels for 0%

profile of v2, /device:TPU:1, one launch (start us, length us, event | category | flops | bytes accessed | tf_op | source)
XLA Modules:
  0.0 68.5 jit_solution(5660706645279883520)
XLA Ops:
  0.6 1.5 %pack.1 = f32[128,128]{1,0:T(8,128)} custom-call(s32[1,4]{1,0:T(1,128)} %count.1, f32[8,128]{1,0:T(8,128)} %bitcast.21, f32[8,128]{1,0:T(8,128)} %bitcast.22, f32[4,128]{1,0:T(4,128)} %bitcast.23, s32[96,128]{1,0:T(8,128)} %bitcast.20), custom_call_target="tpu_custom_call" | custom-call | tf_op jit(solution)/shard_map/pack/pallas_call | solution.py:271
  2.1 0.0 copy-start.3
  2.1 6.6 %collective-permute-start = (f32[128,128]{1,0:T(8,128)}, f32[128,128]{1,0:T(8,128)S(1)}, u32[]{:S(2)}, u32[]{:S(2)}) collective-permute-start(f32[128,128]{1,0:T(8,128)} %pack.1), channel_id=1, source_target_pairs={{0,7},{1,0},{2,1},{3,2},{4,3},{5,4},{6,5},{7,6},{8,15},{9,8},{10,9... | collective-permute-start | bytes 196616 | tf_op jit(solution)/shard_map/ppermute | solution.py:284
  8.8 1.6 %collective-permute-done = f32[128,128]{1,0:T(8,128)S(1)} collective-permute-done((f32[128,128]{1,0:T(8,128)}, f32[128,128]{1,0:T(8,128)S(1)}, u32[]{:S(2)}, u32[]{:S(2)}) %collective-permute-start) | collective-permute-done | bytes 65568 | tf_op jit(solution)/shard_map/ppermute | solution.py:284
  10.4 0.0 copy-done.3
  10.4 0.0 copy-start
  10.4 1.6 %collective-permute-start.1 = (f32[232,128]{1,0:T(8,128)S(1)}, f32[232,128]{1,0:T(8,128)S(1)}, u32[]{:S(2)}, u32[]{:S(2)}) collective-permute-start(f32[232,128]{1,0:T(8,128)S(1)} %pad_maximum_fusion.1.q0), channel_id=1, source_target_pairs={{0,8},{8,0},{16,24},{24,16},{32,40},{40,32},{48,56},{56,48},{64,72... | collective-permute-start | bytes 356360 | tf_op jit(solution)/shard_map/ppermute | solution.py:286
  12.1 1.0 %collective-permute-done.1.q3 = f32[232,128]{1,0:T(8,128)S(1)} collective-permute-done((f32[232,128]{1,0:T(8,128)S(1)}, f32[232,128]{1,0:T(8,128)S(1)}, u32[]{:S(2)}, u32[]{:S(2)}) %collective-permute-start.1) | collective-permute-done | bytes 118816 | tf_op jit(solution)/shard_map/ppermute | solution.py:286
  13.0 0.0 copy-start.2
  13.0 0.0 copy-done
  13.1 0.6 copy-done.2
  13.7 2.9 %collective-permute-start.2 = (f32[296,128]{1,0:T(8,128)S(1)}, f32[296,128]{1,0:T(8,128)S(1)}, u32[]{:S(2)}, u32[]{:S(2)}) collective-permute-start(f32[296,128]{1,0:T(8,128)S(1)} %pad_maximum_fusion), channel_id=1, source_target_pairs={{8,16},{16,8},{24,32},{32,24},{40,48},{48,40},{56,64},{64,56},{72,... | collective-permute-start | bytes 454664 | tf_op jit(solution)/shard_map/ppermute | solution.py:287
  16.6 3.7 %collective-permute-done.2.outer.before = f32[296,128]{1,0:T(8,128)S(1)} collective-permute-done((f32[296,128]{1,0:T(8,128)S(1)}, f32[296,128]{1,0:T(8,128)S(1)}, u32[]{:S(2)}, u32[]{:S(2)}) %collective-permute-start.2) | collective-permute-done | bytes 151584 | tf_op jit(solution)/shard_map/ppermute | solution.py:287
  20.3 0.0 copy-start.1
  20.3 0.0 collective-permute-start.3
  20.3 1.2 %collective-permute-done.3.q1 = f32[64,128]{1,0:T(8,128)S(1)} collective-permute-done((f32[64,128]{1,0:T(8,128)S(1)}, f32[64,128]{1,0:T(8,128)S(1)}, u32[]{:S(2)}, u32[]{:S(2)}) %collective-permute-start.3) | collective-permute-done | bytes 32800 | tf_op jit(solution)/shard_map/ppermute | solution.py:288
  21.5 0.0 copy-start.8
  21.5 0.0 copy-done.1
  21.5 0.6 copy-done.8
  22.1 4.1 %first_step.1 = f32[104,128]{1,0:T(8,128)} custom-call(s32[1]{0:T(128)} %bitcast.parity, f32[232,128]{1,0:T(8,128)} %copy-done, f32[64,128]{1,0:T(8,128)} %copy-done.8, f32[296,128]{1,0:T(8,128)} %copy-done.1, f32[232,128]{1,0:T(8,128)} %copy-done.2), custom_call_target="tpu_custom_call" | custom-call | tf_op jit(solution)/shard_map/first_step/pallas_call | solution.py:289
  26.3 0.0 collective-permute-start.4
  26.3 0.8 %slice.33 = f32[32,128]{1,0:T(8,128)S(1)} slice(f32[104,128]{1,0:T(8,128)} %first_step.1), slice={[0:32], [0:128]} | slice | bytes 32768 | tf_op jit(solution)/shard_map/slice | solution.py:299
  27.0 7.7 %collective-permute-done.4.left = f32[104,128]{1,0:T(8,128)S(1)} collective-permute-done((f32[104,128]{1,0:T(8,128)}, f32[104,128]{1,0:T(8,128)S(1)}, u32[]{:S(2)}, u32[]{:S(2)}) %collective-permute-start.4) | collective-permute-done | bytes 53280 | tf_op jit(solution)/shard_map/ppermute | solution.py:298
  34.7 0.0 copy-start.7
  34.7 0.0 copy-start.5
  34.7 0.8 %collective-permute-start.5 = (f32[64,128]{1,0:T(8,128)S(1)}, f32[64,128]{1,0:T(8,128)S(1)}, u32[]{:S(2)}, u32[]{:S(2)}) collective-permute-start(f32[64,128]{1,0:T(8,128)S(1)} %pad_maximum_fusion.3.r0), channel_id=1, source_target_pairs={{0,8},{8,0},{16,24},{24,16},{32,40},{40,32},{48,56},{56,48},{64,72... | collective-permute-start | bytes 98312 | tf_op jit(solution)/shard_map/ppermute | solution.py:300
  35.5 0.9 %collective-permute-done.5.r3 = f32[64,128]{1,0:T(8,128)S(1)} collective-permute-done((f32[64,128]{1,0:T(8,128)S(1)}, f32[64,128]{1,0:T(8,128)S(1)}, u32[]{:S(2)}, u32[]{:S(2)}) %collective-permute-start.5) | collective-permute-done | bytes 32800 | tf_op jit(solution)/shard_map/ppermute | solution.py:300
  36.4 0.0 copy-start.6
  36.4 0.0 copy-done.7
  36.4 0.0 copy-done.5
  36.4 0.6 copy-done.6
  37.0 3.8 %collective-permute-start.6 = (f32[128,128]{1,0:T(8,128)S(1)}, f32[128,128]{1,0:T(8,128)S(1)}, u32[]{:S(2)}, u32[]{:S(2)}) collective-permute-start(f32[128,128]{1,0:T(8,128)S(1)} %pad_maximum_fusion.2), channel_id=1, source_target_pairs={{8,16},{16,8},{24,32},{32,24},{40,48},{48,40},{56,64},{64,56},{72,... | collective-permute-start | bytes 196616 | tf_op jit(solution)/shard_map/ppermute | solution.py:301
  40.8 1.9 %collective-permute-done.6.outer = f32[128,128]{1,0:T(8,128)S(1)} collective-permute-done((f32[128,128]{1,0:T(8,128)S(1)}, f32[128,128]{1,0:T(8,128)S(1)}, u32[]{:S(2)}, u32[]{:S(2)}) %collective-permute-start.6) | collective-permute-done | bytes 65568 | tf_op jit(solution)/shard_map/ppermute | solution.py:301
  42.7 0.0 copy-start.4
  42.7 0.0 collective-permute-start.7
  42.7 1.2 %collective-permute-done.7.r1 = f32[64,128]{1,0:T(8,128)S(1)} collective-permute-done((f32[64,128]{1,0:T(8,128)S(1)}, f32[64,128]{1,0:T(8,128)S(1)}, u32[]{:S(2)}, u32[]{:S(2)}) %collective-permute-start.7) | collective-permute-done | bytes 32800 | tf_op jit(solution)/shard_map/ppermute | solution.py:302
  43.9 0.0 copy-start.9
  43.9 0.0 copy-done.4
  44.0 0.6 copy-done.9
  44.6 4.7 %second_step.1 = (f32[8,128]{1,0:T(8,128)}, f32[8,128]{1,0:T(8,128)}, f32[4,128]{1,0:T(4,128)}, f32[128,128]{1,0:T(8,128)}) custom-call(s32[1]{0:T(128)} %bitcast.parity, s32[4,128]{1,0:T(4,128)} %bitcast.24, s32[4,128]{1,0:T(4,128)} %bitcast.25, f32[104,128]{1,0:T(8,128)} %copy-done.7, f32[64,128]{1,0:T(8,128)} %copy-done.5, f32[64,128]{1,0:T(8,128)} %copy-done.9, ...), custom_call_target="tpu_custom_call" | custom-call | tf_op jit(solution)/shard_map/second_step/pallas_call | solution.py:303
  49.3 17.6 %all_to_all.11 = f32[128,1,128]{2,1,0:T(1,128)} all-to-all(f32[128,1,128]{2,1,0:T(1,128)} %bitcast.19), channel_id=1, replica_groups=mesh['depth'=16,'azim'=8] {'depth','azim'}, dimensions={0} | all-to-all | bytes 131072 | tf_op jit(solution)/shard_map/all_to_all | solution.py:312
  66.9 1.6 %soil.1 = f32[4,16,128]{2,1,0:T(8,128)} custom-call(f32[128,128]{1,0:T(8,128)} %bitcast.18, f32[4,16,128]{2,1,0:T(8,128)} %stress.1, f32[3,16,128]{2,1,0:T(8,128)} %rate.1, f32[3,16,128]{2,1,0:T(8,128)} %couple.1), custom_call_target="tpu_custom_call" | custom-call | tf_op jit(solution)/shard_map/soil/pallas_call | solution.py:313
  (10 shorter events, 0.1 us)
Async XLA Ops:
  2.1 8.3 %copy-start.3 = (f32[128,128]{1,0:T(8,128)S(1)}, f32[128,128]{1,0:T(8,128)}, u32[]{:S(2)}) copy-start(f32[128,128]{1,0:T(8,128)} %pack.1) | copy-start | bytes 196612
  2.1 8.3 %collective-permute-start = (f32[128,128]{1,0:T(8,128)}, f32[128,128]{1,0:T(8,128)S(1)}, u32[]{:S(2)}, u32[]{:S(2)}) collective-permute-start(f32[128,128]{1,0:T(8,128)} %pack.1), channel_id=1, source_target_pairs={{0,7},{1,0},{2,1},{3,2},{4,3},{5,4},{6,5},{7,6},{8,15},{9,8},{10,9... | collective-permute-start | bytes 196616 | tf_op jit(solution)/shard_map/ppermute | solution.py:284
  10.4 2.6 %copy-start = (f32[232,128]{1,0:T(8,128)}, f32[232,128]{1,0:T(8,128)S(1)}, u32[]{:S(2)}) copy-start(f32[232,128]{1,0:T(8,128)S(1)} %pad_maximum_fusion.1.q0) | copy-start | bytes 356356
  10.4 2.6 %collective-permute-start.1 = (f32[232,128]{1,0:T(8,128)S(1)}, f32[232,128]{1,0:T(8,128)S(1)}, u32[]{:S(2)}, u32[]{:S(2)}) collective-permute-start(f32[232,128]{1,0:T(8,128)S(1)} %pad_maximum_fusion.1.q0), channel_id=1, source_target_pairs={{0,8},{8,0},{16,24},{24,16},{32,40},{40,32},{48,56},{56,48},{64,72... | collective-permute-start | bytes 356360 | tf_op jit(solution)/shard_map/ppermute | solution.py:286
  13.0 0.6 copy-start.2
  13.7 6.6 %collective-permute-start.2 = (f32[296,128]{1,0:T(8,128)S(1)}, f32[296,128]{1,0:T(8,128)S(1)}, u32[]{:S(2)}, u32[]{:S(2)}) collective-permute-start(f32[296,128]{1,0:T(8,128)S(1)} %pad_maximum_fusion), channel_id=1, source_target_pairs={{8,16},{16,8},{24,32},{32,24},{40,48},{48,40},{56,64},{64,56},{72,... | collective-permute-start | bytes 454664 | tf_op jit(solution)/shard_map/ppermute | solution.py:287
  20.3 1.2 %copy-start.1 = (f32[296,128]{1,0:T(8,128)}, f32[296,128]{1,0:T(8,128)S(1)}, u32[]{:S(2)}) copy-start(f32[296,128]{1,0:T(8,128)S(1)} %collective-permute-done.2.outer.before) | copy-start | bytes 454660
  20.3 1.2 %collective-permute-start.3 = (f32[64,128]{1,0:T(8,128)S(1)}, f32[64,128]{1,0:T(8,128)S(1)}, u32[]{:S(2)}, u32[]{:S(2)}) collective-permute-start(f32[64,128]{1,0:T(8,128)S(1)} %slice.31), channel_id=1, source_target_pairs={{0,8},{8,0},{16,24},{24,16},{32,40},{40,32},{48,56},{56,48},{64,72... | collective-permute-start | bytes 98312 | tf_op jit(solution)/shard_map/ppermute | solution.py:288
  21.5 0.6 copy-start.8
  26.3 8.4 %collective-permute-start.4 = (f32[104,128]{1,0:T(8,128)}, f32[104,128]{1,0:T(8,128)S(1)}, u32[]{:S(2)}, u32[]{:S(2)}) collective-permute-start(f32[104,128]{1,0:T(8,128)} %first_step.1), channel_id=1, source_target_pairs={{0,1},{1,2},{2,3},{3,4},{4,5},{5,6},{6,7},{7,0},{8,9},{9,10},{10,1... | collective-permute-start | bytes 159752 | tf_op jit(solution)/shard_map/ppermute | solution.py:298
  34.7 1.7 %copy-start.7 = (f32[104,128]{1,0:T(8,128)}, f32[104,128]{1,0:T(8,128)S(1)}, u32[]{:S(2)}) copy-start(f32[104,128]{1,0:T(8,128)S(1)} %collective-permute-done.4.left) | copy-start | bytes 159748
  34.7 1.7 %copy-start.5 = (f32[64,128]{1,0:T(8,128)}, f32[64,128]{1,0:T(8,128)S(1)}, u32[]{:S(2)}) copy-start(f32[64,128]{1,0:T(8,128)S(1)} %pad_maximum_fusion.3.r0) | copy-start | bytes 98308
  34.7 1.7 %collective-permute-start.5 = (f32[64,128]{1,0:T(8,128)S(1)}, f32[64,128]{1,0:T(8,128)S(1)}, u32[]{:S(2)}, u32[]{:S(2)}) collective-permute-start(f32[64,128]{1,0:T(8,128)S(1)} %pad_maximum_fusion.3.r0), channel_id=1, source_target_pairs={{0,8},{8,0},{16,24},{24,16},{32,40},{40,32},{48,56},{56,48},{64,72... | collective-permute-start | bytes 98312 | tf_op jit(solution)/shard_map/ppermute | solution.py:300
  36.4 0.6 copy-start.6
  37.0 5.7 %collective-permute-start.6 = (f32[128,128]{1,0:T(8,128)S(1)}, f32[128,128]{1,0:T(8,128)S(1)}, u32[]{:S(2)}, u32[]{:S(2)}) collective-permute-start(f32[128,128]{1,0:T(8,128)S(1)} %pad_maximum_fusion.2), channel_id=1, source_target_pairs={{8,16},{16,8},{24,32},{32,24},{40,48},{48,40},{56,64},{64,56},{72,... | collective-permute-start | bytes 196616 | tf_op jit(solution)/shard_map/ppermute | solution.py:301
  42.7 1.2 %copy-start.4 = (f32[128,128]{1,0:T(8,128)}, f32[128,128]{1,0:T(8,128)S(1)}, u32[]{:S(2)}) copy-start(f32[128,128]{1,0:T(8,128)S(1)} %collective-permute-done.6.outer) | copy-start | bytes 196612
  42.7 1.2 %collective-permute-start.7 = (f32[64,128]{1,0:T(8,128)S(1)}, f32[64,128]{1,0:T(8,128)S(1)}, u32[]{:S(2)}, u32[]{:S(2)}) collective-permute-start(f32[64,128]{1,0:T(8,128)S(1)} %slice.34), channel_id=1, source_target_pairs={{0,8},{8,0},{16,24},{24,16},{32,40},{40,32},{48,56},{56,48},{64,72... | collective-permute-start | bytes 98312 | tf_op jit(solution)/shard_map/ppermute | solution.py:302
  43.9 0.6 copy-start.9

commit v3 on v2

--- a/solution.py
+++ b/solution.py
@@ -237,6 +237,10 @@
     return jax.ShapeDtypeStruct((n, S), jnp.float32)
 
 
+def kept(n):
+    return pltpu.VMEM((n, S), jnp.float32)
+
+
 VM = pl.BlockSpec(memory_space=pltpu.MemorySpace.VMEM)
 SM = pl.BlockSpec(memory_space=pltpu.MemorySpace.SMEM)
 WORK = [
@@ -245,6 +249,10 @@
     pltpu.VMEM((3 * RING * NT * 40, S), jnp.float32),
     pltpu.VMEM((3 * RING * 8, S), jnp.float32),
 ]
+
+
+def held(a):
+    return pltpu.with_memory_space_constraint(a, pltpu.MemorySpace.VMEM)
 
 
 def local(
@@ -270,7 +278,7 @@
 
     own = pl.pallas_call(
         pack_kernel,
-        out_shape=rows_of(LISTS + STATE),
+        out_shape=kept(LISTS + STATE),
         in_specs=[SM, VM, VM, VM, VM],
         out_specs=VM,
         name="pack",
@@ -288,12 +296,12 @@
     q1 = lax.ppermute(outer[HEAD:MORE], "depth", pairs)
     mid = pl.pallas_call(
         first_kernel,
-        out_shape=rows_of(STATE + 3 * NB),
+        out_shape=kept(STATE + 3 * NB),
         in_specs=[SM] + [VM] * 4,
         out_specs=VM,
         scratch_shapes=WORK,
         name="first_step",
-    )(parity, q0, q1, outer, q3)
+    )(parity, *[held(a) for a in (q0, q1, outer, q3)])
 
     left = lax.ppermute(mid, "azim", toward_right)
     r0 = jnp.concatenate([left[:STATE], mid[:STATE]], axis=0)
@@ -302,12 +310,12 @@
     r1 = lax.ppermute(beyond[: 2 * STATE], "depth", pairs)
     pos, vel, rho, part = pl.pallas_call(
         second_kernel,
-        out_shape=(rows_of(2 * CELLS), rows_of(2 * CELLS), rows_of(CELLS), rows_of(S)),
+        out_shape=(kept(2 * CELLS), kept(2 * CELLS), kept(CELLS), kept(S)),
         in_specs=[SM] + [VM] * 10,
         out_specs=(VM, VM, VM, VM),
         scratch_shapes=WORK,
         name="second_step",
-    )(parity, iface_dest.reshape(CELLS, S), iface_shell.reshape(CELLS, S), left, r0, r1, beyond, r3, q0, outer, q3)
+    )(parity, *[held(a) for a in (iface_dest.reshape(CELLS, S), iface_shell.reshape(CELLS, S), left, r0, r1, beyond, r3, q0, outer, q3)])
 
     arrived = lax.all_to_all(part, ("depth", "azim"), split_axis=0, concat_axis=0, tiled=True)
     stress_out = pl.pallas_call(
@@ -316,7 +324,7 @@
         in_specs=[VM] * 4,
         out_specs=VM,
         name="soil",
-    )(arrived, soil_stress, soil_rate, soil_couple)
+    )(held(arrived), held(soil_stress), held(soil_rate), held(soil_couple))
     return (
         pos.reshape(fluid_pos.shape),
         vel.reshape(fluid_vel.shape),

time: 68.9 us -> 61.4 us (0.89)
  blocking collectives: 17.6 us -> 0 us
  waiting for transfers between devices: 19.2 us -> 27.6 us
  starting transfers between devices: 15.7 us -> 23.3 us
  Pallas kernels: 12 us -> 7.66 us
  local copies, waits for them, and re-layouts: 3.21 us -> 1.81 us
    all_to_all x1 -> x0, blocking collectives: 17.6 us -> none  [local(): lax.all_to_all(part, ('depth', 'azim'), split_axis=0, concat_axis=0, tile...]
    all_to_all x0 -> x1, waiting for transfers between devices: none -> 8.03 us  [local(): lax.all_to_all(part, ('depth', 'azim'), split_axis=0, concat_axis=0, tile...]
    all_to_all x0 -> x1, starting transfers between devices: none -> 7.46 us  [local(): lax.all_to_all(part, ('depth', 'azim'), split_axis=0, concat_axis=0, tile...]
    pallas_call x3, Pallas kernels: 10.4 us -> 6.91 us  [the longest x1 3.56 us: local(): pl.pallas_call(second_kernel, out_shape=(kept(2 * CELLS), kept(2 * CELLS)...]
    pallas_call x1, Pallas kernels: 1.62 us -> 0.76 us  [local(): pl.pallas_call(soil_kernel, out_shape=jax.ShapeDtypeStruct(soil_stress.sh...]
    slice x2, local copies, waits for them, and re-layouts: 0.75 us -> 0.01 us  [local(): r0 = jnp.concatenate([left[:STATE], mid[:STATE]], axis=0)]
    unnamed x20 -> x13, local copies, waits for them, and re-layouts: 2.44 us -> 1.79 us
  transfers between devices with their start and end apart: 8 -> 9, of which waited for: 8 -> 9; matrix products, arithmetic and copies ran while one was open for 1% -> 3% of each run, Pallas kernels for 0% -> 0%
where the time goes in v3:
time: 61.4 us; the launch traced here: 61.1 us
  waiting for transfers between devices  27.6 us (45%)
  starting transfers between devices  23.3 us (38%)
  Pallas kernels  7.66 us (12%)
  local copies, waits for them, and re-layouts  1.81 us (3%)
  between operations  0.73 us (1%)
    ppermute x1, waiting for transfers between devices, local(): left = lax.ppermute(mid, 'azim', toward_right)  8.32 us
    all_to_all x1, waiting for transfers between devices, local(): lax.all_to_all(part, ('depth', 'azim'), split_axis=0, concat_axis=0, tile...  8.03 us
    all_to_all x1, starting transfers between devices, local(): lax.all_to_all(part, ('depth', 'azim'), split_axis=0, concat_axis=0, tile...  7.46 us
    ppermute x1, starting transfers between devices, local(): right = lax.ppermute(own, 'azim', toward_left)  6.69 us
    ppermute x1, starting transfers between devices, local(): beyond = lax.ppermute(jnp.concatenate([r0, r3], axis=0), 'depth', facing)  3.77 us
    ppermute x1, waiting for transfers between devices, local(): lax.ppermute(jnp.concatenate([q0, q3[HEAD:MORE]], axis=0), 'depth', facing)  3.73 us
    pallas_call x1, Pallas kernels, local(): pl.pallas_call(second_kernel, out_shape=(kept(2 * CELLS), kept(2 * CELLS)...  3.56 us
    ppermute x1, starting transfers between devices, local(): lax.ppermute(jnp.concatenate([q0, q3[HEAD:MORE]], axis=0), 'depth', facing)  2.89 us
  transfers between devices with their start and end apart: 9, of which 9 were waited for; matrix products, arithmetic and copies ran while one was open for 3% of the time, Pallas kernels for 0%

profile of v3, /device:TPU:1, one launch (start us, length us, event | category | flops | bytes accessed | tf_op | source)
XLA Modules:
  0.0 61.1 jit_solution(2182745830804696505)
XLA Ops:
  0.6 0.9 %pack.1 = f32[128,128]{1,0:T(8,128)S(1)} custom-call(s32[1,4]{1,0:T(1,128)} %count.1, f32[8,128]{1,0:T(8,128)} %bitcast.25, f32[8,128]{1,0:T(8,128)} %bitcast.26, f32[4,128]{1,0:T(4,128)} %bitcast.27, s32[96,128]{1,0:T(8,128)} %bitcast.24), custom_call_target="tpu_custom_call" | custom-call | tf_op jit(solution)/shard_map/pack/pallas_call | solution.py:279
  1.5 6.7 %collective-permute-start = (f32[128,128]{1,0:T(8,128)S(1)}, f32[128,128]{1,0:T(8,128)S(1)}, u32[]{:S(2)}, u32[]{:S(2)}) collective-permute-start(f32[128,128]{1,0:T(8,128)S(1)} %pack.1), channel_id=1, source_target_pairs={{0,7},{1,0},{2,1},{3,2},{4,3},{5,4},{6,5},{7,6},{8,15},{9,8},{10,9... | collective-permute-start | bytes 196616 | tf_op jit(solution)/shard_map/ppermute | solution.py:292
  8.2 1.3 %collective-permute-done = f32[128,128]{1,0:T(8,128)S(1)} collective-permute-done((f32[128,128]{1,0:T(8,128)S(1)}, f32[128,128]{1,0:T(8,128)S(1)}, u32[]{:S(2)}, u32[]{:S(2)}) %collective-permute-start) | collective-permute-done | bytes 65568 | tf_op jit(solution)/shard_map/ppermute | solution.py:292
  9.6 1.6 %collective-permute-start.1 = (f32[232,128]{1,0:T(8,128)S(1)}, f32[232,128]{1,0:T(8,128)S(1)}, u32[]{:S(2)}, u32[]{:S(2)}) collective-permute-start(f32[232,128]{1,0:T(8,128)S(1)} %pad_maximum_fusion.1.q0), channel_id=1, source_target_pairs={{0,8},{8,0},{16,24},{24,16},{32,40},{40,32},{48,56},{56,48},{64,72... | collective-permute-start | bytes 356360 | tf_op jit(solution)/shard_map/ppermute | solution.py:294
  11.2 1.0 %collective-permute-done.1.q3 = f32[232,128]{1,0:T(8,128)S(1)} collective-permute-done((f32[232,128]{1,0:T(8,128)S(1)}, f32[232,128]{1,0:T(8,128)S(1)}, u32[]{:S(2)}, u32[]{:S(2)}) %collective-permute-start.1) | collective-permute-done | bytes 118816 | tf_op jit(solution)/shard_map/ppermute | solution.py:294
  12.2 2.9 %collective-permute-start.2 = (f32[296,128]{1,0:T(8,128)S(1)}, f32[296,128]{1,0:T(8,128)S(1)}, u32[]{:S(2)}, u32[]{:S(2)}) collective-permute-start(f32[296,128]{1,0:T(8,128)S(1)} %pad_maximum_fusion), channel_id=1, source_target_pairs={{8,16},{16,8},{24,32},{32,24},{40,48},{48,40},{56,64},{64,56},{72,... | collective-permute-start | bytes 454664 | tf_op jit(solution)/shard_map/ppermute | solution.py:295
  15.1 3.7 %collective-permute-done.2.outer.before = f32[296,128]{1,0:T(8,128)S(1)} collective-permute-done((f32[296,128]{1,0:T(8,128)S(1)}, f32[296,128]{1,0:T(8,128)S(1)}, u32[]{:S(2)}, u32[]{:S(2)}) %collective-permute-start.2) | collective-permute-done | bytes 151584 | tf_op jit(solution)/shard_map/ppermute | solution.py:295
  18.8 0.0 collective-permute-start.3
  18.8 1.2 %collective-permute-done.3.q1 = f32[64,128]{1,0:T(8,128)S(1)} collective-permute-done((f32[64,128]{1,0:T(8,128)S(1)}, f32[64,128]{1,0:T(8,128)S(1)}, u32[]{:S(2)}, u32[]{:S(2)}) %collective-permute-start.3) | collective-permute-done | bytes 32800 | tf_op jit(solution)/shard_map/ppermute | solution.py:296
  20.0 2.5 %first_step.1 = f32[104,128]{1,0:T(8,128)S(1)} custom-call(s32[1]{0:T(128)} %bitcast.parity, f32[232,128]{1,0:T(8,128)S(1)} %pad_maximum_fusion.1.q0, f32[64,128]{1,0:T(8,128)S(1)} %collective-permute-done.3.q1, f32[296,128]{1,0:T(8,128)S(1)} %collective-permute-done.2.outer.before, f32[232,128]{1,0:T(8,128)S(1)} %collective-permute-done.1.q3), custom_call_target="tpu_custom_call" | custom-call | tf_op jit(solution)/shard_map/first_step/pallas_call | solution.py:297
  22.5 0.1 collective-permute-start.4
  22.6 8.3 %collective-permute-done.4.left = f32[104,128]{1,0:T(8,128)S(1)} collective-permute-done((f32[104,128]{1,0:T(8,128)S(1)}, f32[104,128]{1,0:T(8,128)S(1)}, u32[]{:S(2)}, u32[]{:S(2)}) %collective-permute-start.4) | collective-permute-done | bytes 53280 | tf_op jit(solution)/shard_map/ppermute | solution.py:306
  30.9 0.7 %collective-permute-start.5 = (f32[64,128]{1,0:T(8,128)S(1)}, f32[64,128]{1,0:T(8,128)S(1)}, u32[]{:S(2)}, u32[]{:S(2)}) collective-permute-start(f32[64,128]{1,0:T(8,128)S(1)} %pad_maximum_fusion.3.r0), channel_id=1, source_target_pairs={{0,8},{8,0},{16,24},{24,16},{32,40},{40,32},{48,56},{56,48},{64,72... | collective-permute-start | bytes 98312 | tf_op jit(solution)/shard_map/ppermute | solution.py:308
  31.6 0.9 %collective-permute-done.5.r3 = f32[64,128]{1,0:T(8,128)S(1)} collective-permute-done((f32[64,128]{1,0:T(8,128)S(1)}, f32[64,128]{1,0:T(8,128)S(1)}, u32[]{:S(2)}, u32[]{:S(2)}) %collective-permute-start.5) | collective-permute-done | bytes 32800 | tf_op jit(solution)/shard_map/ppermute | solution.py:308
  32.5 3.8 %collective-permute-start.6 = (f32[128,128]{1,0:T(8,128)S(1)}, f32[128,128]{1,0:T(8,128)S(1)}, u32[]{:S(2)}, u32[]{:S(2)}) collective-permute-start(f32[128,128]{1,0:T(8,128)S(1)} %pad_maximum_fusion.2), channel_id=1, source_target_pairs={{8,16},{16,8},{24,32},{32,24},{40,48},{48,40},{56,64},{64,56},{72,... | collective-permute-start | bytes 196616 | tf_op jit(solution)/shard_map/ppermute | solution.py:309
  36.3 1.9 %collective-permute-done.6.outer = f32[128,128]{1,0:T(8,128)S(1)} collective-permute-done((f32[128,128]{1,0:T(8,128)S(1)}, f32[128,128]{1,0:T(8,128)S(1)}, u32[]{:S(2)}, u32[]{:S(2)}) %collective-permute-start.6) | collective-permute-done | bytes 65568 | tf_op jit(solution)/shard_map/ppermute | solution.py:309
  38.2 0.0 copy-start.4
  38.2 0.0 copy-start.3
  38.2 0.1 collective-permute-start.7
  38.3 1.2 %collective-permute-done.7.r1 = f32[64,128]{1,0:T(8,128)S(1)} collective-permute-done((f32[64,128]{1,0:T(8,128)S(1)}, f32[64,128]{1,0:T(8,128)S(1)}, u32[]{:S(2)}, u32[]{:S(2)}) %collective-permute-start.7) | collective-permute-done | bytes 32800 | tf_op jit(solution)/shard_map/ppermute | solution.py:310
  39.5 0.0 copy-done.4
  39.5 0.0 copy-done.3
  39.5 3.6 %second_step.1 = (f32[8,128]{1,0:T(8,128)S(1)}, f32[8,128]{1,0:T(8,128)S(1)}, f32[4,128]{1,0:T(4,128)S(1)}, f32[128,128]{1,0:T(8,128)}) custom-call(s32[1]{0:T(128)} %bitcast.parity, s32[4,128]{1,0:T(4,128)S(1)} %bitcast.22, s32[4,128]{1,0:T(4,128)S(1)} %bitcast.23, f32[104,128]{1,0:T(8,128)S(1)} %collective-permute-done.4.left, ...), custom_call_target="tpu_custom_call" | custom-call | tf_op jit(solution)/shard_map/second_step/pallas_call | solution.py:311
  43.1 0.0 copy-start.1
  43.1 0.0 copy-start.2
  43.1 7.5 %all-to-all-start = ((f32[128,1,128]{2,1,0:T(1,128)}), f32[128,1,128]{2,1,0:T(1,128)S(1)}, u32[]{:S(2)}, u32[]{:S(2)}) async-start(f32[128,1,128]{2,1,0:T(1,128)} %bitcast.13), calls=%async_computation | async-start | bytes 131072 | tf_op jit(solution)/shard_map/all_to_all | solution.py:320
  50.6 0.0 copy-start
  50.6 0.6 copy.19
  51.2 0.6 copy.20
  51.8 0.6 copy.21
  52.3 8.0 %all-to-all-done = f32[128,1,128]{2,1,0:T(1,128)S(1)} async-done(((f32[128,1,128]{2,1,0:T(1,128)}), f32[128,1,128]{2,1,0:T(1,128)S(1)}, u32[]{:S(2)}, u32[]{:S(2)}) %all-to-all-start) | async-done | bytes 65568 | tf_op jit(solution)/shard_map/all_to_all | solution.py:320
  60.4 0.0 copy-done.1
  60.4 0.0 copy-done.2
  60.4 0.0 copy-done
  60.4 0.8 %soil.1 = f32[4,16,128]{2,1,0:T(8,128)} custom-call(f32[128,128]{1,0:T(8,128)S(1)} %bitcast.21, f32[4,16,128]{2,1,0:T(8,128)S(1)} %copy-done, f32[3,16,128]{2,1,0:T(8,128)S(1)} %copy-done.1, f32[3,16,128]{2,1,0:T(8,128)S(1)} %copy-done.2), custom_call_target="tpu_custom_call" | custom-call | tf_op jit(solution)/shard_map/soil/pallas_call | solution.py:321
  (11 shorter events, 0.1 us)
Async XLA Ops:
  1.5 8.0 %collective-permute-start = (f32[128,128]{1,0:T(8,128)S(1)}, f32[128,128]{1,0:T(8,128)S(1)}, u32[]{:S(2)}, u32[]{:S(2)}) collective-permute-start(f32[128,128]{1,0:T(8,128)S(1)} %pack.1), channel_id=1, source_target_pairs={{0,7},{1,0},{2,1},{3,2},{4,3},{5,4},{6,5},{7,6},{8,15},{9,8},{10,9... | collective-permute-start | bytes 196616 | tf_op jit(solution)/shard_map/ppermute | solution.py:292
  9.6 2.6 %collective-permute-start.1 = (f32[232,128]{1,0:T(8,128)S(1)}, f32[232,128]{1,0:T(8,128)S(1)}, u32[]{:S(2)}, u32[]{:S(2)}) collective-permute-start(f32[232,128]{1,0:T(8,128)S(1)} %pad_maximum_fusion.1.q0), channel_id=1, source_target_pairs={{0,8},{8,0},{16,24},{24,16},{32,40},{40,32},{48,56},{56,48},{64,72... | collective-permute-start | bytes 356360 | tf_op jit(solution)/shard_map/ppermute | solution.py:294
  12.2 6.6 %collective-permute-start.2 = (f32[296,128]{1,0:T(8,128)S(1)}, f32[296,128]{1,0:T(8,128)S(1)}, u32[]{:S(2)}, u32[]{:S(2)}) collective-permute-start(f32[296,128]{1,0:T(8,128)S(1)} %pad_maximum_fusion), channel_id=1, source_target_pairs={{8,16},{16,8},{24,32},{32,24},{40,48},{48,40},{56,64},{64,56},{72,... | collective-permute-start | bytes 454664 | tf_op jit(solution)/shard_map/ppermute | solution.py:295
  18.8 1.2 %collective-permute-start.3 = (f32[64,128]{1,0:T(8,128)S(1)}, f32[64,128]{1,0:T(8,128)S(1)}, u32[]{:S(2)}, u32[]{:S(2)}) collective-permute-start(f32[64,128]{1,0:T(8,128)S(1)} %slice.31), channel_id=1, source_target_pairs={{0,8},{8,0},{16,24},{24,16},{32,40},{40,32},{48,56},{56,48},{64,72... | collective-permute-start | bytes 98312 | tf_op jit(solution)/shard_map/ppermute | solution.py:296
  22.5 8.4 %collective-permute-start.4 = (f32[104,128]{1,0:T(8,128)S(1)}, f32[104,128]{1,0:T(8,128)S(1)}, u32[]{:S(2)}, u32[]{:S(2)}) collective-permute-start(f32[104,128]{1,0:T(8,128)S(1)} %first_step.1), channel_id=1, source_target_pairs={{0,1},{1,2},{2,3},{3,4},{4,5},{5,6},{6,7},{7,0},{8,9},{9,10},{10,1... | collective-permute-start | bytes 159752 | tf_op jit(solution)/shard_map/ppermute | solution.py:306
  30.9 1.6 %collective-permute-start.5 = (f32[64,128]{1,0:T(8,128)S(1)}, f32[64,128]{1,0:T(8,128)S(1)}, u32[]{:S(2)}, u32[]{:S(2)}) collective-permute-start(f32[64,128]{1,0:T(8,128)S(1)} %pad_maximum_fusion.3.r0), channel_id=1, source_target_pairs={{0,8},{8,0},{16,24},{24,16},{32,40},{40,32},{48,56},{56,48},{64,72... | collective-permute-start | bytes 98312 | tf_op jit(solution)/shard_map/ppermute | solution.py:308
  32.5 5.7 %collective-permute-start.6 = (f32[128,128]{1,0:T(8,128)S(1)}, f32[128,128]{1,0:T(8,128)S(1)}, u32[]{:S(2)}, u32[]{:S(2)}) collective-permute-start(f32[128,128]{1,0:T(8,128)S(1)} %pad_maximum_fusion.2), channel_id=1, source_target_pairs={{8,16},{16,8},{24,32},{32,24},{40,48},{48,40},{56,64},{64,56},{72,... | collective-permute-start | bytes 196616 | tf_op jit(solution)/shard_map/ppermute | solution.py:309
  38.2 1.3 %copy-start.4 = (s32[1,512]{1,0:T(1,128)S(1)}, s32[1,512]{1,0:T(1,128)}, u32[]{:S(2)}) copy-start(s32[1,512]{1,0:T(1,128)} %param.16) | copy-start | bytes 6148
  38.2 1.3 %copy-start.3 = (s32[1,512,1]{1,2,0:T(1,128)S(1)}, s32[1,512,1]{1,2,0:T(1,128)}, u32[]{:S(2)}) copy-start(s32[1,512,1]{1,2,0:T(1,128)} %param.15) | copy-start | bytes 6148
  38.2 1.3 %collective-permute-start.7 = (f32[64,128]{1,0:T(8,128)S(1)}, f32[64,128]{1,0:T(8,128)S(1)}, u32[]{:S(2)}, u32[]{:S(2)}) collective-permute-start(f32[64,128]{1,0:T(8,128)S(1)} %slice.34), channel_id=1, source_target_pairs={{0,8},{8,0},{16,24},{24,16},{32,40},{40,32},{48,56},{56,48},{64,72... | collective-permute-start | bytes 98312 | tf_op jit(solution)/shard_map/ppermute | solution.py:310
  43.1 17.3 %copy-start.1 = (f32[3,16,128]{2,1,0:T(8,128)S(1)}, f32[3,16,128]{2,1,0:T(8,128)}, u32[]{:S(2)}) copy-start(f32[3,16,128]{2,1,0:T(8,128)} %rate.1) | copy-start | bytes 73732
  43.1 17.3 %copy-start.2 = (f32[3,16,128]{2,1,0:T(8,128)S(1)}, f32[3,16,128]{2,1,0:T(8,128)}, u32[]{:S(2)}) copy-start(f32[3,16,128]{2,1,0:T(8,128)} %couple.1) | copy-start | bytes 73732
  43.1 17.3 %all-to-all-start = ((f32[128,1,128]{2,1,0:T(1,128)}), f32[128,1,128]{2,1,0:T(1,128)S(1)}, u32[]{:S(2)}, u32[]{:S(2)}) async-start(f32[128,1,128]{2,1,0:T(1,128)} %bitcast.13), calls=%async_computation | async-start | bytes 131072 | tf_op jit(solution)/shard_map/all_to_all | solution.py:320
  50.6 9.8 %copy-start = (f32[4,16,128]{2,1,0:T(8,128)S(1)}, f32[4,16,128]{2,1,0:T(8,128)}, u32[]{:S(2)}) copy-start(f32[4,16,128]{2,1,0:T(8,128)} %stress.1) | copy-start | bytes 98308

commit v4 on v3

v4 whole, which is shorter than its diff:
```python
import jax
import jax.numpy as jnp
from jax import lax
from jax.experimental import pallas as pl
from jax.experimental.pallas import tpu as pltpu
from jax.sharding import PartitionSpec as P

step_dt = 0.05
sound_sq = 1.0
visc_alpha = 0.5
soil_dt = 0.1
shear_mod = 1.0
bulk_mod = 2.0
cohesion = 1.0
friction = 0.3

CELLS = 4
NB = 24
NT = 3
WIDE = 8
RING = 6
S = 128
LISTS = NB * CELLS
PX, PY, PM, PVX, PVY, PL = range(6)
HALF = 6 * CELLS
SENT = 5 * WIDE
PLACE = 3 * WIDE
PAIR = 40
NEAR = [(dr, dc) for dr in (-1, 0, 1) for dc in (-1, 0, 1)]


def pack_kernel(count, pos, vel, mass, nb, out, last):
    lane = lax.broadcasted_iota(jnp.int32, (1, S), 1)
    out[0 : 2 * CELLS, :] = pos[...]
    out[PVX * CELLS : (PVX + 2) * CELLS, :] = vel[...]
    for c in range(CELLS):
        live = (lane < count[0, c]).astype(jnp.float32)
        out[PM * CELLS + c : PM * CELLS + c + 1, :] = mass[c : c + 1, :] * live
        out[PL * CELLS + c : PL * CELLS + c + 1, :] = live
        codes = nb[pl.ds(c, NB, stride=CELLS), :].astype(jnp.float32)
        if c < CELLS - 1:
            out[HALF + NB * c : HALF + NB * (c + 1), :] = codes
        else:
            last[...] = codes


def spread(row):
    return jnp.broadcast_to(row, (8, S))


def pick(tables, slot, masks):
    out = None
    for table, mask in zip(tables, masks):
        got = jnp.take_along_axis(table, slot, axis=1)
        out = got if out is None else jnp.where(mask, got, out)
    return out


def numbers_of(parity):
    sign = 1 - 2 * parity[0]
    return [3 * (1 + sign * dr) + dc + 1 for dr, dc in NEAR]


def decode(ref, start, numbers):
    code = ref[start : start + 8, :].astype(jnp.int32)
    which = code >> 7
    return code & (S - 1), which, [which == n for n in numbers]


def density(parity, rows, lists, rho_out, pair):
    numbers = numbers_of(parity)
    rho_out[...] = jnp.zeros((WIDE, S), jnp.float32)
    for k in range(RING):
        col = k + 1
        ref, start = rows[0]
        own_x, own_y = spread(ref[start + col : start + col + 1, :]), spread(ref[start + WIDE + col : start + WIDE + col + 1, :])
        own_m = ref[start + PM * WIDE + col : start + PM * WIDE + col + 1, :]

        def table(f):
            out = []
            for dr, dc in NEAR:
                r, base = rows[dr]
                at = base + f * WIDE + col + dc
                out.append(spread(r[at : at + 1, :]))
            return out

        xs, ys, ms = table(PX), table(PY), table(PM)
        total = jnp.zeros((8, S), jnp.float32)
        ref, start = lists[k]
        for t in range(NT):
            slot, which, masks = decode(ref, start + 8 * t, numbers)
            third = (which * 11) >> 5
            dx = own_x - ((third - 1).astype(jnp.float32) + pick(xs, slot, masks))
            dy = own_y - ((which - 3 * third - 1).astype(jnp.float32) + pick(ys, slot, masks))
            mass = pick(ms, slot, masks)
            dist = jnp.sqrt(dx * dx + dy * dy)
            tail = jnp.maximum(1.0 - dist, 0.0)
            cube = tail * tail * tail
            total = total + mass * (cube * tail * (4.0 * dist + 1.0))
            if pair is not None and 1 <= k <= CELLS:
                base = ((k - 1) * NT + t) * PAIR
                pair[base : base + 8, :] = dx
                pair[base + 8 : base + 16, :] = dy
                pair[base + 16 : base + 24, :] = mass
                pair[base + 24 : base + 32, :] = dist * dist + 0.01
                pair[base + 32 : base + 40, :] = 20.0 * cube
        rho = own_m + jnp.sum(total, axis=0, keepdims=True) + jnp.where(own_m > 0.0, 0.0, 1.0)
        rho_out[col : col + 1, :] = rho


def term(rho):
    return sound_sq * (rho - 1.0) / (rho * rho)


def force(c, numbers, frame, states, rhos, lists, pair):
    col = c + 2
    ref, start = lists

    def own(f):
        return frame[f * WIDE + col : f * WIDE + col + 1, :]

    def table(refs, f):
        return [spread(refs[dr][f * WIDE + col + dc : f * WIDE + col + dc + 1, :]) for dr, dc in NEAR]

    own_rho = rhos[0][col : col + 1, :]
    own_vx, own_vy = spread(own(PVX)), spread(own(PVY))
    own_q, own_r = spread(term(own_rho)), spread(own_rho)
    vxs, vys, rs = table(states, PVX), table(states, PVY), table(rhos, 0)
    ax = jnp.zeros((8, S), jnp.float32)
    ay = jnp.zeros((8, S), jnp.float32)
    for t in range(NT):
        slot, _, masks = decode(ref, start + 8 * t, numbers)
        base = (c * NT + t) * PAIR
        dx = pair[base : base + 8, :]
        dy = pair[base + 8 : base + 16, :]
        mass = pair[base + 16 : base + 24, :]
        soft = pair[base + 24 : base + 32, :]
        slope = pair[base + 32 : base + 40, :]
        rho = pick(rs, slot, masks)
        vdot = (own_vx - pick(vxs, slot, masks)) * dx + (own_vy - pick(vys, slot, masks)) * dy
        visc = visc_alpha * jnp.maximum(-vdot, 0.0) / (soft * (0.5 * (own_r + rho)))
        coef = mass * (own_q + term(rho) + visc) * slope
        ax = ax + coef * dx
        ay = ay + coef * dy
    live = own(PL)
    vx = own(PVX) + step_dt * jnp.sum(ax, axis=0, keepdims=True) * live
    vy = own(PVY) + step_dt * jnp.sum(ay, axis=0, keepdims=True) * live
    x = own(PX) + step_dt * vx * live
    y = own(PY) + step_dt * vy * live
    return (x, y, own(PM), vx, vy, live), own_rho


OUTER = SENT + PLACE


def middle_first_kernel(parity, frame, other, outer, send, last, right, rho, pair):
    lists = [(send, HALF + NB), (send, HALF + 2 * NB), (last, 0)] + [(right, HALF + NB * c) for c in range(3)]
    density(parity, {-1: (outer, 0), 0: (frame, 0), 1: (other, 0)}, lists, rho, pair)


def outer_first_kernel(parity, frame, outer, after, rho):
    lists = [(outer, OUTER + NB * (k + 1)) for k in range(RING)]
    density(parity, {-1: (outer, SENT), 0: (outer, 0), 1: (frame, 0)}, lists, rho, None)


def force_first_kernel(parity, frame, other, outer, rho_outer, rho_own, rho_other, send, last, right, pair, out):
    numbers = numbers_of(parity)
    lists = [(send, HALF + 2 * NB), (last, 0), (right, HALF), (right, HALF + NB)]
    for c in range(CELLS):
        fields, _ = force(
            c, numbers, frame, {-1: outer, 0: frame, 1: other}, {-1: rho_outer, 0: rho_own, 1: rho_other}, lists[c], pair
        )
        for k, v in enumerate(fields):
            out[k * CELLS + c : k * CELLS + c + 1, :] = v
    out[HALF : HALF + NB, :] = outer[OUTER + 3 * NB : OUTER + 4 * NB, :]
    out[HALF + NB : HALF + 2 * NB, :] = last[...]


def middle_second_kernel(parity, frame, other, outer, left, send, last, right, rho, pair):
    lists = [(left, HALF + NB)] + [(send, HALF + NB * c) for c in range(3)] + [(last, 0), (right, HALF)]
    density(parity, {-1: (outer, 0), 0: (frame, 0), 1: (other, 0)}, lists, rho, pair)


def outer_second_kernel(parity, frame, outer, left, before, after, rho):
    lists = [(left, HALF)] + [(before, OUTER + NB * c) for c in range(5)]
    density(parity, {-1: (outer, SENT), 0: (outer, 0), 1: (frame, 0)}, lists, rho, None)


def force_second_kernel(
    parity, dest, shell, frame, other, outer, rho_outer, rho_own, rho_other, send, last, pair, pos_out, vel_out, rho_out, part
):
    numbers = numbers_of(parity)
    lists = [(send, HALF), (send, HALF + NB), (send, HALF + 2 * NB), (last, 0)]
    total = jnp.zeros((S, S), jnp.float32)
    devices = lax.broadcasted_iota(jnp.int32, (S, S), 0)
    shells = lax.broadcasted_iota(jnp.int32, (16, S), 0)
    for c in range(CELLS):
        (x, y, m, vx, vy, live), rho = force(
            c, numbers, frame, {-1: outer, 0: frame, 1: other}, {-1: rho_outer, 0: rho_own, 1: rho_other}, lists[c], pair
        )
        pos_out[c : c + 1, :] = x
        pos_out[CELLS + c : CELLS + c + 1, :] = y
        vel_out[c : c + 1, :] = vx
        vel_out[CELLS + c : CELLS + c + 1, :] = vy
        rho_out[c : c + 1, :] = rho
        loads = (m * vx, m * vy, m * (sound_sq * (rho - 1.0)), 0.5 * m * (vx * vx + vy * vy))
        owner = (devices == dest[c : c + 1, :]).astype(jnp.bfloat16)
        member = shells == shell[c : c + 1, :]
        rest = jnp.concatenate([jnp.where(member, load, 0.0) for load in loads] + [jnp.zeros((S - 64, S), jnp.float32)], axis=0)
        for _ in range(3):
            some = rest.astype(jnp.bfloat16)
            total = total + lax.dot_general(owner, some, (((1,), (1,)), ((), ())), preferred_element_type=jnp.float32)
            rest = rest - some.astype(jnp.float32)
    part[...] = total


def soil_kernel(arrived, stress, rate, couple, out):
    total = jnp.sum(arrived[...], axis=0, keepdims=True)
    lane = lax.broadcasted_iota(jnp.int32, (16, S), 1)
    row = lax.broadcasted_iota(jnp.int32, (16, S), 0)
    force_x, force_y, force_p, force_e = [
        jnp.sum(jnp.where(lane == row + 16 * k, total, 0.0), axis=1, keepdims=True) for k in range(4)
    ]
    exx = rate[0] + couple[0] * force_x
    eyy = rate[1] + couple[1] * force_y
    exy = rate[2] + couple[2] * force_p
    ezz = -0.5 * (couple[0] + couple[1]) * force_e
    trace = exx + eyy + ezz
    sxx = stress[0] + soil_dt * (2.0 * shear_mod * (exx - trace / 3.0) + bulk_mod * trace)
    syy = stress[1] + soil_dt * (2.0 * shear_mod * (eyy - trace / 3.0) + bulk_mod * trace)
    szz = stress[2] + soil_dt * (2.0 * shear_mod * (ezz - trace / 3.0) + bulk_mod * trace)
    sxy = stress[3] + soil_dt * 2.0 * shear_mod * exy
    first = sxx + syy + szz
    mean = first / 3.0
    dxx = sxx - mean
    dyy = syy - mean
    dzz = szz - mean
    root = jnp.sqrt(0.5 * (dxx * dxx + dyy * dyy + dzz * dzz) + sxy * sxy)
    radius = jnp.maximum(cohesion - friction * first, 0.2 * cohesion)
    factor = radius / jnp.maximum(root, radius)
    out[0] = mean + factor * dxx
    out[1] = mean + factor * dyy
    out[2] = mean + factor * dzz
    out[3] = factor * sxy


def rows_of(n):
    return jax.ShapeDtypeStruct((n, S), jnp.float32)


def kept(n):
    return pltpu.VMEM((n, S), jnp.float32)


VM = pl.BlockSpec(memory_space=pltpu.MemorySpace.VMEM)
SM = pl.BlockSpec(memory_space=pltpu.MemorySpace.SMEM)


def held(a):
    return pltpu.with_memory_space_constraint(a, pltpu.MemorySpace.VMEM)


def local(
    fluid_pos,
    fluid_vel,
    fluid_mass,
    cell_count,
    nb_list,
    iface_dest,
    iface_shell,
    soil_stress,
    soil_rate,
    soil_couple,
):
    n_depth = lax.axis_size("depth")
    n_azim = lax.axis_size("azim")
    parity = (lax.axis_index("depth") % 2).astype(jnp.int32).reshape(1)
    toward_left = [(i, (i - 1) % n_azim) for i in range(n_azim)]
    toward_right = [(i, (i + 1) % n_azim) for i in range(n_azim)]
    pairs = [(i, i ^ 1) for i in range(n_depth)]
    facing = [(i, i + 1 if i % 2 else i - 1) for i in range(n_depth)]
    facing = [(i, j) for i, j in facing if 0 <= j < n_depth]

    def call(kernel, name, shapes, *args):
        return pl.pallas_call(
            kernel,
            out_shape=tuple(kept(n) for n in shapes),
            in_specs=[SM] + [VM] * len(args),
            out_specs=(VM,) * len(shapes),
            name=name,
        )(parity, *[held(a) for a in args])

    def merged(first, second):
        halves = [a[:HALF].reshape(6, CELLS, S) for a in (first, second)]
        return jnp.concatenate(halves, axis=1).reshape(6 * WIDE, S)

    def swapped(a):
        return lax.ppermute(a, "depth", pairs)

    send, last = pl.pallas_call(
        pack_kernel,
        out_shape=(kept(HALF + 3 * NB), kept(NB)),
        in_specs=[SM, VM, VM, VM, VM],
        out_specs=(VM, VM),
        name="pack",
    )(
        cell_count,
        fluid_pos.reshape(2 * CELLS, S),
        fluid_vel.reshape(2 * CELLS, S),
        fluid_mass.reshape(CELLS, S),
        nb_list.reshape(NB * CELLS, S),
    )
    right = lax.ppermute(send, "azim", toward_left)
    frame = merged(send, right)
    other = swapped(frame[:SENT])
    outer = lax.ppermute(
        jnp.concatenate([frame[:SENT], other[:PLACE], send[HALF:], last, right[HALF:]], axis=0), "depth", facing
    )
    rho_own, pair = call(
        middle_first_kernel, "middle_first", (WIDE, CELLS * NT * PAIR), frame, other, outer, send, last, right
    )
    rho_other = swapped(rho_own)
    (rho_outer,) = call(outer_first_kernel, "outer_first", (WIDE,), frame, outer, rho_own)
    (mid,) = call(
        force_first_kernel,
        "force_first",
        (HALF + 2 * NB,),
        frame, other, outer, rho_outer, rho_own, rho_other, send, last, right, pair,
    )

    left = lax.ppermute(mid, "azim", toward_right)
    frame = merged(left, mid)
    other = swapped(frame[:SENT])
    beyond = lax.ppermute(jnp.concatenate([frame[:SENT], other[:PLACE]], axis=0), "depth", facing)
    rho_own, pair = call(
        middle_second_kernel, "middle_second", (WIDE, CELLS * NT * PAIR), frame, other, beyond, left, send, last, right
    )
    rho_other = swapped(rho_own)
    (rho_outer,) = call(outer_second_kernel, "outer_second", (WIDE,), frame, beyond, left, outer, rho_own)
    pos, vel, rho, part = call(
        force_second_kernel,
        "force_second",
        (2 * CELLS, 2 * CELLS, CELLS, S),
        iface_dest.reshape(CELLS, S), iface_shell.reshape(CELLS, S),
        frame, other, beyond, rho_outer, rho_own, rho_other, send, last, pair,
    )

    arrived = lax.all_to_all(part, ("depth", "azim"), split_axis=0, concat_axis=0, tiled=True)
    stress_out = pl.pallas_call(
        soil_kernel,
        out_shape=jax.ShapeDtypeStruct(soil_stress.shape, jnp.float32),
        in_specs=[VM] * 4,
        out_specs=VM,
        name="soil",
    )(held(arrived), held(soil_stress), held(soil_rate), held(soil_couple))
    return (
        pos.reshape(fluid_pos.shape),
        vel.reshape(fluid_vel.shape),
        rho.reshape(fluid_mass.shape),
        stress_out,
    )


def solution(mesh):
    return jax.shard_map(
        local,
        mesh=mesh,
        in_specs=(
            P(None, "depth", "azim", None),
            P(None, "depth", "azim", None),
            P("depth", "azim", None),
            P("depth", "azim"),
            P(None, "depth", "azim", None),
            P(("depth", "azim"), None, None),
            P(("depth", "azim"), None),
            P(None, ("depth", "azim"), None),
            P(None, ("depth", "azim"), None),
            P(None, ("depth", "azim"), None),
        ),
        out_specs=(
            P(None, "depth", "azim", None),
            P(None, "depth", "azim", None),
            P("depth", "azim", None),
            P(None, ("depth", "azim"), None),
        ),
        check_vma=False,
    )
```

time: 61.4 us -> 57.7 us (0.940)
  waiting for transfers between devices: 27.6 us -> 24.1 us
  Pallas kernels: 7.66 us -> 6.21 us
  local copies, waits for them, and re-layouts: 1.81 us -> 2.5 us
    ppermute x7, waiting for transfers between devices: 11.2 us -> 8.66 us  [the longest x1 3.24 us: local(): lax.ppermute(jnp.concatenate([frame[:SENT], other[:PLACE], send[HALF:], l...]
    pallas_call x3 -> x7, Pallas kernels: 6.91 us -> 5.45 us  [the longest x6 4.58 us: call(): pl.pallas_call(kernel, out_shape=tuple((kept(n) for n in shapes)), in_spe...]
    ppermute x1, waiting for transfers between devices: 8.32 us -> 7.43 us  [local(): left = lax.ppermute(mid, 'azim', toward_right)]
    unnamed x13 -> x16, local copies, waits for them, and re-layouts: 1.79 us -> 2.48 us
  transfers between devices with their start and end apart: 9 -> 9, of which waited for: 9 -> 9; matrix products, arithmetic and copies ran while one was open for 3% -> 3% of each run, Pallas kernels for 0% -> 2%
where the time goes in v4:
time: 57.7 us; the launch traced here: 57.4 us
  waiting for transfers between devices  24.1 us (42%)
  starting transfers between devices  23.8 us (41%)
  Pallas kernels  6.21 us (11%)
  local copies, waits for them, and re-layouts  2.5 us (4%)
  between operations  0.78 us (1%)
    all_to_all x1, waiting for transfers between devices, local(): lax.all_to_all(part, ('depth', 'azim'), split_axis=0, concat_axis=0, tile...  8.03 us
    all_to_all x1, starting transfers between devices, local(): lax.all_to_all(part, ('depth', 'azim'), split_axis=0, concat_axis=0, tile...  7.82 us
    ppermute x1, waiting for transfers between devices, local(): left = lax.ppermute(mid, 'azim', toward_right)  7.43 us
    ppermute x1, starting transfers between devices, local(): right = lax.ppermute(send, 'azim', toward_left)  6.69 us
    pallas_call x6, Pallas kernels, call(): pl.pallas_call(kernel, out_shape=tuple((kept(n) for n in shapes)), in_spe...  4.58 us
    ppermute x1, starting transfers between devices, local(): lax.ppermute(jnp.concatenate([frame[:SENT], other[:PLACE]], axis=0), 'dep...  3.79 us
    ppermute x1, waiting for transfers between devices, local(): lax.ppermute(jnp.concatenate([frame[:SENT], other[:PLACE], send[HALF:], l...  3.24 us
    ppermute x1, starting transfers between devices, local(): lax.ppermute(jnp.concatenate([frame[:SENT], other[:PLACE], send[HALF:], l...  2.88 us
  transfers between devices with their start and end apart: 9, of which 9 were waited for; matrix products, arithmetic and copies ran while one was open for 3% of the time, Pallas kernels for 2%

profile of v4, /device:TPU:1, one launch (start us, length us, event | category | flops | bytes accessed | tf_op | source)
XLA Modules:
  0.0 57.4 jit_solution(6105572590294367095)
XLA Ops:
  0.6 0.9 %pack.1 = (f32[96,128]{1,0:T(8,128)S(1)}, f32[24,128]{1,0:T(8,128)S(1)}) custom-call(s32[1,4]{1,0:T(1,128)} %count.1, f32[8,128]{1,0:T(8,128)} %bitcast.46, f32[8,128]{1,0:T(8,128)} %bitcast.47, f32[4,128]{1,0:T(4,128)} %bitcast.48, s32[96,128]{1,0:T(8,128)} %bitcast.45), custom_call_target="tpu_custom_call" | custom-call | tf_op jit(solution)/shard_map/pack/pallas_call | solution.py:300
  1.5 6.7 %collective-permute-start = (f32[96,128]{1,0:T(8,128)S(1)}, f32[96,128]{1,0:T(8,128)S(1)}, u32[]{:S(2)}, u32[]{:S(2)}) collective-permute-start(f32[96,128]{1,0:T(8,128)S(1)} %get-tuple-element.14.send), channel_id=1, source_target_pairs={{0,7},{1,0},{2,1},{3,2},{4,3},{5,4},{6,5},{7,6},{8,15},{9,8},{10,9... | collective-permute-start | bytes 147464 | tf_op jit(solution)/shard_map/ppermute | solution.py:313
  8.2 1.2 %collective-permute-done.right = f32[96,128]{1,0:T(8,128)S(1)} collective-permute-done((f32[96,128]{1,0:T(8,128)S(1)}, f32[96,128]{1,0:T(8,128)S(1)}, u32[]{:S(2)}, u32[]{:S(2)}) %collective-permute-start) | collective-permute-done | bytes 49184 | tf_op jit(solution)/shard_map/ppermute | solution.py:313
  9.4 1.6 %collective-permute-start.1 = (f32[40,128]{1,0:T(8,128)S(1)}, f32[40,128]{1,0:T(8,128)S(1)}, u32[]{:S(2)}, u32[]{:S(2)}) collective-permute-start(f32[40,128]{1,0:T(8,128)S(1)} %get-tuple-element.33), channel_id=1, source_target_pairs={{0,8},{8,0},{16,24},{24,16},{32,40},{40,32},{48,56},{56,48},{64,72... | collective-permute-start | bytes 61448 | tf_op jit(solution)/shard_map/ppermute | solution.py:298
  11.0 0.8 %collective-permute-done.1.other = f32[40,128]{1,0:T(8,128)S(1)} collective-permute-done((f32[40,128]{1,0:T(8,128)S(1)}, f32[40,128]{1,0:T(8,128)S(1)}, u32[]{:S(2)}, u32[]{:S(2)}) %collective-permute-start.1) | collective-permute-done | bytes 20512 | tf_op jit(solution)/shard_map/ppermute | solution.py:298
  11.9 2.9 %collective-permute-start.2 = (f32[232,128]{1,0:T(8,128)S(1)}, f32[232,128]{1,0:T(8,128)S(1)}, u32[]{:S(2)}, u32[]{:S(2)}) collective-permute-start(f32[232,128]{1,0:T(8,128)S(1)} %slice_dynamic-update-slice_fusion), channel_id=1, source_target_pairs={{8,16},{16,8},{24,32},{32,24},{40,48},{48,40},{56,64},{64,56},{72,... | collective-permute-start | bytes 356360 | tf_op jit(solution)/shard_map/ppermute | solution.py:316
  14.8 3.2 %collective-permute-done.2.outer.before = f32[232,128]{1,0:T(8,128)S(1)} collective-permute-done((f32[232,128]{1,0:T(8,128)S(1)}, f32[232,128]{1,0:T(8,128)S(1)}, u32[]{:S(2)}, u32[]{:S(2)}) %collective-permute-start.2) | collective-permute-done | bytes 118816 | tf_op jit(solution)/shard_map/ppermute | solution.py:316
  18.0 0.6 %middle_first.1 = (f32[8,128]{1,0:T(8,128)S(1)}, f32[480,128]{1,0:T(8,128)S(1)}) custom-call(s32[1]{0:T(128)} %bitcast.parity, f32[48,128]{1,0:T(8,128)S(1)} %fusion.1.frame, f32[40,128]{1,0:T(8,128)S(1)} %collective-permute-done.1.other, f32[232,128]{1,0:T(8,128)S(1)} %collective-permute-done.2.outer.before, f32[96,128]{1,0:T(8,128)S(1)} %get-tuple-element.14.send, ...), custom_call_target="tpu_custom_call" | custom-call | tf_op jit(solution)/shard_map/middle_first/pallas_call | solution.py:285
  18.7 0.1 collective-permute-start.3
  18.8 0.7 %outer_first.1.rho_outer = f32[8,128]{1,0:T(8,128)S(1)} custom-call(s32[1]{0:T(128)} %bitcast.parity, f32[48,128]{1,0:T(8,128)S(1)} %fusion.1.frame, f32[232,128]{1,0:T(8,128)S(1)} %collective-permute-done.2.outer.before, f32[8,128]{1,0:T(8,128)S(1)} %get-tuple-element.16.after.rho_own), custom_call_target="tpu_custom_call" | custom-call | tf_op jit(solution)/shard_map/outer_first/pallas_call | solution.py:285
  19.4 0.5 collective-permute-done.3.rho_other
  19.9 0.5 force_first.1
  20.4 0.1 collective-permute-start.4
  20.5 7.4 %collective-permute-done.4.left = f32[72,128]{1,0:T(8,128)S(1)} collective-permute-done((f32[72,128]{1,0:T(8,128)S(1)}, f32[72,128]{1,0:T(8,128)S(1)}, u32[]{:S(2)}, u32[]{:S(2)}) %collective-permute-start.4) | collective-permute-done | bytes 36896 | tf_op jit(solution)/shard_map/ppermute | solution.py:331
  28.0 0.7 %collective-permute-start.5 = (f32[40,128]{1,0:T(8,128)S(1)}, f32[40,128]{1,0:T(8,128)S(1)}, u32[]{:S(2)}, u32[]{:S(2)}) collective-permute-start(f32[40,128]{1,0:T(8,128)S(1)} %fusion.3), channel_id=1, source_target_pairs={{0,8},{8,0},{16,24},{24,16},{32,40},{40,32},{48,56},{56,48},{64,72... | collective-permute-start | bytes 61448 | tf_op jit(solution)/shard_map/ppermute | solution.py:298
  28.7 0.8 %collective-permute-done.5.other = f32[40,128]{1,0:T(8,128)S(1)} collective-permute-done((f32[40,128]{1,0:T(8,128)S(1)}, f32[40,128]{1,0:T(8,128)S(1)}, u32[]{:S(2)}, u32[]{:S(2)}) %collective-permute-start.5) | collective-permute-done | bytes 20512 | tf_op jit(solution)/shard_map/ppermute | solution.py:298
  29.5 3.8 %collective-permute-start.6 = (f32[64,128]{1,0:T(8,128)S(1)}, f32[64,128]{1,0:T(8,128)S(1)}, u32[]{:S(2)}, u32[]{:S(2)}) collective-permute-start(f32[64,128]{1,0:T(8,128)S(1)} %pad_maximum_fusion), channel_id=1, source_target_pairs={{8,16},{16,8},{24,32},{32,24},{40,48},{48,40},{56,64},{64,56},{72,... | collective-permute-start | bytes 98312 | tf_op jit(solution)/shard_map/ppermute | solution.py:334
  33.4 1.6 %collective-permute-done.6.outer = f32[64,128]{1,0:T(8,128)S(1)} collective-permute-done((f32[64,128]{1,0:T(8,128)S(1)}, f32[64,128]{1,0:T(8,128)S(1)}, u32[]{:S(2)}, u32[]{:S(2)}) %collective-permute-start.6) | collective-permute-done | bytes 32800 | tf_op jit(solution)/shard_map/ppermute | solution.py:334
  34.9 0.7 %middle_second.1 = (f32[8,128]{1,0:T(8,128)S(1)}, f32[480,128]{1,0:T(8,128)S(1)}) custom-call(s32[1]{0:T(128)} %bitcast.parity, f32[48,128]{1,0:T(8,128)S(1)} %fusion.frame, f32[40,128]{1,0:T(8,128)S(1)} %collective-permute-done.5.other, f32[64,128]{1,0:T(8,128)S(1)} %collective-permute-done.6.outer, f32[72,128]{1,0:T(8,128)S(1)} %collective-permute-done.4.left, ...), custom_call_target="tpu_custom_call" | custom-call | tf_op jit(solution)/shard_map/middle_second/pallas_call | solution.py:285
  35.6 0.1 collective-permute-start.7
  35.7 0.7 %outer_second.1.rho_outer = f32[8,128]{1,0:T(8,128)S(1)} custom-call(s32[1]{0:T(128)} %bitcast.parity, f32[48,128]{1,0:T(8,128)S(1)} %fusion.frame, f32[64,128]{1,0:T(8,128)S(1)} %collective-permute-done.6.outer, f32[72,128]{1,0:T(8,128)S(1)} %collective-permute-done.4.left, f32[232,128]{1,0:T(8,128)S(1)} %collective-permute-done.2.outer.before, ...), custom_call_target="tpu_custom_call" | custom-call | tf_op jit(solution)/shard_map/outer_second/pallas_call | solution.py:285
  36.3 0.5 collective-permute-done.7.rho_other
  36.8 0.0 copy-start.4
  36.8 0.0 copy-start.3
  36.8 0.7 %copy-done.4 = s32[1,512]{1,0:T(1,128)S(1)} copy-done((s32[1,512]{1,0:T(1,128)S(1)}, s32[1,512]{1,0:T(1,128)}, u32[]{:S(2)}) %copy-start.4) | copy-done | bytes 2072
  37.5 0.0 copy-done.3
  37.5 1.5 %force_second.1 = (f32[8,128]{1,0:T(8,128)S(1)}, f32[8,128]{1,0:T(8,128)S(1)}, f32[4,128]{1,0:T(4,128)S(1)}, f32[128,128]{1,0:T(8,128)}) custom-call(s32[1]{0:T(128)} %bitcast.parity, s32[4,128]{1,0:T(4,128)S(1)} %bitcast.35, s32[4,128]{1,0:T(4,128)S(1)} %bitcast.36, f32[48,128]{1,0:T(8,128)S(1)} %fusion.frame, f32[40,128]{1,0:T(8,128)S(1)} %collective-permute-done.5.other, ...), custom_call_target="tpu_custom_call" | custom-call | tf_op jit(solution)/shard_map/force_second/pallas_call | solution.py:285
  39.0 0.0 copy-start.1
  39.0 0.0 copy-start.2
  39.0 7.8 %all-to-all-start = ((f32[128,1,128]{2,1,0:T(1,128)}), f32[128,1,128]{2,1,0:T(1,128)S(1)}, u32[]{:S(2)}, u32[]{:S(2)}) async-start(f32[128,1,128]{2,1,0:T(1,128)} %bitcast.21), calls=%async_computation | async-start | bytes 131072 | tf_op jit(solution)/shard_map/all_to_all | solution.py:348
  46.8 0.0 copy-start
  46.9 0.6 %copy.23 = f32[2,1,4,128]{3,2,1,0:T(4,128)} copy(f32[2,1,4,128]{3,2,1,0:T(4,128)S(1)} %bitcast.32) | data formatting | bytes 8192
  47.5 0.6 %copy.24 = f32[2,1,4,128]{3,2,1,0:T(4,128)} copy(f32[2,1,4,128]{3,2,1,0:T(4,128)S(1)} %bitcast.31) | data formatting | bytes 8192
  48.0 0.6 %copy.25 = f32[1,4,128]{2,1,0:T(4,128)} copy(f32[1,4,128]{2,1,0:T(4,128)S(1)} %bitcast.33) | data formatting | bytes 4096
  48.6 8.0 %all-to-all-done = f32[128,1,128]{2,1,0:T(1,128)S(1)} async-done(((f32[128,1,128]{2,1,0:T(1,128)}), f32[128,1,128]{2,1,0:T(1,128)S(1)}, u32[]{:S(2)}, u32[]{:S(2)}) %all-to-all-start) | async-done | bytes 65568 | tf_op jit(solution)/shard_map/all_to_all | solution.py:348
  56.6 0.0 copy-done.1
  56.7 0.0 copy-done.2
  56.7 0.0 copy-done
  56.7 0.8 %soil.1 = f32[4,16,128]{2,1,0:T(8,128)} custom-call(f32[128,128]{1,0:T(8,128)S(1)} %bitcast.34, f32[4,16,128]{2,1,0:T(8,128)S(1)} %copy-done, f32[3,16,128]{2,1,0:T(8,128)S(1)} %copy-done.1, f32[3,16,128]{2,1,0:T(8,128)S(1)} %copy-done.2), custom_call_target="tpu_custom_call" | custom-call | tf_op jit(solution)/shard_map/soil/pallas_call | solution.py:349
  (14 shorter events, 0.1 us)
Async XLA Ops:
  1.5 7.9 %collective-permute-start = (f32[96,128]{1,0:T(8,128)S(1)}, f32[96,128]{1,0:T(8,128)S(1)}, u32[]{:S(2)}, u32[]{:S(2)}) collective-permute-start(f32[96,128]{1,0:T(8,128)S(1)} %get-tuple-element.14.send), channel_id=1, source_target_pairs={{0,7},{1,0},{2,1},{3,2},{4,3},{5,4},{6,5},{7,6},{8,15},{9,8},{10,9... | collective-permute-start | bytes 147464 | tf_op jit(solution)/shard_map/ppermute | solution.py:313
  9.4 2.5 %collective-permute-start.1 = (f32[40,128]{1,0:T(8,128)S(1)}, f32[40,128]{1,0:T(8,128)S(1)}, u32[]{:S(2)}, u32[]{:S(2)}) collective-permute-start(f32[40,128]{1,0:T(8,128)S(1)} %get-tuple-element.33), channel_id=1, source_target_pairs={{0,8},{8,0},{16,24},{24,16},{32,40},{40,32},{48,56},{56,48},{64,72... | collective-permute-start | bytes 61448 | tf_op jit(solution)/shard_map/ppermute | solution.py:298
  11.9 6.2 %collective-permute-start.2 = (f32[232,128]{1,0:T(8,128)S(1)}, f32[232,128]{1,0:T(8,128)S(1)}, u32[]{:S(2)}, u32[]{:S(2)}) collective-permute-start(f32[232,128]{1,0:T(8,128)S(1)} %slice_dynamic-update-slice_fusion), channel_id=1, source_target_pairs={{8,16},{16,8},{24,32},{32,24},{40,48},{48,40},{56,64},{64,56},{72,... | collective-permute-start | bytes 356360 | tf_op jit(solution)/shard_map/ppermute | solution.py:316
  18.7 1.2 %collective-permute-start.3 = (f32[8,128]{1,0:T(8,128)S(1)}, f32[8,128]{1,0:T(8,128)S(1)}, u32[]{:S(2)}, u32[]{:S(2)}) collective-permute-start(f32[8,128]{1,0:T(8,128)S(1)} %get-tuple-element.16.after.rho_own), channel_id=1, source_target_pairs={{0,8},{8,0},{16,24},{24,16},{32,40},{40,32},{48,56},{56,48},{64,72... | collective-permute-start | bytes 12296 | tf_op jit(solution)/shard_map/ppermute | solution.py:298
  20.4 7.5 %collective-permute-start.4 = (f32[72,128]{1,0:T(8,128)S(1)}, f32[72,128]{1,0:T(8,128)S(1)}, u32[]{:S(2)}, u32[]{:S(2)}) collective-permute-start(f32[72,128]{1,0:T(8,128)S(1)} %force_first.1), channel_id=1, source_target_pairs={{0,1},{1,2},{2,3},{3,4},{4,5},{5,6},{6,7},{7,0},{8,9},{9,10},{10,1... | collective-permute-start | bytes 110600 | tf_op jit(solution)/shard_map/ppermute | solution.py:331
  28.0 1.6 %collective-permute-start.5 = (f32[40,128]{1,0:T(8,128)S(1)}, f32[40,128]{1,0:T(8,128)S(1)}, u32[]{:S(2)}, u32[]{:S(2)}) collective-permute-start(f32[40,128]{1,0:T(8,128)S(1)} %fusion.3), channel_id=1, source_target_pairs={{0,8},{8,0},{16,24},{24,16},{32,40},{40,32},{48,56},{56,48},{64,72... | collective-permute-start | bytes 61448 | tf_op jit(solution)/shard_map/ppermute | solution.py:298
  29.5 5.4 %collective-permute-start.6 = (f32[64,128]{1,0:T(8,128)S(1)}, f32[64,128]{1,0:T(8,128)S(1)}, u32[]{:S(2)}, u32[]{:S(2)}) collective-permute-start(f32[64,128]{1,0:T(8,128)S(1)} %pad_maximum_fusion), channel_id=1, source_target_pairs={{8,16},{16,8},{24,32},{32,24},{40,48},{48,40},{56,64},{64,56},{72,... | collective-permute-start | bytes 98312 | tf_op jit(solution)/shard_map/ppermute | solution.py:334
  35.6 1.2 %collective-permute-start.7 = (f32[8,128]{1,0:T(8,128)S(1)}, f32[8,128]{1,0:T(8,128)S(1)}, u32[]{:S(2)}, u32[]{:S(2)}) collective-permute-start(f32[8,128]{1,0:T(8,128)S(1)} %get-tuple-element.18.after.rho_own), channel_id=1, source_target_pairs={{0,8},{8,0},{16,24},{24,16},{32,40},{40,32},{48,56},{56,48},{64,72... | collective-permute-start | bytes 12296 | tf_op jit(solution)/shard_map/ppermute | solution.py:298
  36.8 0.7 %copy-start.4 = (s32[1,512]{1,0:T(1,128)S(1)}, s32[1,512]{1,0:T(1,128)}, u32[]{:S(2)}) copy-start(s32[1,512]{1,0:T(1,128)} %param.16) | copy-start | bytes 6148
  36.8 0.7 %copy-start.3 = (s32[1,512,1]{1,2,0:T(1,128)S(1)}, s32[1,512,1]{1,2,0:T(1,128)}, u32[]{:S(2)}) copy-start(s32[1,512,1]{1,2,0:T(1,128)} %param.15) | copy-start | bytes 6148
  39.0 17.6 %copy-start.1 = (f32[3,16,128]{2,1,0:T(8,128)S(1)}, f32[3,16,128]{2,1,0:T(8,128)}, u32[]{:S(2)}) copy-start(f32[3,16,128]{2,1,0:T(8,128)} %rate.1) | copy-start | bytes 73732
  39.0 17.6 %copy-start.2 = (f32[3,16,128]{2,1,0:T(8,128)S(1)}, f32[3,16,128]{2,1,0:T(8,128)}, u32[]{:S(2)}) copy-start(f32[3,16,128]{2,1,0:T(8,128)} %couple.1) | copy-start | bytes 73732
  39.0 17.6 %all-to-all-start = ((f32[128,1,128]{2,1,0:T(1,128)}), f32[128,1,128]{2,1,0:T(1,128)S(1)}, u32[]{:S(2)}, u32[]{:S(2)}) async-start(f32[128,1,128]{2,1,0:T(1,128)} %bitcast.21), calls=%async_computation | async-start | bytes 131072 | tf_op jit(solution)/shard_map/all_to_all | solution.py:348
  46.8 9.8 %copy-start = (f32[4,16,128]{2,1,0:T(8,128)S(1)}, f32[4,16,128]{2,1,0:T(8,128)}, u32[]{:S(2)}) copy-start(f32[4,16,128]{2,1,0:T(8,128)} %stress.1) | copy-start | bytes 98308

commit v5 on v4

--- a/solution.py
+++ b/solution.py
@@ -29,7 +29,12 @@
 NEAR = [(dr, dc) for dr in (-1, 0, 1) for dc in (-1, 0, 1)]
 
 
-def pack_kernel(count, pos, vel, mass, nb, out, last):
+def pack_kernel(count, pos, vel, mass, nb, dest, shell, stress, rate, couple, out, first, home, soil):
+    soil[0:4] = stress[...]
+    soil[4:7] = rate[...]
+    soil[7:10] = couple[...]
+    home[0:CELLS, :] = dest[...]
+    home[CELLS : 2 * CELLS, :] = shell[...]
     lane = lax.broadcasted_iota(jnp.int32, (1, S), 1)
     out[0 : 2 * CELLS, :] = pos[...]
     out[PVX * CELLS : (PVX + 2) * CELLS, :] = vel[...]
@@ -38,10 +43,10 @@
         out[PM * CELLS + c : PM * CELLS + c + 1, :] = mass[c : c + 1, :] * live
         out[PL * CELLS + c : PL * CELLS + c + 1, :] = live
         codes = nb[pl.ds(c, NB, stride=CELLS), :].astype(jnp.float32)
-        if c < CELLS - 1:
-            out[HALF + NB * c : HALF + NB * (c + 1), :] = codes
+        if c:
+            out[HALF + NB * (c - 1) : HALF + NB * c, :] = codes
         else:
-            last[...] = codes
+            first[...] = codes
 
 
 def spread(row):
@@ -153,19 +158,19 @@
 OUTER = SENT + PLACE
 
 
-def middle_first_kernel(parity, frame, other, outer, send, last, right, rho, pair):
-    lists = [(send, HALF + NB), (send, HALF + 2 * NB), (last, 0)] + [(right, HALF + NB * c) for c in range(3)]
+def middle_first_kernel(parity, frame, other, outer, left, first, send, rho, pair):
+    lists = [(left, HALF + NB * c) for c in range(3)] + [(first, 0), (send, HALF), (send, HALF + NB)]
     density(parity, {-1: (outer, 0), 0: (frame, 0), 1: (other, 0)}, lists, rho, pair)
 
 
 def outer_first_kernel(parity, frame, outer, after, rho):
-    lists = [(outer, OUTER + NB * (k + 1)) for k in range(RING)]
+    lists = [(outer, OUTER + NB * k) for k in range(RING)]
     density(parity, {-1: (outer, SENT), 0: (outer, 0), 1: (frame, 0)}, lists, rho, None)
 
 
-def force_first_kernel(parity, frame, other, outer, rho_outer, rho_own, rho_other, send, last, right, pair, out):
+def force_first_kernel(parity, frame, other, outer, rho_outer, rho_own, rho_other, left, first, send, pair, out):
     numbers = numbers_of(parity)
-    lists = [(send, HALF + 2 * NB), (last, 0), (right, HALF), (right, HALF + NB)]
+    lists = [(left, HALF + NB), (left, HALF + 2 * NB), (first, 0), (send, HALF)]
     for c in range(CELLS):
         fields, _ = force(
             c, numbers, frame, {-1: outer, 0: frame, 1: other}, {-1: rho_outer, 0: rho_own, 1: rho_other}, lists[c], pair
@@ -173,27 +178,27 @@
         for k, v in enumerate(fields):
             out[k * CELLS + c : k * CELLS + c + 1, :] = v
     out[HALF : HALF + NB, :] = outer[OUTER + 3 * NB : OUTER + 4 * NB, :]
-    out[HALF + NB : HALF + 2 * NB, :] = last[...]
-
-
-def middle_second_kernel(parity, frame, other, outer, left, send, last, right, rho, pair):
-    lists = [(left, HALF + NB)] + [(send, HALF + NB * c) for c in range(3)] + [(last, 0), (right, HALF)]
+    out[HALF + NB : HALF + 2 * NB, :] = first[...]
+
+
+def middle_second_kernel(parity, frame, other, outer, right, left, first, send, rho, pair):
+    lists = [(left, HALF + 2 * NB), (first, 0)] + [(send, HALF + NB * c) for c in range(3)] + [(right, HALF + NB)]
     density(parity, {-1: (outer, 0), 0: (frame, 0), 1: (other, 0)}, lists, rho, pair)
 
 
-def outer_second_kernel(parity, frame, outer, left, before, after, rho):
-    lists = [(left, HALF)] + [(before, OUTER + NB * c) for c in range(5)]
+def outer_second_kernel(parity, frame, outer, right, before, after, rho):
+    lists = [(before, OUTER + NB * (2 + c)) for c in range(5)] + [(right, HALF)]
     density(parity, {-1: (outer, SENT), 0: (outer, 0), 1: (frame, 0)}, lists, rho, None)
 
 
 def force_second_kernel(
-    parity, dest, shell, frame, other, outer, rho_outer, rho_own, rho_other, send, last, pair, pos_out, vel_out, rho_out, part
+    parity, home, frame, other, outer, rho_outer, rho_own, rho_other, first, send, pair, pos_out, vel_out, rho_out, part
 ):
     numbers = numbers_of(parity)
-    lists = [(send, HALF), (send, HALF + NB), (send, HALF + 2 * NB), (last, 0)]
-    total = jnp.zeros((S, S), jnp.float32)
+    lists = [(first, 0), (send, HALF), (send, HALF + NB), (send, HALF + 2 * NB)]
     devices = lax.broadcasted_iota(jnp.int32, (S, S), 0)
     shells = lax.broadcasted_iota(jnp.int32, (16, S), 0)
+    owners, shares = [], []
     for c in range(CELLS):
         (x, y, m, vx, vy, live), rho = force(
             c, numbers, frame, {-1: outer, 0: frame, 1: other}, {-1: rho_outer, 0: rho_own, 1: rho_other}, lists[c], pair
@@ -204,17 +209,30 @@
         vel_out[CELLS + c : CELLS + c + 1, :] = vy
         rho_out[c : c + 1, :] = rho
         loads = (m * vx, m * vy, m * (sound_sq * (rho - 1.0)), 0.5 * m * (vx * vx + vy * vy))
-        owner = (devices == dest[c : c + 1, :]).astype(jnp.bfloat16)
-        member = shells == shell[c : c + 1, :]
-        rest = jnp.concatenate([jnp.where(member, load, 0.0) for load in loads] + [jnp.zeros((S - 64, S), jnp.float32)], axis=0)
+        owner = (devices == home[c : c + 1, :]).astype(jnp.bfloat16)
+        member = shells == home[CELLS + c : CELLS + c + 1, :]
+        rest = jnp.concatenate([jnp.where(member, load, 0.0) for load in loads], axis=0)
         for _ in range(3):
             some = rest.astype(jnp.bfloat16)
-            total = total + lax.dot_general(owner, some, (((1,), (1,)), ((), ())), preferred_element_type=jnp.float32)
+            owners.append(owner)
+            shares.append(some)
             rest = rest - some.astype(jnp.float32)
-    part[...] = total
-
-
-def soil_kernel(arrived, stress, rate, couple, out):
+    total = lax.dot_general(
+        jnp.concatenate(owners, axis=1),
+        jnp.concatenate(shares, axis=1),
+        (((1,), (1,)), ((), ())),
+        preferred_element_type=jnp.float32,
+    )
+    part[...] = jnp.concatenate([total, jnp.zeros((S, S - 64), jnp.float32)], axis=1)
+
+
+def soil_kernel(arrived, soil, pos, vel, rho, stress_out, pos_out, vel_out, rho_out):
+    pos_out[...] = pos[...]
+    vel_out[...] = vel[...]
+    rho_out[...] = rho[...]
+    stress = [soil[k] for k in range(4)]
+    rate = [soil[4 + k] for k in range(3)]
+    couple = [soil[7 + k] for k in range(3)]
     total = jnp.sum(arrived[...], axis=0, keepdims=True)
     lane = lax.broadcasted_iota(jnp.int32, (16, S), 1)
     row = lax.broadcasted_iota(jnp.int32, (16, S), 0)
@@ -238,10 +256,10 @@
     root = jnp.sqrt(0.5 * (dxx * dxx + dyy * dyy + dzz * dzz) + sxy * sxy)
     radius = jnp.maximum(cohesion - friction * first, 0.2 * cohesion)
     factor = radius / jnp.maximum(root, radius)
-    out[0] = mean + factor * dxx
-    out[1] = mean + factor * dyy
-    out[2] = mean + factor * dzz
-    out[3] = factor * sxy
+    stress_out[0] = mean + factor * dxx
+    stress_out[1] = mean + factor * dyy
+    stress_out[2] = mean + factor * dzz
+    stress_out[3] = factor * sxy
 
 
 def rows_of(n):
@@ -297,11 +315,16 @@
     def swapped(a):
         return lax.ppermute(a, "depth", pairs)
 
-    send, last = pl.pallas_call(
+    send, first, home, soil = pl.pallas_call(
         pack_kernel,
-        out_shape=(kept(HALF + 3 * NB), kept(NB)),
-        in_specs=[SM, VM, VM, VM, VM],
-        out_specs=(VM, VM),
+        out_shape=(
+            kept(HALF + 3 * NB),
+            kept(NB),
+            pltpu.VMEM((2 * CELLS, S), jnp.int32),
+            pltpu.VMEM((10,) + soil_stress.shape[1:], jnp.float32),
+        ),
+        in_specs=[SM] + [VM] * 9,
+        out_specs=(VM, VM, VM, VM),
         name="pack",
     )(
         cell_count,
@@ -309,15 +332,20 @@
         fluid_vel.reshape(2 * CELLS, S),
         fluid_mass.reshape(CELLS, S),
         nb_list.reshape(NB * CELLS, S),
-    )
-    right = lax.ppermute(send, "azim", toward_left)
-    frame = merged(send, right)
+        iface_dest.reshape(CELLS, S),
+        iface_shell.reshape(CELLS, S),
+        soil_stress,
+        soil_rate,
+        soil_couple,
+    )
+    left = lax.ppermute(send, "azim", toward_right)
+    frame = merged(left, send)
     other = swapped(frame[:SENT])
     outer = lax.ppermute(
-        jnp.concatenate([frame[:SENT], other[:PLACE], send[HALF:], last, right[HALF:]], axis=0), "depth", facing
+        jnp.concatenate([frame[:SENT], other[:PLACE], left[HALF:], first, send[HALF:]], axis=0), "depth", facing
     )
     rho_own, pair = call(
-        middle_first_kernel, "middle_first", (WIDE, CELLS * NT * PAIR), frame, other, outer, send, last, right
+        middle_first_kernel, "middle_first", (WIDE, CELLS * NT * PAIR), frame, other, outer, left, first, send
     )
     rho_other = swapped(rho_own)
     (rho_outer,) = call(outer_first_kernel, "outer_first", (WIDE,), frame, outer, rho_own)
@@ -325,34 +353,35 @@
         force_first_kernel,
         "force_first",
         (HALF + 2 * NB,),
-        frame, other, outer, rho_outer, rho_own, rho_other, send, last, right, pair,
-    )
-
-    left = lax.ppermute(mid, "azim", toward_right)
-    frame = merged(left, mid)
+        frame, other, outer, rho_outer, rho_own, rho_other, left, first, send, pair,
+    )
+
+    right = lax.ppermute(mid, "azim", toward_left)
+    frame = merged(mid, right)
     other = swapped(frame[:SENT])
     beyond = lax.ppermute(jnp.concatenate([frame[:SENT], other[:PLACE]], axis=0), "depth", facing)
     rho_own, pair = call(
-        middle_second_kernel, "middle_second", (WIDE, CELLS * NT * PAIR), frame, other, beyond, left, send, last, right
+        middle_second_kernel, "middle_second", (WIDE, CELLS * NT * PAIR), frame, other, beyond, right, left, first, send
     )
     rho_other = swapped(rho_own)
-    (rho_outer,) = call(outer_second_kernel, "outer_second", (WIDE,), frame, beyond, left, outer, rho_own)
+    (rho_outer,) = call(outer_second_kernel, "outer_second", (WIDE,), frame, beyond, right, outer, rho_own)
     pos, vel, rho, part = call(
         force_second_kernel,
         "force_second",
         (2 * CELLS, 2 * CELLS, CELLS, S),
-        iface_dest.reshape(CELLS, S), iface_shell.reshape(CELLS, S),
-        frame, other, beyond, rho_outer, rho_own, rho_other, send, last, pair,
+        home, frame, other, beyond, rho_outer, rho_own, rho_other, first, send, pair,
     )
 
     arrived = lax.all_to_all(part, ("depth", "azim"), split_axis=0, concat_axis=0, tiled=True)
-    stress_out = pl.pallas_call(
+    stress_out, pos, vel, rho = pl.pallas_call(
         soil_kernel,
-        out_shape=jax.ShapeDtypeStruct(soil_stress.shape, jnp.float32),
-        in_specs=[VM] * 4,
-        out_specs=VM,
+        out_shape=(
+            jax.ShapeDtypeStruct(soil_stress.shape, jnp.float32), rows_of(2 * CELLS), rows_of(2 * CELLS), rows_of(CELLS)
+        ),
+        in_specs=[VM] * 5,
+        out_specs=(VM, VM, VM, VM),
         name="soil",
-    )(held(arrived), held(soil_stress), held(soil_rate), held(soil_couple))
+    )(*[held(a) for a in (arrived, soil, pos, vel, rho)])
     return (
         pos.reshape(fluid_pos.shape),
         vel.reshape(fluid_vel.shape),

time: 57.7 us -> 56.1 us (0.972)
  blocking collectives: 0 us -> 20.6 us
  waiting for transfers between devices: 24.1 us -> 14.1 us
  starting transfers between devices: 23.8 us -> 14.7 us
  local copies, waits for them, and re-layouts: 2.5 us -> 0.02 us
  Pallas kernels: 6.21 us -> 5.57 us
    all_to_all x0 -> x1, blocking collectives: none -> 20.6 us  [local(): lax.all_to_all(part, ('depth', 'azim'), split_axis=0, concat_axis=0, tile...]
    all_to_all x1 -> x0, waiting for transfers between devices: 8.03 us -> none  [local(): lax.all_to_all(part, ('depth', 'azim'), split_axis=0, concat_axis=0, tile...]
    all_to_all x1 -> x0, starting transfers between devices: 7.82 us -> none  [local(): lax.all_to_all(part, ('depth', 'azim'), split_axis=0, concat_axis=0, tile...]
    unnamed x16 -> x3, local copies, waits for them, and re-layouts: 2.48 us -> 0.01 us
    ppermute x3, starting transfers between devices: 9.64 us -> 7.26 us  [the longest x1 3.34 us: local(): lax.ppermute(jnp.concatenate([frame[:SENT], other[:PLACE], left[HALF:], f...]
    ppermute x3, waiting for transfers between devices: 11.8 us -> 9.9 us  [the longest x1 6.06 us: local(): left = lax.ppermute(send, 'azim', toward_right)]
    ppermute x4, starting transfers between devices: 2.51 us -> 3.19 us  [swapped(): return lax.ppermute(a, 'depth', pairs)]
    pallas_call x6, Pallas kernels: 4.58 us -> 3.91 us  [call(): pl.pallas_call(kernel, out_shape=tuple((kept(n) for n in shapes)), in_spe...]
  transfers between devices with their start and end apart: 9 -> 8, of which waited for: 9 -> 8; matrix products, arithmetic and copies ran while one was open for 3% -> 0% of each run, Pallas kernels for 2% -> 2%
where the time goes in v5:
time: 56.1 us; the launch traced here: 55.9 us
  blocking collectives  20.6 us (37%)
  starting transfers between devices  14.7 us (26%)
  waiting for transfers between devices  14.1 us (25%)
  Pallas kernels  5.57 us (10%)
  between operations  0.75 us (1%)
    all_to_all x1, blocking collectives, local(): lax.all_to_all(part, ('depth', 'azim'), split_axis=0, concat_axis=0, tile...  20.6 us
    ppermute x1, waiting for transfers between devices, local(): left = lax.ppermute(send, 'azim', toward_right)  6.06 us
    ppermute x1, starting transfers between devices, local(): lax.ppermute(jnp.concatenate([frame[:SENT], other[:PLACE]], axis=0), 'dep...  4.26 us
    pallas_call x6, Pallas kernels, call(): pl.pallas_call(kernel, out_shape=tuple((kept(n) for n in shapes)), in_spe...  3.91 us
    ppermute x1, starting transfers between devices, local(): lax.ppermute(jnp.concatenate([frame[:SENT], other[:PLACE], left[HALF:], f...  3.34 us
    ppermute x4, starting transfers between devices, swapped(): return lax.ppermute(a, 'depth', pairs)  3.19 us
    ppermute x1, waiting for transfers between devices, local(): lax.ppermute(jnp.concatenate([frame[:SENT], other[:PLACE], left[HALF:], f...  2.78 us
    ppermute x4, waiting for transfers between devices, swapped(): return lax.ppermute(a, 'depth', pairs)  2.68 us
  transfers between devices with their start and end apart: 8, of which 8 were waited for; matrix products, arithmetic and copies ran while one was open for 0% of the time, Pallas kernels for 2%

profile of v5, /device:TPU:1, one launch (start us, length us, event | category | flops | bytes accessed | tf_op | source)
XLA Modules:
  0.0 55.9 jit_solution(12661448983150246012)
XLA Ops:
  0.6 0.9 %pack.1 = (f32[96,128]{1,0:T(8,128)S(1)}, f32[24,128]{1,0:T(8,128)S(1)}, s32[8,128]{1,0:T(8,128)S(1)}, f32[10,16,128]{2,1,0:T(8,128)S(1)}) custom-call(s32[1,4]{1,0:T(1,128)} %count.1, f32[8,128]{1,0:T(8,128)} %bitcast.42, f32[8,128]{1,0:T(8,128)} %bitcast.43, f32[4,128]{1,0:T(4,128)} %bitcast.44, s32[96,128]{1,0:T(8,128)} %bitcast.41, s32[4,128]{1,0:T(4,128)} %bitcast.45, ...), custom_call_target="tpu_custom_call" | custom-call | tf_op jit(solution)/shard_map/pack/pallas_call | solution.py:318
  1.5 2.1 %collective-permute-start = (f32[96,128]{1,0:T(8,128)S(1)}, f32[96,128]{1,0:T(8,128)S(1)}, u32[]{:S(2)}, u32[]{:S(2)}) collective-permute-start(f32[96,128]{1,0:T(8,128)S(1)} %get-tuple-element.21.send), channel_id=1, source_target_pairs={{0,1},{1,2},{2,3},{3,4},{4,5},{5,6},{6,7},{7,0},{8,9},{9,10},{10,1... | collective-permute-start | bytes 147464 | tf_op jit(solution)/shard_map/ppermute | solution.py:341
  3.7 6.1 %collective-permute-done.left = f32[96,128]{1,0:T(8,128)S(1)} collective-permute-done((f32[96,128]{1,0:T(8,128)S(1)}, f32[96,128]{1,0:T(8,128)S(1)}, u32[]{:S(2)}, u32[]{:S(2)}) %collective-permute-start) | collective-permute-done | bytes 49184 | tf_op jit(solution)/shard_map/ppermute | solution.py:341
  9.7 1.6 %collective-permute-start.1 = (f32[40,128]{1,0:T(8,128)S(1)}, f32[40,128]{1,0:T(8,128)S(1)}, u32[]{:S(2)}, u32[]{:S(2)}) collective-permute-start(f32[40,128]{1,0:T(8,128)S(1)} %get-tuple-element.45), channel_id=1, source_target_pairs={{0,8},{8,0},{16,24},{24,16},{32,40},{40,32},{48,56},{56,48},{64,72... | collective-permute-start | bytes 61448 | tf_op jit(solution)/shard_map/ppermute | solution.py:316
  11.4 0.8 %collective-permute-done.1.other = f32[40,128]{1,0:T(8,128)S(1)} collective-permute-done((f32[40,128]{1,0:T(8,128)S(1)}, f32[40,128]{1,0:T(8,128)S(1)}, u32[]{:S(2)}, u32[]{:S(2)}) %collective-permute-start.1) | collective-permute-done | bytes 20512 | tf_op jit(solution)/shard_map/ppermute | solution.py:316
  12.2 3.3 %collective-permute-start.2 = (f32[232,128]{1,0:T(8,128)S(1)}, f32[232,128]{1,0:T(8,128)S(1)}, u32[]{:S(2)}, u32[]{:S(2)}) collective-permute-start(f32[232,128]{1,0:T(8,128)S(1)} %slice_dynamic-update-slice_fusion.1), channel_id=1, source_target_pairs={{8,16},{16,8},{24,32},{32,24},{40,48},{48,40},{56,64},{64,56},{72,... | collective-permute-start | bytes 356360 | tf_op jit(solution)/shard_map/ppermute | solution.py:344
  15.6 2.8 %collective-permute-done.2.outer.before = f32[232,128]{1,0:T(8,128)S(1)} collective-permute-done((f32[232,128]{1,0:T(8,128)S(1)}, f32[232,128]{1,0:T(8,128)S(1)}, u32[]{:S(2)}, u32[]{:S(2)}) %collective-permute-start.2) | collective-permute-done | bytes 118816 | tf_op jit(solution)/shard_map/ppermute | solution.py:344
  18.4 0.7 %middle_first.1 = (f32[8,128]{1,0:T(8,128)S(1)}, f32[480,128]{1,0:T(8,128)S(1)}) custom-call(s32[1]{0:T(128)} %bitcast.parity, f32[48,128]{1,0:T(8,128)S(1)} %fusion.1.frame, f32[40,128]{1,0:T(8,128)S(1)} %collective-permute-done.1.other, f32[232,128]{1,0:T(8,128)S(1)} %collective-permute-done.2.outer.before, f32[96,128]{1,0:T(8,128)S(1)} %collective-permute-done.left, ...), custom_call_target="tpu_custom_call" | custom-call | tf_op jit(solution)/shard_map/middle_first/pallas_call | solution.py:303
  19.0 0.1 collective-permute-start.3
  19.1 0.7 %outer_first.1.rho_outer = f32[8,128]{1,0:T(8,128)S(1)} custom-call(s32[1]{0:T(128)} %bitcast.parity, f32[48,128]{1,0:T(8,128)S(1)} %fusion.1.frame, f32[232,128]{1,0:T(8,128)S(1)} %collective-permute-done.2.outer.before, f32[8,128]{1,0:T(8,128)S(1)} %get-tuple-element.23.after.rho_own), custom_call_target="tpu_custom_call" | custom-call | tf_op jit(solution)/shard_map/outer_first/pallas_call | solution.py:303
  19.8 0.5 collective-permute-done.3.rho_other
  20.3 0.5 force_first.1
  20.8 1.8 %collective-permute-start.4 = (f32[72,128]{1,0:T(8,128)S(1)}, f32[72,128]{1,0:T(8,128)S(1)}, u32[]{:S(2)}, u32[]{:S(2)}) collective-permute-start(f32[72,128]{1,0:T(8,128)S(1)} %force_first.1), channel_id=1, source_target_pairs={{0,7},{1,0},{2,1},{3,2},{4,3},{5,4},{6,5},{7,6},{8,15},{9,8},{10,9... | collective-permute-start | bytes 110600 | tf_op jit(solution)/shard_map/ppermute | solution.py:359
  22.6 1.1 %collective-permute-done.4.right = f32[72,128]{1,0:T(8,128)S(1)} collective-permute-done((f32[72,128]{1,0:T(8,128)S(1)}, f32[72,128]{1,0:T(8,128)S(1)}, u32[]{:S(2)}, u32[]{:S(2)}) %collective-permute-start.4) | collective-permute-done | bytes 36896 | tf_op jit(solution)/shard_map/ppermute | solution.py:359
  23.7 1.4 %collective-permute-start.5 = (f32[40,128]{1,0:T(8,128)S(1)}, f32[40,128]{1,0:T(8,128)S(1)}, u32[]{:S(2)}, u32[]{:S(2)}) collective-permute-start(f32[40,128]{1,0:T(8,128)S(1)} %fusion.3), channel_id=1, source_target_pairs={{0,8},{8,0},{16,24},{24,16},{32,40},{40,32},{48,56},{56,48},{64,72... | collective-permute-start | bytes 61448 | tf_op jit(solution)/shard_map/ppermute | solution.py:316
  25.1 0.8 %collective-permute-done.5.other = f32[40,128]{1,0:T(8,128)S(1)} collective-permute-done((f32[40,128]{1,0:T(8,128)S(1)}, f32[40,128]{1,0:T(8,128)S(1)}, u32[]{:S(2)}, u32[]{:S(2)}) %collective-permute-start.5) | collective-permute-done | bytes 20512 | tf_op jit(solution)/shard_map/ppermute | solution.py:316
  25.9 4.3 %collective-permute-start.6 = (f32[64,128]{1,0:T(8,128)S(1)}, f32[64,128]{1,0:T(8,128)S(1)}, u32[]{:S(2)}, u32[]{:S(2)}) collective-permute-start(f32[64,128]{1,0:T(8,128)S(1)} %pad_maximum_fusion), channel_id=1, source_target_pairs={{8,16},{16,8},{24,32},{32,24},{40,48},{48,40},{56,64},{64,56},{72,... | collective-permute-start | bytes 98312 | tf_op jit(solution)/shard_map/ppermute | solution.py:362
  30.2 1.6 %collective-permute-done.6.outer = f32[64,128]{1,0:T(8,128)S(1)} collective-permute-done((f32[64,128]{1,0:T(8,128)S(1)}, f32[64,128]{1,0:T(8,128)S(1)}, u32[]{:S(2)}, u32[]{:S(2)}) %collective-permute-start.6) | collective-permute-done | bytes 32800 | tf_op jit(solution)/shard_map/ppermute | solution.py:362
  31.8 0.6 %middle_second.1 = (f32[8,128]{1,0:T(8,128)S(1)}, f32[480,128]{1,0:T(8,128)S(1)}) custom-call(s32[1]{0:T(128)} %bitcast.parity, f32[48,128]{1,0:T(8,128)S(1)} %fusion.frame, f32[40,128]{1,0:T(8,128)S(1)} %collective-permute-done.5.other, f32[64,128]{1,0:T(8,128)S(1)} %collective-permute-done.6.outer, f32[72,128]{1,0:T(8,128)S(1)} %collective-permute-done.4.right, ...), custom_call_target="tpu_custom_call" | custom-call | tf_op jit(solution)/shard_map/middle_second/pallas_call | solution.py:303
  32.4 0.1 collective-permute-start.7
  32.5 0.7 %outer_second.1.rho_outer = f32[8,128]{1,0:T(8,128)S(1)} custom-call(s32[1]{0:T(128)} %bitcast.parity, f32[48,128]{1,0:T(8,128)S(1)} %fusion.frame, f32[64,128]{1,0:T(8,128)S(1)} %collective-permute-done.6.outer, f32[72,128]{1,0:T(8,128)S(1)} %collective-permute-done.4.right, f32[232,128]{1,0:T(8,128)S(1)} %collective-permute-done.2.outer.before, ...), custom_call_target="tpu_custom_call" | custom-call | tf_op jit(solution)/shard_map/outer_second/pallas_call | solution.py:303
  33.2 0.5 collective-permute-done.7.rho_other
  33.7 0.8 %force_second.1 = (f32[8,128]{1,0:T(8,128)S(1)}, f32[8,128]{1,0:T(8,128)S(1)}, f32[4,128]{1,0:T(4,128)S(1)}, f32[128,128]{1,0:T(8,128)S(1)}) custom-call(s32[1]{0:T(128)} %bitcast.parity, s32[8,128]{1,0:T(8,128)S(1)} %get-tuple-element.20.home, f32[48,128]{1,0:T(8,128)S(1)} %fusion.frame, f32[40,128]{1,0:T(8,128)S(1)} %collective-permute-done.5.other, ...), custom_call_target="tpu_custom_call" | custom-call | tf_op jit(solution)/shard_map/force_second/pallas_call | solution.py:303
  34.5 20.6 %all_to_all.11 = f32[128,1,128]{2,1,0:T(1,128)S(1)} all-to-all(f32[128,1,128]{2,1,0:T(1,128)S(1)} %bitcast.32), channel_id=1, replica_groups=mesh['depth'=16,'azim'=8] {'depth','azim'}, dimensions={0} | all-to-all | bytes 131072 | tf_op jit(solution)/shard_map/all_to_all | solution.py:375
  55.1 0.8 %soil.1 = (f32[4,16,128]{2,1,0:T(8,128)}, f32[8,128]{1,0:T(8,128)}, f32[8,128]{1,0:T(8,128)}, f32[4,128]{1,0:T(4,128)}) custom-call(f32[128,128]{1,0:T(8,128)S(1)} %bitcast.31, f32[10,16,128]{2,1,0:T(8,128)S(1)} %get-tuple-element.28.soil, f32[8,128]{1,0:T(8,128)S(1)} %get-tuple-element.29.pos, f32[8,128]{1,0:T(8,128)S(1)} %get-tuple-element.30.vel, ...), custom_call_target="tpu_custom_call" | custom-call | tf_op jit(solution)/shard_map/soil/pallas_call | solution.py:376
  (14 shorter events, 0.1 us)
Async XLA Ops:
  1.5 8.2 %collective-permute-start = (f32[96,128]{1,0:T(8,128)S(1)}, f32[96,128]{1,0:T(8,128)S(1)}, u32[]{:S(2)}, u32[]{:S(2)}) collective-permute-start(f32[96,128]{1,0:T(8,128)S(1)} %get-tuple-element.21.send), channel_id=1, source_target_pairs={{0,1},{1,2},{2,3},{3,4},{4,5},{5,6},{6,7},{7,0},{8,9},{9,10},{10,1... | collective-permute-start | bytes 147464 | tf_op jit(solution)/shard_map/ppermute | solution.py:341
  9.7 2.5 %collective-permute-start.1 = (f32[40,128]{1,0:T(8,128)S(1)}, f32[40,128]{1,0:T(8,128)S(1)}, u32[]{:S(2)}, u32[]{:S(2)}) collective-permute-start(f32[40,128]{1,0:T(8,128)S(1)} %get-tuple-element.45), channel_id=1, source_target_pairs={{0,8},{8,0},{16,24},{24,16},{32,40},{40,32},{48,56},{56,48},{64,72... | collective-permute-start | bytes 61448 | tf_op jit(solution)/shard_map/ppermute | solution.py:316
  12.2 6.2 %collective-permute-start.2 = (f32[232,128]{1,0:T(8,128)S(1)}, f32[232,128]{1,0:T(8,128)S(1)}, u32[]{:S(2)}, u32[]{:S(2)}) collective-permute-start(f32[232,128]{1,0:T(8,128)S(1)} %slice_dynamic-update-slice_fusion.1), channel_id=1, source_target_pairs={{8,16},{16,8},{24,32},{32,24},{40,48},{48,40},{56,64},{64,56},{72,... | collective-permute-start | bytes 356360 | tf_op jit(solution)/shard_map/ppermute | solution.py:344
  19.0 1.2 %collective-permute-start.3 = (f32[8,128]{1,0:T(8,128)S(1)}, f32[8,128]{1,0:T(8,128)S(1)}, u32[]{:S(2)}, u32[]{:S(2)}) collective-permute-start(f32[8,128]{1,0:T(8,128)S(1)} %get-tuple-element.23.after.rho_own), channel_id=1, source_target_pairs={{0,8},{8,0},{16,24},{24,16},{32,40},{40,32},{48,56},{56,48},{64,72... | collective-permute-start | bytes 12296 | tf_op jit(solution)/shard_map/ppermute | solution.py:316
  20.8 2.9 %collective-permute-start.4 = (f32[72,128]{1,0:T(8,128)S(1)}, f32[72,128]{1,0:T(8,128)S(1)}, u32[]{:S(2)}, u32[]{:S(2)}) collective-permute-start(f32[72,128]{1,0:T(8,128)S(1)} %force_first.1), channel_id=1, source_target_pairs={{0,7},{1,0},{2,1},{3,2},{4,3},{5,4},{6,5},{7,6},{8,15},{9,8},{10,9... | collective-permute-start | bytes 110600 | tf_op jit(solution)/shard_map/ppermute | solution.py:359
  23.7 2.2 %collective-permute-start.5 = (f32[40,128]{1,0:T(8,128)S(1)}, f32[40,128]{1,0:T(8,128)S(1)}, u32[]{:S(2)}, u32[]{:S(2)}) collective-permute-start(f32[40,128]{1,0:T(8,128)S(1)} %fusion.3), channel_id=1, source_target_pairs={{0,8},{8,0},{16,24},{24,16},{32,40},{40,32},{48,56},{56,48},{64,72... | collective-permute-start | bytes 61448 | tf_op jit(solution)/shard_map/ppermute | solution.py:316
  25.9 5.8 %collective-permute-start.6 = (f32[64,128]{1,0:T(8,128)S(1)}, f32[64,128]{1,0:T(8,128)S(1)}, u32[]{:S(2)}, u32[]{:S(2)}) collective-permute-start(f32[64,128]{1,0:T(8,128)S(1)} %pad_maximum_fusion), channel_id=1, source_target_pairs={{8,16},{16,8},{24,32},{32,24},{40,48},{48,40},{56,64},{64,56},{72,... | collective-permute-start | bytes 98312 | tf_op jit(solution)/shard_map/ppermute | solution.py:362
  32.4 1.2 %collective-permute-start.7 = (f32[8,128]{1,0:T(8,128)S(1)}, f32[8,128]{1,0:T(8,128)S(1)}, u32[]{:S(2)}, u32[]{:S(2)}) collective-permute-start(f32[8,128]{1,0:T(8,128)S(1)} %get-tuple-element.25.after.rho_own), channel_id=1, source_target_pairs={{0,8},{8,0},{16,24},{24,16},{32,40},{40,32},{48,56},{56,48},{64,72... | collective-permute-start | bytes 12296 | tf_op jit(solution)/shard_map/ppermute | solution.py:316

commit v6 on v5

--- a/solution.py
+++ b/solution.py
@@ -29,7 +29,7 @@
 NEAR = [(dr, dc) for dr in (-1, 0, 1) for dc in (-1, 0, 1)]
 
 
-def pack_kernel(count, pos, vel, mass, nb, dest, shell, stress, rate, couple, out, first, home, soil):
+def pack_kernel(count, pos, vel, mass, nb, dest, shell, stress, rate, couple, out, half, first, home, soil):
     soil[0:4] = stress[...]
     soil[4:7] = rate[...]
     soil[7:10] = couple[...]
@@ -38,11 +38,15 @@
     lane = lax.broadcasted_iota(jnp.int32, (1, S), 1)
     out[0 : 2 * CELLS, :] = pos[...]
     out[PVX * CELLS : (PVX + 2) * CELLS, :] = vel[...]
+    half[0 : 2 * CELLS, :] = pos[...]
+    half[PVX * CELLS : (PVX + 2) * CELLS, :] = vel[...]
     for c in range(CELLS):
         live = (lane < count[0, c]).astype(jnp.float32)
         out[PM * CELLS + c : PM * CELLS + c + 1, :] = mass[c : c + 1, :] * live
         out[PL * CELLS + c : PL * CELLS + c + 1, :] = live
         codes = nb[pl.ds(c, NB, stride=CELLS), :].astype(jnp.float32)
+        half[PM * CELLS + c : PM * CELLS + c + 1, :] = mass[c : c + 1, :] * live
+        half[PL * CELLS + c : PL * CELLS + c + 1, :] = live
         if c:
             out[HALF + NB * (c - 1) : HALF + NB * c, :] = codes
         else:
@@ -168,7 +172,7 @@
     density(parity, {-1: (outer, SENT), 0: (outer, 0), 1: (frame, 0)}, lists, rho, None)
 
 
-def force_first_kernel(parity, frame, other, outer, rho_outer, rho_own, rho_other, left, first, send, pair, out):
+def force_first_kernel(parity, frame, other, outer, rho_outer, rho_own, rho_other, left, first, send, pair, out, half):
     numbers = numbers_of(parity)
     lists = [(left, HALF + NB), (left, HALF + 2 * NB), (first, 0), (send, HALF)]
     for c in range(CELLS):
@@ -177,6 +181,7 @@
         )
         for k, v in enumerate(fields):
             out[k * CELLS + c : k * CELLS + c + 1, :] = v
+            half[k * CELLS + c : k * CELLS + c + 1, :] = v
     out[HALF : HALF + NB, :] = outer[OUTER + 3 * NB : OUTER + 4 * NB, :]
     out[HALF + NB : HALF + 2 * NB, :] = first[...]
 
@@ -312,19 +317,25 @@
         halves = [a[:HALF].reshape(6, CELLS, S) for a in (first, second)]
         return jnp.concatenate(halves, axis=1).reshape(6 * WIDE, S)
 
+    def crossing(step):
+        return [
+            (r * n_azim + c, (r ^ 1) * n_azim + (c + step) % n_azim) for r in range(n_depth) for c in range(n_azim)
+        ]
+
     def swapped(a):
         return lax.ppermute(a, "depth", pairs)
 
-    send, first, home, soil = pl.pallas_call(
+    send, half, first, home, soil = pl.pallas_call(
         pack_kernel,
         out_shape=(
             kept(HALF + 3 * NB),
+            kept(HALF),
             kept(NB),
             pltpu.VMEM((2 * CELLS, S), jnp.int32),
             pltpu.VMEM((10,) + soil_stress.shape[1:], jnp.float32),
         ),
         in_specs=[SM] + [VM] * 9,
-        out_specs=(VM, VM, VM, VM),
+        out_specs=(VM,) * 5,
         name="pack",
     )(
         cell_count,
@@ -339,8 +350,11 @@
         soil_couple,
     )
     left = lax.ppermute(send, "azim", toward_right)
+    across = lax.ppermute(half, ("depth", "azim"), crossing(1))
+    beside = swapped(half)
+    left, across, beside = lax.optimization_barrier((left, across, beside))
     frame = merged(left, send)
-    other = swapped(frame[:SENT])
+    other = merged(across, beside)
     outer = lax.ppermute(
         jnp.concatenate([frame[:SENT], other[:PLACE], left[HALF:], first, send[HALF:]], axis=0), "depth", facing
     )
@@ -349,16 +363,19 @@
     )
     rho_other = swapped(rho_own)
     (rho_outer,) = call(outer_first_kernel, "outer_first", (WIDE,), frame, outer, rho_own)
-    (mid,) = call(
+    mid, half = call(
         force_first_kernel,
         "force_first",
-        (HALF + 2 * NB,),
+        (HALF + 2 * NB, HALF),
         frame, other, outer, rho_outer, rho_own, rho_other, left, first, send, pair,
     )
 
     right = lax.ppermute(mid, "azim", toward_left)
+    across = lax.ppermute(half, ("depth", "azim"), crossing(-1))
+    beside = swapped(half)
+    right, across, beside = lax.optimization_barrier((right, across, beside))
     frame = merged(mid, right)
-    other = swapped(frame[:SENT])
+    other = merged(beside, across)
     beyond = lax.ppermute(jnp.concatenate([frame[:SENT], other[:PLACE]], axis=0), "depth", facing)
     rho_own, pair = call(
         middle_second_kernel, "middle_second", (WIDE, CELLS * NT * PAIR), frame, other, beyond, right, left, first, send

time: 56.1 us -> 54.4 us (0.970)
  waiting for transfers between devices: 14.1 us -> 12.9 us
    ppermute x0 -> x2, waiting for transfers between devices: none -> 7.62 us  [the longest x1 5.63 us: local(): across = lax.ppermute(half, ('depth', 'azim'), crossing(1))]
    ppermute x1, waiting for transfers between devices: 6.06 us -> 0.01 us  [local(): left = lax.ppermute(send, 'azim', toward_right)]
    ppermute x0 -> x2, starting transfers between devices: none -> 2.22 us  [the longest x1 1.12 us: local(): across = lax.ppermute(half, ('depth', 'azim'), crossing(-1))]
    ppermute x4, waiting for transfers between devices: 2.68 us -> 0.99 us  [swapped(): return lax.ppermute(a, 'depth', pairs)]
    ppermute x4, starting transfers between devices: 3.19 us -> 1.57 us  [swapped(): return lax.ppermute(a, 'depth', pairs)]
    ppermute x1, waiting for transfers between devices: 1.06 us -> 0.01 us  [local(): right = lax.ppermute(mid, 'azim', toward_left)]
  transfers between devices with their start and end apart: 8 -> 10, of which waited for: 8 -> 6; matrix products, arithmetic and copies ran while one was open for 0% -> 0% of each run, Pallas kernels for 2% -> 2%
where the time goes in v6:
time: 54.4 us; the launch traced here: 54.1 us
  blocking collectives  20.4 us (38%)
  starting transfers between devices  14.4 us (26%)
  waiting for transfers between devices  12.9 us (24%)
  Pallas kernels  5.57 us (10%)
  between operations  0.8 us (1%)
    all_to_all x1, blocking collectives, local(): lax.all_to_all(part, ('depth', 'azim'), split_axis=0, concat_axis=0, tile...  20.4 us
    ppermute x1, waiting for transfers between devices, local(): across = lax.ppermute(half, ('depth', 'azim'), crossing(1))  5.63 us
    pallas_call x6, Pallas kernels, call(): pl.pallas_call(kernel, out_shape=tuple((kept(n) for n in shapes)), in_spe...  3.91 us
    ppermute x1, starting transfers between devices, local(): lax.ppermute(jnp.concatenate([frame[:SENT], other[:PLACE]], axis=0), 'dep...  3.75 us
    ppermute x1, starting transfers between devices, local(): lax.ppermute(jnp.concatenate([frame[:SENT], other[:PLACE], left[HALF:], f...  3.43 us
    ppermute x1, waiting for transfers between devices, local(): lax.ppermute(jnp.concatenate([frame[:SENT], other[:PLACE], left[HALF:], f...  2.68 us
    ppermute x1, starting transfers between devices, local(): left = lax.ppermute(send, 'azim', toward_right)  2.11 us
    ppermute x1, waiting for transfers between devices, local(): across = lax.ppermute(half, ('depth', 'azim'), crossing(-1))  1.99 us
  transfers between devices with their start and end apart: 10, of which 6 were waited for; matrix products, arithmetic and copies ran while one was open for 0% of the time, Pallas kernels for 2%

profile of v6, /device:TPU:1, one launch (start us, length us, event | category | flops | bytes accessed | tf_op | source)
XLA Modules:
  0.0 54.1 jit_solution(2459681076873587037)
XLA Ops:
  0.6 0.9 %pack.1 = (f32[96,128]{1,0:T(8,128)S(1)}, f32[24,128]{1,0:T(8,128)S(1)}, f32[24,128]{1,0:T(8,128)S(1)}, s32[8,128]{1,0:T(8,128)S(1)}, f32[10,16,128]{2,1,0:T(8,128)S(1)}) custom-call(s32[1,4]{1,0:T(1,128)} %count.1, f32[8,128]{1,0:T(8,128)} %bitcast.65, f32[8,128]{1,0:T(8,128)} %bitcast.66, f32[4,128]{1,0:T(4,128)} %bitcast.67, s32[96,128]{1,0:T(8,128)} %bitcast.60, ...), custom_call_target="tpu_custom_call" | custom-call | tf_op jit(solution)/shard_map/pack/pallas_call | solution.py:328
  1.5 2.1 %collective-permute-start = (f32[96,128]{1,0:T(8,128)S(1)}, f32[96,128]{1,0:T(8,128)S(1)}, u32[]{:S(2)}, u32[]{:S(2)}) collective-permute-start(f32[96,128]{1,0:T(8,128)S(1)} %get-tuple-element.30.send), channel_id=1, source_target_pairs={{0,1},{1,2},{2,3},{3,4},{4,5},{5,6},{6,7},{7,0},{8,9},{9,10},{10,1... | collective-permute-start | bytes 147464 | tf_op jit(solution)/shard_map/ppermute | solution.py:352
  3.7 1.0 %collective-permute-start.2 = (f32[24,128]{1,0:T(8,128)S(1)}, f32[24,128]{1,0:T(8,128)S(1)}, u32[]{:S(2)}, u32[]{:S(2)}) collective-permute-start(f32[24,128]{1,0:T(8,128)S(1)} %get-tuple-element.31), channel_id=1, source_target_pairs={{0,8},{8,0},{16,24},{24,16},{32,40},{40,32},{48,56},{56,48},{64,72... | collective-permute-start | bytes 36872 | tf_op jit(solution)/shard_map/ppermute | solution.py:326
  4.6 1.1 %collective-permute-start.1 = (f32[24,128]{1,0:T(8,128)S(1)}, f32[24,128]{1,0:T(8,128)S(1)}, u32[]{:S(2)}, u32[]{:S(2)}) collective-permute-start(f32[24,128]{1,0:T(8,128)S(1)} %get-tuple-element.31), channel_id=1, source_target_pairs={{0,9},{1,10},{2,11},{3,12},{4,13},{5,14},{6,15},{7,8},{8,1},{9,2},... | collective-permute-start | bytes 36872 | tf_op jit(solution)/shard_map/ppermute | solution.py:353
  5.7 0.0 collective-permute-done.2
  5.7 5.6 %collective-permute-done.1 = f32[24,128]{1,0:T(8,128)S(1)} collective-permute-done((f32[24,128]{1,0:T(8,128)S(1)}, f32[24,128]{1,0:T(8,128)S(1)}, u32[]{:S(2)}, u32[]{:S(2)}) %collective-permute-start.1) | collective-permute-done | bytes 12320 | tf_op jit(solution)/shard_map/ppermute | solution.py:353
  11.3 0.0 collective-permute-done.left
  11.4 3.4 %collective-permute-start.3 = (f32[232,128]{1,0:T(8,128)S(1)}, f32[232,128]{1,0:T(8,128)S(1)}, u32[]{:S(2)}, u32[]{:S(2)}) collective-permute-start(f32[232,128]{1,0:T(8,128)S(1)} %slice_dynamic-update-slice_fusion), channel_id=1, source_target_pairs={{8,16},{16,8},{24,32},{32,24},{40,48},{48,40},{56,64},{64,56},{72,... | collective-permute-start | bytes 356360 | tf_op jit(solution)/shard_map/ppermute | solution.py:358
  14.9 2.7 %collective-permute-done.3.outer.before = f32[232,128]{1,0:T(8,128)S(1)} collective-permute-done((f32[232,128]{1,0:T(8,128)S(1)}, f32[232,128]{1,0:T(8,128)S(1)}, u32[]{:S(2)}, u32[]{:S(2)}) %collective-permute-start.3) | collective-permute-done | bytes 118816 | tf_op jit(solution)/shard_map/ppermute | solution.py:358
  17.6 0.7 %middle_first.1 = (f32[8,128]{1,0:T(8,128)S(1)}, f32[480,128]{1,0:T(8,128)S(1)}) custom-call(s32[1]{0:T(128)} %bitcast.parity, f32[48,128]{1,0:T(8,128)S(1)} %get-tuple-element.63.frame, f32[48,128]{1,0:T(8,128)S(1)} %get-tuple-element.62.other, f32[232,128]{1,0:T(8,128)S(1)} %collective-permute-done.3.outer.before, ...), custom_call_target="tpu_custom_call" | custom-call | tf_op jit(solution)/shard_map/middle_first/pallas_call | solution.py:308
  18.2 0.1 collective-permute-start.4
  18.3 0.7 %outer_first.1.rho_outer = f32[8,128]{1,0:T(8,128)S(1)} custom-call(s32[1]{0:T(128)} %bitcast.parity, f32[48,128]{1,0:T(8,128)S(1)} %get-tuple-element.63.frame, f32[232,128]{1,0:T(8,128)S(1)} %collective-permute-done.3.outer.before, f32[8,128]{1,0:T(8,128)S(1)} %get-tuple-element.36.after.rho_own), custom_call_target="tpu_custom_call" | custom-call | tf_op jit(solution)/shard_map/outer_first/pallas_call | solution.py:308
  19.0 0.5 collective-permute-done.4.rho_other
  19.5 0.5 force_first.1
  20.0 1.3 %collective-permute-start.5 = (f32[72,128]{1,0:T(8,128)S(1)}, f32[72,128]{1,0:T(8,128)S(1)}, u32[]{:S(2)}, u32[]{:S(2)}) collective-permute-start(f32[72,128]{1,0:T(8,128)S(1)} %get-tuple-element.38), channel_id=1, source_target_pairs={{0,7},{1,0},{2,1},{3,2},{4,3},{5,4},{6,5},{7,6},{8,15},{9,8},{10,9... | collective-permute-start | bytes 110600 | tf_op jit(solution)/shard_map/ppermute | solution.py:373
  21.3 0.4 collective-permute-start.7
  21.7 1.1 %collective-permute-start.6 = (f32[24,128]{1,0:T(8,128)S(1)}, f32[24,128]{1,0:T(8,128)S(1)}, u32[]{:S(2)}, u32[]{:S(2)}) collective-permute-start(f32[24,128]{1,0:T(8,128)S(1)} %get-tuple-element.39), channel_id=1, source_target_pairs={{0,15},{1,8},{2,9},{3,10},{4,11},{5,12},{6,13},{7,14},{8,7},{9,0},... | collective-permute-start | bytes 36872 | tf_op jit(solution)/shard_map/ppermute | solution.py:374
  22.9 0.0 collective-permute-done.7
  22.9 2.0 %collective-permute-done.6 = f32[24,128]{1,0:T(8,128)S(1)} collective-permute-done((f32[24,128]{1,0:T(8,128)S(1)}, f32[24,128]{1,0:T(8,128)S(1)}, u32[]{:S(2)}, u32[]{:S(2)}) %collective-permute-start.6) | collective-permute-done | bytes 12320 | tf_op jit(solution)/shard_map/ppermute | solution.py:374
  24.9 0.0 collective-permute-done.5.right
  24.9 3.8 %collective-permute-start.8 = (f32[64,128]{1,0:T(8,128)S(1)}, f32[64,128]{1,0:T(8,128)S(1)}, u32[]{:S(2)}, u32[]{:S(2)}) collective-permute-start(f32[64,128]{1,0:T(8,128)S(1)} %pad_maximum_fusion), channel_id=1, source_target_pairs={{8,16},{16,8},{24,32},{32,24},{40,48},{48,40},{56,64},{64,56},{72,... | collective-permute-start | bytes 98312 | tf_op jit(solution)/shard_map/ppermute | solution.py:379
  28.7 1.6 %collective-permute-done.8.outer = f32[64,128]{1,0:T(8,128)S(1)} collective-permute-done((f32[64,128]{1,0:T(8,128)S(1)}, f32[64,128]{1,0:T(8,128)S(1)}, u32[]{:S(2)}, u32[]{:S(2)}) %collective-permute-start.8) | collective-permute-done | bytes 32800 | tf_op jit(solution)/shard_map/ppermute | solution.py:379
  30.3 0.6 %middle_second.1 = (f32[8,128]{1,0:T(8,128)S(1)}, f32[480,128]{1,0:T(8,128)S(1)}) custom-call(s32[1]{0:T(128)} %bitcast.parity, f32[48,128]{1,0:T(8,128)S(1)} %fusion.1.frame, f32[48,128]{1,0:T(8,128)S(1)} %fusion.other, f32[64,128]{1,0:T(8,128)S(1)} %collective-permute-done.8.outer, f32[72,128]{1,0:T(8,128)S(1)} %collective-permute-done.5.right, ...), custom_call_target="tpu_custom_call" | custom-call | tf_op jit(solution)/shard_map/middle_second/pallas_call | solution.py:308
  30.9 0.1 collective-permute-start.9
  31.0 0.7 %outer_second.1.rho_outer = f32[8,128]{1,0:T(8,128)S(1)} custom-call(s32[1]{0:T(128)} %bitcast.parity, f32[48,128]{1,0:T(8,128)S(1)} %fusion.1.frame, f32[64,128]{1,0:T(8,128)S(1)} %collective-permute-done.8.outer, f32[72,128]{1,0:T(8,128)S(1)} %collective-permute-done.5.right, f32[232,128]{1,0:T(8,128)S(1)} %collective-permute-done.3.outer.before, ...), custom_call_target="tpu_custom_call" | custom-call | tf_op jit(solution)/shard_map/outer_second/pallas_call | solution.py:308
  31.7 0.5 collective-permute-done.9.rho_other
  32.2 0.8 %force_second.1 = (f32[8,128]{1,0:T(8,128)S(1)}, f32[8,128]{1,0:T(8,128)S(1)}, f32[4,128]{1,0:T(4,128)S(1)}, f32[128,128]{1,0:T(8,128)S(1)}) custom-call(s32[1]{0:T(128)} %bitcast.parity, s32[8,128]{1,0:T(8,128)S(1)} %get-tuple-element.29.home, f32[48,128]{1,0:T(8,128)S(1)} %fusion.1.frame, f32[48,128]{1,0:T(8,128)S(1)} %fusion.other, ...), custom_call_target="tpu_custom_call" | custom-call | tf_op jit(solution)/shard_map/force_second/pallas_call | solution.py:308
  33.0 20.4 %all_to_all.11 = f32[128,1,128]{2,1,0:T(1,128)S(1)} all-to-all(f32[128,1,128]{2,1,0:T(1,128)S(1)} %bitcast.47), channel_id=1, replica_groups=mesh['depth'=16,'azim'=8] {'depth','azim'}, dimensions={0} | all-to-all | bytes 131072 | tf_op jit(solution)/shard_map/all_to_all | solution.py:392
  53.4 0.8 %soil.1 = (f32[4,16,128]{2,1,0:T(8,128)}, f32[8,128]{1,0:T(8,128)}, f32[8,128]{1,0:T(8,128)}, f32[4,128]{1,0:T(4,128)}) custom-call(f32[128,128]{1,0:T(8,128)S(1)} %bitcast.46, f32[10,16,128]{2,1,0:T(8,128)S(1)} %get-tuple-element.46.soil, f32[8,128]{1,0:T(8,128)S(1)} %get-tuple-element.47.pos, f32[8,128]{1,0:T(8,128)S(1)} %get-tuple-element.48.vel, ...), custom_call_target="tpu_custom_call" | custom-call | tf_op jit(solution)/shard_map/soil/pallas_call | solution.py:393
  (15 shorter events, 0.1 us)
Async XLA Ops:
  1.5 9.8 %collective-permute-start = (f32[96,128]{1,0:T(8,128)S(1)}, f32[96,128]{1,0:T(8,128)S(1)}, u32[]{:S(2)}, u32[]{:S(2)}) collective-permute-start(f32[96,128]{1,0:T(8,128)S(1)} %get-tuple-element.30.send), channel_id=1, source_target_pairs={{0,1},{1,2},{2,3},{3,4},{4,5},{5,6},{6,7},{7,0},{8,9},{9,10},{10,1... | collective-permute-start | bytes 147464 | tf_op jit(solution)/shard_map/ppermute | solution.py:352
  3.7 2.1 %collective-permute-start.2 = (f32[24,128]{1,0:T(8,128)S(1)}, f32[24,128]{1,0:T(8,128)S(1)}, u32[]{:S(2)}, u32[]{:S(2)}) collective-permute-start(f32[24,128]{1,0:T(8,128)S(1)} %get-tuple-element.31), channel_id=1, source_target_pairs={{0,8},{8,0},{16,24},{24,16},{32,40},{40,32},{48,56},{56,48},{64,72... | collective-permute-start | bytes 36872 | tf_op jit(solution)/shard_map/ppermute | solution.py:326
  4.6 6.7 %collective-permute-start.1 = (f32[24,128]{1,0:T(8,128)S(1)}, f32[24,128]{1,0:T(8,128)S(1)}, u32[]{:S(2)}, u32[]{:S(2)}) collective-permute-start(f32[24,128]{1,0:T(8,128)S(1)} %get-tuple-element.31), channel_id=1, source_target_pairs={{0,9},{1,10},{2,11},{3,12},{4,13},{5,14},{6,15},{7,8},{8,1},{9,2},... | collective-permute-start | bytes 36872 | tf_op jit(solution)/shard_map/ppermute | solution.py:353
  11.4 6.2 %collective-permute-start.3 = (f32[232,128]{1,0:T(8,128)S(1)}, f32[232,128]{1,0:T(8,128)S(1)}, u32[]{:S(2)}, u32[]{:S(2)}) collective-permute-start(f32[232,128]{1,0:T(8,128)S(1)} %slice_dynamic-update-slice_fusion), channel_id=1, source_target_pairs={{8,16},{16,8},{24,32},{32,24},{40,48},{48,40},{56,64},{64,56},{72,... | collective-permute-start | bytes 356360 | tf_op jit(solution)/shard_map/ppermute | solution.py:358
  18.2 1.2 %collective-permute-start.4 = (f32[8,128]{1,0:T(8,128)S(1)}, f32[8,128]{1,0:T(8,128)S(1)}, u32[]{:S(2)}, u32[]{:S(2)}) collective-permute-start(f32[8,128]{1,0:T(8,128)S(1)} %get-tuple-element.36.after.rho_own), channel_id=1, source_target_pairs={{0,8},{8,0},{16,24},{24,16},{32,40},{40,32},{48,56},{56,48},{64,72... | collective-permute-start | bytes 12296 | tf_op jit(solution)/shard_map/ppermute | solution.py:326
  20.0 4.9 %collective-permute-start.5 = (f32[72,128]{1,0:T(8,128)S(1)}, f32[72,128]{1,0:T(8,128)S(1)}, u32[]{:S(2)}, u32[]{:S(2)}) collective-permute-start(f32[72,128]{1,0:T(8,128)S(1)} %get-tuple-element.38), channel_id=1, source_target_pairs={{0,7},{1,0},{2,1},{3,2},{4,3},{5,4},{6,5},{7,6},{8,15},{9,8},{10,9... | collective-permute-start | bytes 110600 | tf_op jit(solution)/shard_map/ppermute | solution.py:373
  21.3 1.6 %collective-permute-start.7 = (f32[24,128]{1,0:T(8,128)S(1)}, f32[24,128]{1,0:T(8,128)S(1)}, u32[]{:S(2)}, u32[]{:S(2)}) collective-permute-start(f32[24,128]{1,0:T(8,128)S(1)} %get-tuple-element.39), channel_id=1, source_target_pairs={{0,8},{8,0},{16,24},{24,16},{32,40},{40,32},{48,56},{56,48},{64,72... | collective-permute-start | bytes 36872 | tf_op jit(solution)/shard_map/ppermute | solution.py:326
  21.7 3.1 %collective-permute-start.6 = (f32[24,128]{1,0:T(8,128)S(1)}, f32[24,128]{1,0:T(8,128)S(1)}, u32[]{:S(2)}, u32[]{:S(2)}) collective-permute-start(f32[24,128]{1,0:T(8,128)S(1)} %get-tuple-element.39), channel_id=1, source_target_pairs={{0,15},{1,8},{2,9},{3,10},{4,11},{5,12},{6,13},{7,14},{8,7},{9,0},... | collective-permute-start | bytes 36872 | tf_op jit(solution)/shard_map/ppermute | solution.py:374
  24.9 5.3 %collective-permute-start.8 = (f32[64,128]{1,0:T(8,128)S(1)}, f32[64,128]{1,0:T(8,128)S(1)}, u32[]{:S(2)}, u32[]{:S(2)}) collective-permute-start(f32[64,128]{1,0:T(8,128)S(1)} %pad_maximum_fusion), channel_id=1, source_target_pairs={{8,16},{16,8},{24,32},{32,24},{40,48},{48,40},{56,64},{64,56},{72,... | collective-permute-start | bytes 98312 | tf_op jit(solution)/shard_map/ppermute | solution.py:379
  30.9 1.2 %collective-permute-start.9 = (f32[8,128]{1,0:T(8,128)S(1)}, f32[8,128]{1,0:T(8,128)S(1)}, u32[]{:S(2)}, u32[]{:S(2)}) collective-permute-start(f32[8,128]{1,0:T(8,128)S(1)} %get-tuple-element.43.after.rho_own), channel_id=1, source_target_pairs={{0,8},{8,0},{16,24},{24,16},{32,40},{40,32},{48,56},{56,48},{64,72... | collective-permute-start | bytes 12296 | tf_op jit(solution)/shard_map/ppermute | solution.py:326

commit v7 on v6

--- a/solution.py
+++ b/solution.py
@@ -25,7 +25,8 @@
 HALF = 6 * CELLS
 SENT = 5 * WIDE
 PLACE = 3 * WIDE
-PAIR = 40
+PAIR = 32
+EARLY = 24
 NEAR = [(dr, dc) for dr in (-1, 0, 1) for dc in (-1, 0, 1)]
 
 
@@ -57,8 +58,7 @@
     return jnp.broadcast_to(row, (8, S))
 
 
-def pick(tables, slot, masks):
-    out = None
+def pick(tables, slot, masks, out=None):
     for table, mask in zip(tables, masks):
         got = jnp.take_along_axis(table, slot, axis=1)
         out = got if out is None else jnp.where(mask, got, out)
@@ -76,8 +76,24 @@
     return code & (S - 1), which, [which == n for n in numbers]
 
 
-def density(parity, rows, lists, rho_out, pair):
-    numbers = numbers_of(parity)
+def early(parity, rows, lists, out):
+    numbers = numbers_of(parity)[3:]
+    for k in range(RING):
+        ref, start = lists[k]
+        for t in range(NT):
+            slot, _, masks = decode(ref, start + 8 * t, numbers)
+            for f in (PX, PY, PM):
+                tables = []
+                for dr, dc in NEAR[3:]:
+                    at = f * WIDE + k + 1 + dc
+                    tables.append(spread(rows[dr][at : at + 1, :]))
+                base = (k * NT + t) * EARLY + 8 * f
+                out[base : base + 8, :] = pick(tables, slot, masks)
+
+
+def density(parity, rows, lists, rho_out, pair=None, gathered=None):
+    near = NEAR if gathered is None else NEAR[:3]
+    numbers = numbers_of(parity)[: len(near)]
     rho_out[...] = jnp.zeros((WIDE, S), jnp.float32)
     for k in range(RING):
         col = k + 1
@@ -87,7 +103,7 @@
 
         def table(f):
             out = []
-            for dr, dc in NEAR:
+            for dr, dc in near:
                 r, base = rows[dr]
                 at = base + f * WIDE + col + dc
                 out.append(spread(r[at : at + 1, :]))
@@ -99,9 +115,13 @@
         for t in range(NT):
             slot, which, masks = decode(ref, start + 8 * t, numbers)
             third = (which * 11) >> 5
-            dx = own_x - ((third - 1).astype(jnp.float32) + pick(xs, slot, masks))
-            dy = own_y - ((which - 3 * third - 1).astype(jnp.float32) + pick(ys, slot, masks))
-            mass = pick(ms, slot, masks)
+            before = [None] * 3
+            if gathered is not None:
+                base = (k * NT + t) * EARLY
+                before = [gathered[base + 8 * f : base + 8 * f + 8, :] for f in range(3)]
+            dx = own_x - ((third - 1).astype(jnp.float32) + pick(xs, slot, masks, before[0]))
+            dy = own_y - ((which - 3 * third - 1).astype(jnp.float32) + pick(ys, slot, masks, before[1]))
+            mass = pick(ms, slot, masks, before[2])
             dist = jnp.sqrt(dx * dx + dy * dy)
             tail = jnp.maximum(1.0 - dist, 0.0)
             cube = tail * tail * tail
@@ -110,9 +130,8 @@
                 base = ((k - 1) * NT + t) * PAIR
                 pair[base : base + 8, :] = dx
                 pair[base + 8 : base + 16, :] = dy
-                pair[base + 16 : base + 24, :] = mass
-                pair[base + 24 : base + 32, :] = dist * dist + 0.01
-                pair[base + 32 : base + 40, :] = 20.0 * cube
+                pair[base + 16 : base + 24, :] = dist * dist + 0.01
+                pair[base + 24 : base + 32, :] = mass * (20.0 * cube)
         rho = own_m + jnp.sum(total, axis=0, keepdims=True) + jnp.where(own_m > 0.0, 0.0, 1.0)
         rho_out[col : col + 1, :] = rho
 
@@ -121,36 +140,48 @@
     return sound_sq * (rho - 1.0) / (rho * rho)
 
 
-def force(c, numbers, frame, states, rhos, lists, pair):
+def drag(parity, frame, states, lists, pair, out):
+    numbers = numbers_of(parity)
+    for c in range(CELLS):
+        col = c + 2
+        ref, start = lists[c]
+
+        def table(f):
+            return [spread(states[dr][f * WIDE + col + dc : f * WIDE + col + dc + 1, :]) for dr, dc in NEAR]
+
+        own_vx = spread(frame[PVX * WIDE + col : PVX * WIDE + col + 1, :])
+        own_vy = spread(frame[PVY * WIDE + col : PVY * WIDE + col + 1, :])
+        vxs, vys = table(PVX), table(PVY)
+        for t in range(NT):
+            slot, _, masks = decode(ref, start + 8 * t, numbers)
+            base = (c * NT + t) * PAIR
+            dx = pair[base : base + 8, :]
+            dy = pair[base + 8 : base + 16, :]
+            vdot = (own_vx - pick(vxs, slot, masks)) * dx + (own_vy - pick(vys, slot, masks)) * dy
+            base = (c * NT + t) * 8
+            out[base : base + 8, :] = visc_alpha * jnp.maximum(-vdot, 0.0) / pair[4 * base + 16 : 4 * base + 24, :]
+
+
+def force(c, numbers, frame, rhos, lists, pair, dragged):
     col = c + 2
     ref, start = lists
 
     def own(f):
         return frame[f * WIDE + col : f * WIDE + col + 1, :]
 
-    def table(refs, f):
-        return [spread(refs[dr][f * WIDE + col + dc : f * WIDE + col + dc + 1, :]) for dr, dc in NEAR]
-
     own_rho = rhos[0][col : col + 1, :]
-    own_vx, own_vy = spread(own(PVX)), spread(own(PVY))
     own_q, own_r = spread(term(own_rho)), spread(own_rho)
-    vxs, vys, rs = table(states, PVX), table(states, PVY), table(rhos, 0)
+    tables = [spread(rhos[dr][col + dc : col + dc + 1, :]) for dr, dc in NEAR]
     ax = jnp.zeros((8, S), jnp.float32)
     ay = jnp.zeros((8, S), jnp.float32)
     for t in range(NT):
         slot, _, masks = decode(ref, start + 8 * t, numbers)
         base = (c * NT + t) * PAIR
-        dx = pair[base : base + 8, :]
-        dy = pair[base + 8 : base + 16, :]
-        mass = pair[base + 16 : base + 24, :]
-        soft = pair[base + 24 : base + 32, :]
-        slope = pair[base + 32 : base + 40, :]
-        rho = pick(rs, slot, masks)
-        vdot = (own_vx - pick(vxs, slot, masks)) * dx + (own_vy - pick(vys, slot, masks)) * dy
-        visc = visc_alpha * jnp.maximum(-vdot, 0.0) / (soft * (0.5 * (own_r + rho)))
-        coef = mass * (own_q + term(rho) + visc) * slope
-        ax = ax + coef * dx
-        ay = ay + coef * dy
+        rho = pick(tables, slot, masks)
+        visc = dragged[base // 4 : base // 4 + 8, :] / (0.5 * (own_r + rho))
+        coef = (own_q + term(rho) + visc) * pair[base + 24 : base + 32, :]
+        ax = ax + coef * pair[base : base + 8, :]
+        ay = ay + coef * pair[base + 8 : base + 16, :]
     live = own(PL)
     vx = own(PVX) + step_dt * jnp.sum(ax, axis=0, keepdims=True) * live
     vy = own(PVY) + step_dt * jnp.sum(ay, axis=0, keepdims=True) * live
@@ -162,22 +193,30 @@
 OUTER = SENT + PLACE
 
 
-def middle_first_kernel(parity, frame, other, outer, left, first, send, rho, pair):
-    lists = [(left, HALF + NB * c) for c in range(3)] + [(first, 0), (send, HALF), (send, HALF + NB)]
-    density(parity, {-1: (outer, 0), 0: (frame, 0), 1: (other, 0)}, lists, rho, pair)
-
-
-def outer_first_kernel(parity, frame, outer, after, rho):
+def lists_first(left, first, send):
+    return [(left, HALF + NB * c) for c in range(3)] + [(first, 0), (send, HALF), (send, HALF + NB)]
+
+
+def early_first_kernel(parity, frame, other, left, first, send, out):
+    early(parity, {0: frame, 1: other}, lists_first(left, first, send), out)
+
+
+def middle_first_kernel(parity, frame, outer, left, first, send, gathered, rho, pair):
+    density(parity, {-1: (outer, 0), 0: (frame, 0)}, lists_first(left, first, send), rho, pair, gathered)
+
+
+def outer_first_kernel(parity, frame, other, outer, left, first, send, pair, after, rho, dragged):
     lists = [(outer, OUTER + NB * k) for k in range(RING)]
-    density(parity, {-1: (outer, SENT), 0: (outer, 0), 1: (frame, 0)}, lists, rho, None)
-
-
-def force_first_kernel(parity, frame, other, outer, rho_outer, rho_own, rho_other, left, first, send, pair, out, half):
+    density(parity, {-1: (outer, SENT), 0: (outer, 0), 1: (frame, 0)}, lists, rho)
+    drag(parity, frame, {-1: outer, 0: frame, 1: other}, lists_first(left, first, send)[1:], pair, dragged)
+
+
+def force_first_kernel(parity, frame, outer, rho_outer, rho_own, rho_other, left, first, send, pair, dragged, out, half):
     numbers = numbers_of(parity)
-    lists = [(left, HALF + NB), (left, HALF + 2 * NB), (first, 0), (send, HALF)]
+    lists = lists_first(left, first, send)[1:]
     for c in range(CELLS):
         fields, _ = force(
-            c, numbers, frame, {-1: outer, 0: frame, 1: other}, {-1: rho_outer, 0: rho_own, 1: rho_other}, lists[c], pair
+            c, numbers, frame, {-1: rho_outer, 0: rho_own, 1: rho_other}, lists[c], pair, dragged
         )
         for k, v in enumerate(fields):
             out[k * CELLS + c : k * CELLS + c + 1, :] = v
@@ -186,18 +225,27 @@
     out[HALF + NB : HALF + 2 * NB, :] = first[...]
 
 
-def middle_second_kernel(parity, frame, other, outer, right, left, first, send, rho, pair):
-    lists = [(left, HALF + 2 * NB), (first, 0)] + [(send, HALF + NB * c) for c in range(3)] + [(right, HALF + NB)]
-    density(parity, {-1: (outer, 0), 0: (frame, 0), 1: (other, 0)}, lists, rho, pair)
-
-
-def outer_second_kernel(parity, frame, outer, right, before, after, rho):
+def lists_second(right, left, first, send):
+    return [(left, HALF + 2 * NB), (first, 0)] + [(send, HALF + NB * c) for c in range(3)] + [(right, HALF + NB)]
+
+
+def early_second_kernel(parity, frame, other, right, left, first, send, out):
+    early(parity, {0: frame, 1: other}, lists_second(right, left, first, send), out)
+
+
+def middle_second_kernel(parity, frame, outer, right, left, first, send, gathered, rho, pair):
+    density(parity, {-1: (outer, 0), 0: (frame, 0)}, lists_second(right, left, first, send), rho, pair, gathered)
+
+
+def outer_second_kernel(parity, frame, other, outer, right, before, first, send, pair, after, rho, dragged):
     lists = [(before, OUTER + NB * (2 + c)) for c in range(5)] + [(right, HALF)]
-    density(parity, {-1: (outer, SENT), 0: (outer, 0), 1: (frame, 0)}, lists, rho, None)
+    density(parity, {-1: (outer, SENT), 0: (outer, 0), 1: (frame, 0)}, lists, rho)
+    lists = [(first, 0)] + [(send, HALF + NB * c) for c in range(3)]
+    drag(parity, frame, {-1: outer, 0: frame, 1: other}, lists, pair, dragged)
 
 
 def force_second_kernel(
-    parity, home, frame, other, outer, rho_outer, rho_own, rho_other, first, send, pair, pos_out, vel_out, rho_out, part
+    parity, home, frame, rho_outer, rho_own, rho_other, first, send, pair, dragged, pos_out, vel_out, rho_out, part
 ):
     numbers = numbers_of(parity)
     lists = [(first, 0), (send, HALF), (send, HALF + NB), (send, HALF + 2 * NB)]
@@ -206,7 +254,7 @@
     owners, shares = [], []
     for c in range(CELLS):
         (x, y, m, vx, vy, live), rho = force(
-            c, numbers, frame, {-1: outer, 0: frame, 1: other}, {-1: rho_outer, 0: rho_own, 1: rho_other}, lists[c], pair
+            c, numbers, frame, {-1: rho_outer, 0: rho_own, 1: rho_other}, lists[c], pair, dragged
         )
         pos_out[c : c + 1, :] = x
         pos_out[CELLS + c : CELLS + c + 1, :] = y
@@ -358,16 +406,22 @@
     outer = lax.ppermute(
         jnp.concatenate([frame[:SENT], other[:PLACE], left[HALF:], first, send[HALF:]], axis=0), "depth", facing
     )
+    tiles = CELLS * NT
+    (gathered,) = call(
+        early_first_kernel, "early_first", (RING * NT * EARLY,), frame, other, left, first, send
+    )
     rho_own, pair = call(
-        middle_first_kernel, "middle_first", (WIDE, CELLS * NT * PAIR), frame, other, outer, left, first, send
+        middle_first_kernel, "middle_first", (WIDE, tiles * PAIR), frame, outer, left, first, send, gathered
     )
     rho_other = swapped(rho_own)
-    (rho_outer,) = call(outer_first_kernel, "outer_first", (WIDE,), frame, outer, rho_own)
+    rho_outer, dragged = call(
+        outer_first_kernel, "outer_first", (WIDE, tiles * 8), frame, other, outer, left, first, send, pair, rho_own
+    )
     mid, half = call(
         force_first_kernel,
         "force_first",
         (HALF + 2 * NB, HALF),
-        frame, other, outer, rho_outer, rho_own, rho_other, left, first, send, pair,
+        frame, outer, rho_outer, rho_own, rho_other, left, first, send, pair, dragged,
     )
 
     right = lax.ppermute(mid, "azim", toward_left)
@@ -377,16 +431,24 @@
     frame = merged(mid, right)
     other = merged(beside, across)
     beyond = lax.ppermute(jnp.concatenate([frame[:SENT], other[:PLACE]], axis=0), "depth", facing)
+    (gathered,) = call(
+        early_second_kernel, "early_second", (RING * NT * EARLY,), frame, other, right, left, first, send
+    )
     rho_own, pair = call(
-        middle_second_kernel, "middle_second", (WIDE, CELLS * NT * PAIR), frame, other, beyond, right, left, first, send
+        middle_second_kernel, "middle_second", (WIDE, tiles * PAIR), frame, beyond, right, left, first, send, gathered
     )
     rho_other = swapped(rho_own)
-    (rho_outer,) = call(outer_second_kernel, "outer_second", (WIDE,), frame, beyond, right, outer, rho_own)
+    rho_outer, dragged = call(
+        outer_second_kernel,
+        "outer_second",
+        (WIDE, tiles * 8),
+        frame, other, beyond, right, outer, first, send, pair, rho_own,
+    )
     pos, vel, rho, part = call(
         force_second_kernel,
         "force_second",
         (2 * CELLS, 2 * CELLS, CELLS, S),
-        home, frame, other, beyond, rho_outer, rho_own, rho_other, first, send, pair,
+        home, frame, rho_outer, rho_own, rho_other, first, send, pair, dragged,
     )
 
     arrived = lax.all_to_all(part, ("depth", "azim"), split_axis=0, concat_axis=0, tiled=True)

time: 54.4 us -> 53.4 us (0.982)
  waiting for transfers between devices: 12.9 us -> 11.4 us
    pallas_call x6 -> x8, Pallas kernels: 3.91 us -> 4.33 us  [call(): pl.pallas_call(kernel, out_shape=tuple((kept(n) for n in shapes)), in_spe...]
  transfers between devices with their start and end apart: 10 -> 10, of which waited for: 6 -> 6; matrix products, arithmetic and copies ran while one was open for 0% -> 0% of each run, Pallas kernels for 2% -> 5%
where the time goes in v7:
time: 53.4 us; the launch traced here: 53.2 us
  blocking collectives  20.3 us (38%)
  starting transfers between devices  14.5 us (27%)
  waiting for transfers between devices  11.4 us (21%)
  Pallas kernels  5.99 us (11%)
  between operations  0.82 us (2%)
    all_to_all x1, blocking collectives, local(): lax.all_to_all(part, ('depth', 'azim'), split_axis=0, concat_axis=0, tile...  20.3 us
    ppermute x1, waiting for transfers between devices, local(): across = lax.ppermute(half, ('depth', 'azim'), crossing(1))  5.63 us
    pallas_call x8, Pallas kernels, call(): pl.pallas_call(kernel, out_shape=tuple((kept(n) for n in shapes)), in_spe...  4.33 us
    ppermute x1, starting transfers between devices, local(): lax.ppermute(jnp.concatenate([frame[:SENT], other[:PLACE]], axis=0), 'dep...  3.75 us
    ppermute x1, starting transfers between devices, local(): lax.ppermute(jnp.concatenate([frame[:SENT], other[:PLACE], left[HALF:], f...  3.43 us
    ppermute x1, waiting for transfers between devices, local(): lax.ppermute(jnp.concatenate([frame[:SENT], other[:PLACE], left[HALF:], f...  2.2 us
    ppermute x1, starting transfers between devices, local(): left = lax.ppermute(send, 'azim', toward_right)  2.11 us
    ppermute x1, waiting for transfers between devices, local(): across = lax.ppermute(half, ('depth', 'azim'), crossing(-1))  2.05 us
  transfers between devices with their start and end apart: 10, of which 6 were waited for; matrix products, arithmetic and copies ran while one was open for 0% of the time, Pallas kernels for 5%

profile of v7, /device:TPU:1, one launch (start us, length us, event | category | flops | bytes accessed | tf_op | source)
XLA Modules:
  0.0 53.2 jit_solution(13400997029848002522)
XLA Ops:
  0.6 0.9 %pack.1 = (f32[96,128]{1,0:T(8,128)S(1)}, f32[24,128]{1,0:T(8,128)S(1)}, f32[24,128]{1,0:T(8,128)S(1)}, s32[8,128]{1,0:T(8,128)S(1)}, f32[10,16,128]{2,1,0:T(8,128)S(1)}) custom-call(s32[1,4]{1,0:T(1,128)} %count.1, f32[8,128]{1,0:T(8,128)} %bitcast.65, f32[8,128]{1,0:T(8,128)} %bitcast.66, f32[4,128]{1,0:T(4,128)} %bitcast.67, s32[96,128]{1,0:T(8,128)} %bitcast.60, ...), custom_call_target="tpu_custom_call" | custom-call | tf_op jit(solution)/shard_map/pack/pallas_call | solution.py:376
  1.5 2.1 %collective-permute-start = (f32[96,128]{1,0:T(8,128)S(1)}, f32[96,128]{1,0:T(8,128)S(1)}, u32[]{:S(2)}, u32[]{:S(2)}) collective-permute-start(f32[96,128]{1,0:T(8,128)S(1)} %get-tuple-element.34.send), channel_id=1, source_target_pairs={{0,1},{1,2},{2,3},{3,4},{4,5},{5,6},{6,7},{7,0},{8,9},{9,10},{10,1... | collective-permute-start | bytes 147464 | tf_op jit(solution)/shard_map/ppermute | solution.py:400
  3.7 1.0 %collective-permute-start.2 = (f32[24,128]{1,0:T(8,128)S(1)}, f32[24,128]{1,0:T(8,128)S(1)}, u32[]{:S(2)}, u32[]{:S(2)}) collective-permute-start(f32[24,128]{1,0:T(8,128)S(1)} %get-tuple-element.35), channel_id=1, source_target_pairs={{0,8},{8,0},{16,24},{24,16},{32,40},{40,32},{48,56},{56,48},{64,72... | collective-permute-start | bytes 36872 | tf_op jit(solution)/shard_map/ppermute | solution.py:374
  4.6 1.1 %collective-permute-start.1 = (f32[24,128]{1,0:T(8,128)S(1)}, f32[24,128]{1,0:T(8,128)S(1)}, u32[]{:S(2)}, u32[]{:S(2)}) collective-permute-start(f32[24,128]{1,0:T(8,128)S(1)} %get-tuple-element.35), channel_id=1, source_target_pairs={{0,9},{1,10},{2,11},{3,12},{4,13},{5,14},{6,15},{7,8},{8,1},{9,2},... | collective-permute-start | bytes 36872 | tf_op jit(solution)/shard_map/ppermute | solution.py:401
  5.7 0.0 collective-permute-done.2
  5.7 5.6 %collective-permute-done.1 = f32[24,128]{1,0:T(8,128)S(1)} collective-permute-done((f32[24,128]{1,0:T(8,128)S(1)}, f32[24,128]{1,0:T(8,128)S(1)}, u32[]{:S(2)}, u32[]{:S(2)}) %collective-permute-start.1) | collective-permute-done | bytes 12320 | tf_op jit(solution)/shard_map/ppermute | solution.py:401
  11.3 0.0 collective-permute-done.left
  11.4 3.4 %collective-permute-start.3 = (f32[232,128]{1,0:T(8,128)S(1)}, f32[232,128]{1,0:T(8,128)S(1)}, u32[]{:S(2)}, u32[]{:S(2)}) collective-permute-start(f32[232,128]{1,0:T(8,128)S(1)} %slice_dynamic-update-slice_fusion), channel_id=1, source_target_pairs={{8,16},{16,8},{24,32},{32,24},{40,48},{48,40},{56,64},{64,56},{72,... | collective-permute-start | bytes 356360 | tf_op jit(solution)/shard_map/ppermute | solution.py:406
  14.9 0.5 early_first.1.gathered
  15.4 2.2 %collective-permute-done.3.outer.before = f32[232,128]{1,0:T(8,128)S(1)} collective-permute-done((f32[232,128]{1,0:T(8,128)S(1)}, f32[232,128]{1,0:T(8,128)S(1)}, u32[]{:S(2)}, u32[]{:S(2)}) %collective-permute-start.3) | collective-permute-done | bytes 118816 | tf_op jit(solution)/shard_map/ppermute | solution.py:406
  17.6 0.3 middle_first.1
  17.9 0.1 collective-permute-start.4
  18.0 0.9 %outer_first.1 = (f32[8,128]{1,0:T(8,128)S(1)}, f32[96,128]{1,0:T(8,128)S(1)}) custom-call(s32[1]{0:T(128)} %bitcast.parity, f32[48,128]{1,0:T(8,128)S(1)} %get-tuple-element.71.frame, f32[48,128]{1,0:T(8,128)S(1)} %get-tuple-element.70.other, f32[232,128]{1,0:T(8,128)S(1)} %collective-permute-done.3.outer.before, f32[96,128]{1,0:T(8,128)S(1)} %collective-permute-done.left, ...), custom_call_target="tpu_custom_call" | custom-call | tf_op jit(solution)/shard_map/outer_first/pallas_call | solution.py:356
  18.9 0.2 collective-permute-done.4.rho_other
  19.2 0.3 force_first.1
  19.4 1.3 %collective-permute-start.5 = (f32[72,128]{1,0:T(8,128)S(1)}, f32[72,128]{1,0:T(8,128)S(1)}, u32[]{:S(2)}, u32[]{:S(2)}) collective-permute-start(f32[72,128]{1,0:T(8,128)S(1)} %get-tuple-element.44), channel_id=1, source_target_pairs={{0,7},{1,0},{2,1},{3,2},{4,3},{5,4},{6,5},{7,6},{8,15},{9,8},{10,9... | collective-permute-start | bytes 110600 | tf_op jit(solution)/shard_map/ppermute | solution.py:427
  20.8 0.6 %collective-permute-start.7 = (f32[24,128]{1,0:T(8,128)S(1)}, f32[24,128]{1,0:T(8,128)S(1)}, u32[]{:S(2)}, u32[]{:S(2)}) collective-permute-start(f32[24,128]{1,0:T(8,128)S(1)} %get-tuple-element.45), channel_id=1, source_target_pairs={{0,8},{8,0},{16,24},{24,16},{32,40},{40,32},{48,56},{56,48},{64,72... | collective-permute-start | bytes 36872 | tf_op jit(solution)/shard_map/ppermute | solution.py:374
  21.3 1.1 %collective-permute-start.6 = (f32[24,128]{1,0:T(8,128)S(1)}, f32[24,128]{1,0:T(8,128)S(1)}, u32[]{:S(2)}, u32[]{:S(2)}) collective-permute-start(f32[24,128]{1,0:T(8,128)S(1)} %get-tuple-element.45), channel_id=1, source_target_pairs={{0,15},{1,8},{2,9},{3,10},{4,11},{5,12},{6,13},{7,14},{8,7},{9,0},... | collective-permute-start | bytes 36872 | tf_op jit(solution)/shard_map/ppermute | solution.py:428
  22.4 0.0 collective-permute-done.7
  22.4 2.1 %collective-permute-done.6 = f32[24,128]{1,0:T(8,128)S(1)} collective-permute-done((f32[24,128]{1,0:T(8,128)S(1)}, f32[24,128]{1,0:T(8,128)S(1)}, u32[]{:S(2)}, u32[]{:S(2)}) %collective-permute-start.6) | collective-permute-done | bytes 12320 | tf_op jit(solution)/shard_map/ppermute | solution.py:428
  24.5 0.0 collective-permute-done.5.right
  24.5 3.8 %collective-permute-start.8 = (f32[64,128]{1,0:T(8,128)S(1)}, f32[64,128]{1,0:T(8,128)S(1)}, u32[]{:S(2)}, u32[]{:S(2)}) collective-permute-start(f32[64,128]{1,0:T(8,128)S(1)} %pad_maximum_fusion), channel_id=1, source_target_pairs={{8,16},{16,8},{24,32},{32,24},{40,48},{48,40},{56,64},{64,56},{72,... | collective-permute-start | bytes 98312 | tf_op jit(solution)/shard_map/ppermute | solution.py:433
  28.3 0.5 early_second.1.gathered
  28.8 1.1 %collective-permute-done.8.outer = f32[64,128]{1,0:T(8,128)S(1)} collective-permute-done((f32[64,128]{1,0:T(8,128)S(1)}, f32[64,128]{1,0:T(8,128)S(1)}, u32[]{:S(2)}, u32[]{:S(2)}) %collective-permute-start.8) | collective-permute-done | bytes 32800 | tf_op jit(solution)/shard_map/ppermute | solution.py:433
  29.9 0.3 middle_second.1
  30.2 0.1 collective-permute-start.9
  30.3 0.9 %outer_second.1 = (f32[8,128]{1,0:T(8,128)S(1)}, f32[96,128]{1,0:T(8,128)S(1)}) custom-call(s32[1]{0:T(128)} %bitcast.parity, f32[48,128]{1,0:T(8,128)S(1)} %fusion.1.frame, f32[48,128]{1,0:T(8,128)S(1)} %fusion.other, f32[64,128]{1,0:T(8,128)S(1)} %collective-permute-done.8.outer, f32[72,128]{1,0:T(8,128)S(1)} %collective-permute-done.5.right, ...), custom_call_target="tpu_custom_call" | custom-call | tf_op jit(solution)/shard_map/outer_second/pallas_call | solution.py:356
  31.2 0.2 collective-permute-done.9.rho_other
  31.5 0.6 %force_second.1 = (f32[8,128]{1,0:T(8,128)S(1)}, f32[8,128]{1,0:T(8,128)S(1)}, f32[4,128]{1,0:T(4,128)S(1)}, f32[128,128]{1,0:T(8,128)S(1)}) custom-call(s32[1]{0:T(128)} %bitcast.parity, s32[8,128]{1,0:T(8,128)S(1)} %get-tuple-element.33.home, f32[48,128]{1,0:T(8,128)S(1)} %fusion.1.frame, f32[8,128]{1,0:T(8,128)S(1)} %get-tuple-element.51.rho_outer, ...), custom_call_target="tpu_custom_call" | custom-call | tf_op jit(solution)/shard_map/force_second/pallas_call | solution.py:356
  32.1 20.3 %all_to_all.11 = f32[128,1,128]{2,1,0:T(1,128)S(1)} all-to-all(f32[128,1,128]{2,1,0:T(1,128)S(1)} %bitcast.47), channel_id=1, replica_groups=mesh['depth'=16,'azim'=8] {'depth','azim'}, dimensions={0} | all-to-all | bytes 131072 | tf_op jit(solution)/shard_map/all_to_all | solution.py:454
  52.4 0.8 %soil.1 = (f32[4,16,128]{2,1,0:T(8,128)}, f32[8,128]{1,0:T(8,128)}, f32[8,128]{1,0:T(8,128)}, f32[4,128]{1,0:T(4,128)}) custom-call(f32[128,128]{1,0:T(8,128)S(1)} %bitcast.46, f32[10,16,128]{2,1,0:T(8,128)S(1)} %get-tuple-element.54.soil, f32[8,128]{1,0:T(8,128)S(1)} %get-tuple-element.55.pos, f32[8,128]{1,0:T(8,128)S(1)} %get-tuple-element.56.vel, ...), custom_call_target="tpu_custom_call" | custom-call | tf_op jit(solution)/shard_map/soil/pallas_call | solution.py:455
  (15 shorter events, 0.1 us)
Async XLA Ops:
  1.5 9.8 %collective-permute-start = (f32[96,128]{1,0:T(8,128)S(1)}, f32[96,128]{1,0:T(8,128)S(1)}, u32[]{:S(2)}, u32[]{:S(2)}) collective-permute-start(f32[96,128]{1,0:T(8,128)S(1)} %get-tuple-element.34.send), channel_id=1, source_target_pairs={{0,1},{1,2},{2,3},{3,4},{4,5},{5,6},{6,7},{7,0},{8,9},{9,10},{10,1... | collective-permute-start | bytes 147464 | tf_op jit(solution)/shard_map/ppermute | solution.py:400
  3.7 2.1 %collective-permute-start.2 = (f32[24,128]{1,0:T(8,128)S(1)}, f32[24,128]{1,0:T(8,128)S(1)}, u32[]{:S(2)}, u32[]{:S(2)}) collective-permute-start(f32[24,128]{1,0:T(8,128)S(1)} %get-tuple-element.35), channel_id=1, source_target_pairs={{0,8},{8,0},{16,24},{24,16},{32,40},{40,32},{48,56},{56,48},{64,72... | collective-permute-start | bytes 36872 | tf_op jit(solution)/shard_map/ppermute | solution.py:374
  4.6 6.7 %collective-permute-start.1 = (f32[24,128]{1,0:T(8,128)S(1)}, f32[24,128]{1,0:T(8,128)S(1)}, u32[]{:S(2)}, u32[]{:S(2)}) collective-permute-start(f32[24,128]{1,0:T(8,128)S(1)} %get-tuple-element.35), channel_id=1, source_target_pairs={{0,9},{1,10},{2,11},{3,12},{4,13},{5,14},{6,15},{7,8},{8,1},{9,2},... | collective-permute-start | bytes 36872 | tf_op jit(solution)/shard_map/ppermute | solution.py:401
  11.4 6.2 %collective-permute-start.3 = (f32[232,128]{1,0:T(8,128)S(1)}, f32[232,128]{1,0:T(8,128)S(1)}, u32[]{:S(2)}, u32[]{:S(2)}) collective-permute-start(f32[232,128]{1,0:T(8,128)S(1)} %slice_dynamic-update-slice_fusion), channel_id=1, source_target_pairs={{8,16},{16,8},{24,32},{32,24},{40,48},{48,40},{56,64},{64,56},{72,... | collective-permute-start | bytes 356360 | tf_op jit(solution)/shard_map/ppermute | solution.py:406
  17.9 1.2 %collective-permute-start.4 = (f32[8,128]{1,0:T(8,128)S(1)}, f32[8,128]{1,0:T(8,128)S(1)}, u32[]{:S(2)}, u32[]{:S(2)}) collective-permute-start(f32[8,128]{1,0:T(8,128)S(1)} %get-tuple-element.41.after.rho_own), channel_id=1, source_target_pairs={{0,8},{8,0},{16,24},{24,16},{32,40},{40,32},{48,56},{56,48},{64,72... | collective-permute-start | bytes 12296 | tf_op jit(solution)/shard_map/ppermute | solution.py:374
  19.4 5.0 %collective-permute-start.5 = (f32[72,128]{1,0:T(8,128)S(1)}, f32[72,128]{1,0:T(8,128)S(1)}, u32[]{:S(2)}, u32[]{:S(2)}) collective-permute-start(f32[72,128]{1,0:T(8,128)S(1)} %get-tuple-element.44), channel_id=1, source_target_pairs={{0,7},{1,0},{2,1},{3,2},{4,3},{5,4},{6,5},{7,6},{8,15},{9,8},{10,9... | collective-permute-start | bytes 110600 | tf_op jit(solution)/shard_map/ppermute | solution.py:427
  20.8 1.6 %collective-permute-start.7 = (f32[24,128]{1,0:T(8,128)S(1)}, f32[24,128]{1,0:T(8,128)S(1)}, u32[]{:S(2)}, u32[]{:S(2)}) collective-permute-start(f32[24,128]{1,0:T(8,128)S(1)} %get-tuple-element.45), channel_id=1, source_target_pairs={{0,8},{8,0},{16,24},{24,16},{32,40},{40,32},{48,56},{56,48},{64,72... | collective-permute-start | bytes 36872 | tf_op jit(solution)/shard_map/ppermute | solution.py:374
  21.3 3.1 %collective-permute-start.6 = (f32[24,128]{1,0:T(8,128)S(1)}, f32[24,128]{1,0:T(8,128)S(1)}, u32[]{:S(2)}, u32[]{:S(2)}) collective-permute-start(f32[24,128]{1,0:T(8,128)S(1)} %get-tuple-element.45), channel_id=1, source_target_pairs={{0,15},{1,8},{2,9},{3,10},{4,11},{5,12},{6,13},{7,14},{8,7},{9,0},... | collective-permute-start | bytes 36872 | tf_op jit(solution)/shard_map/ppermute | solution.py:428
  24.5 5.3 %collective-permute-start.8 = (f32[64,128]{1,0:T(8,128)S(1)}, f32[64,128]{1,0:T(8,128)S(1)}, u32[]{:S(2)}, u32[]{:S(2)}) collective-permute-start(f32[64,128]{1,0:T(8,128)S(1)} %pad_maximum_fusion), channel_id=1, source_target_pairs={{8,16},{16,8},{24,32},{32,24},{40,48},{48,40},{56,64},{64,56},{72,... | collective-permute-start | bytes 98312 | tf_op jit(solution)/shard_map/ppermute | solution.py:433
  30.2 1.2 %collective-permute-start.9 = (f32[8,128]{1,0:T(8,128)S(1)}, f32[8,128]{1,0:T(8,128)S(1)}, u32[]{:S(2)}, u32[]{:S(2)}) collective-permute-start(f32[8,128]{1,0:T(8,128)S(1)} %get-tuple-element.50.after.rho_own), channel_id=1, source_target_pairs={{0,8},{8,0},{16,24},{24,16},{32,40},{40,32},{48,56},{56,48},{64,72... | collective-permute-start | bytes 12296 | tf_op jit(solution)/shard_map/ppermute | solution.py:374

commit v8 on v7

--- a/solution.py
+++ b/solution.py
@@ -400,7 +400,7 @@
     left = lax.ppermute(send, "azim", toward_right)
     across = lax.ppermute(half, ("depth", "azim"), crossing(1))
     beside = swapped(half)
-    left, across, beside = lax.optimization_barrier((left, across, beside))
+    left, across = lax.optimization_barrier((left, across))
     frame = merged(left, send)
     other = merged(across, beside)
     outer = lax.ppermute(
@@ -427,7 +427,7 @@
     right = lax.ppermute(mid, "azim", toward_left)
     across = lax.ppermute(half, ("depth", "azim"), crossing(-1))
     beside = swapped(half)
-    right, across, beside = lax.optimization_barrier((right, across, beside))
+    right, across = lax.optimization_barrier((right, across))
     frame = merged(mid, right)
     other = merged(beside, across)
     beyond = lax.ppermute(jnp.concatenate([frame[:SENT], other[:PLACE]], axis=0), "depth", facing)

time: 53.4 us -> 53.1 us (level)
    ppermute x4, starting transfers between devices: 1.68 us -> 0.18 us  [swapped(): return lax.ppermute(a, 'depth', pairs)]
    ppermute x1, starting transfers between devices: 1.1 us -> 2.05 us  [local(): across = lax.ppermute(half, ('depth', 'azim'), crossing(1))]
where the time goes in v8:
time: 53.1 us; the launch traced here: 52.9 us
  blocking collectives  19.9 us (37%)
  starting transfers between devices  14.6 us (27%)
  waiting for transfers between devices  11.4 us (21%)
  Pallas kernels  5.99 us (11%)
  between operations  0.82 us (2%)
    all_to_all x1, blocking collectives, local(): lax.all_to_all(part, ('depth', 'azim'), split_axis=0, concat_axis=0, tile...  19.9 us
    ppermute x1, waiting for transfers between devices, local(): across = lax.ppermute(half, ('depth', 'azim'), crossing(1))  5.29 us
    pallas_call x8, Pallas kernels, call(): pl.pallas_call(kernel, out_shape=tuple((kept(n) for n in shapes)), in_spe...  4.33 us
    ppermute x1, starting transfers between devices, local(): lax.ppermute(jnp.concatenate([frame[:SENT], other[:PLACE]], axis=0), 'dep...  4.25 us
    ppermute x1, starting transfers between devices, local(): lax.ppermute(jnp.concatenate([frame[:SENT], other[:PLACE], left[HALF:], f...  3.77 us
    ppermute x1, waiting for transfers between devices, local(): lax.ppermute(jnp.concatenate([frame[:SENT], other[:PLACE], left[HALF:], f...  2.52 us
    ppermute x1, starting transfers between devices, local(): left = lax.ppermute(send, 'azim', toward_right)  2.11 us
    ppermute x1, waiting for transfers between devices, local(): across = lax.ppermute(half, ('depth', 'azim'), crossing(-1))  2.07 us
  transfers between devices with their start and end apart: 10, of which 6 were waited for; matrix products, arithmetic and copies ran while one was open for 0% of the time, Pallas kernels for 5%

profile of v8, /device:TPU:1, one launch (start us, length us, event | category | flops | bytes accessed | tf_op | source)
XLA Modules:
  0.0 52.9 jit_solution(2367695523985353403)
XLA Ops:
  0.6 0.9 %pack.1 = (f32[96,128]{1,0:T(8,128)S(1)}, f32[24,128]{1,0:T(8,128)S(1)}, f32[24,128]{1,0:T(8,128)S(1)}, s32[8,128]{1,0:T(8,128)S(1)}, f32[10,16,128]{2,1,0:T(8,128)S(1)}) custom-call(s32[1,4]{1,0:T(1,128)} %count.1, f32[8,128]{1,0:T(8,128)} %bitcast.65, f32[8,128]{1,0:T(8,128)} %bitcast.66, f32[4,128]{1,0:T(4,128)} %bitcast.67, s32[96,128]{1,0:T(8,128)} %bitcast.56, ...), custom_call_target="tpu_custom_call" | custom-call | tf_op jit(solution)/shard_map/pack/pallas_call | solution.py:376
  1.5 2.1 %collective-permute-start = (f32[96,128]{1,0:T(8,128)S(1)}, f32[96,128]{1,0:T(8,128)S(1)}, u32[]{:S(2)}, u32[]{:S(2)}) collective-permute-start(f32[96,128]{1,0:T(8,128)S(1)} %get-tuple-element.32.send), channel_id=1, source_target_pairs={{0,1},{1,2},{2,3},{3,4},{4,5},{5,6},{6,7},{7,0},{8,9},{9,10},{10,1... | collective-permute-start | bytes 147464 | tf_op jit(solution)/shard_map/ppermute | solution.py:400
  3.7 2.1 %collective-permute-start.1 = (f32[24,128]{1,0:T(8,128)S(1)}, f32[24,128]{1,0:T(8,128)S(1)}, u32[]{:S(2)}, u32[]{:S(2)}) collective-permute-start(f32[24,128]{1,0:T(8,128)S(1)} %get-tuple-element.33), channel_id=1, source_target_pairs={{0,9},{1,10},{2,11},{3,12},{4,13},{5,14},{6,15},{7,8},{8,1},{9,2},... | collective-permute-start | bytes 36872 | tf_op jit(solution)/shard_map/ppermute | solution.py:401
  5.7 0.0 collective-permute-start.2
  5.7 5.3 %collective-permute-done.1 = f32[24,128]{1,0:T(8,128)S(1)} collective-permute-done((f32[24,128]{1,0:T(8,128)S(1)}, f32[24,128]{1,0:T(8,128)S(1)}, u32[]{:S(2)}, u32[]{:S(2)}) %collective-permute-start.1) | collective-permute-done | bytes 12320 | tf_op jit(solution)/shard_map/ppermute | solution.py:401
  11.0 0.0 collective-permute-done.left
  11.0 0.0 collective-permute-done.2
  11.1 3.8 %collective-permute-start.3 = (f32[232,128]{1,0:T(8,128)S(1)}, f32[232,128]{1,0:T(8,128)S(1)}, u32[]{:S(2)}, u32[]{:S(2)}) collective-permute-start(f32[232,128]{1,0:T(8,128)S(1)} %slice_dynamic-update-slice_fusion), channel_id=1, source_target_pairs={{8,16},{16,8},{24,32},{32,24},{40,48},{48,40},{56,64},{64,56},{72,... | collective-permute-start | bytes 356360 | tf_op jit(solution)/shard_map/ppermute | solution.py:406
  14.9 0.5 early_first.1.gathered
  15.4 2.5 %collective-permute-done.3.outer.before = f32[232,128]{1,0:T(8,128)S(1)} collective-permute-done((f32[232,128]{1,0:T(8,128)S(1)}, f32[232,128]{1,0:T(8,128)S(1)}, u32[]{:S(2)}, u32[]{:S(2)}) %collective-permute-start.3) | collective-permute-done | bytes 118816 | tf_op jit(solution)/shard_map/ppermute | solution.py:406
  17.9 0.3 middle_first.1
  18.2 0.1 collective-permute-start.4
  18.3 0.9 %outer_first.1 = (f32[8,128]{1,0:T(8,128)S(1)}, f32[96,128]{1,0:T(8,128)S(1)}) custom-call(s32[1]{0:T(128)} %bitcast.parity, f32[48,128]{1,0:T(8,128)S(1)} %fusion.3.frame, f32[48,128]{1,0:T(8,128)S(1)} %fusion.2.other, f32[232,128]{1,0:T(8,128)S(1)} %collective-permute-done.3.outer.before, f32[96,128]{1,0:T(8,128)S(1)} %collective-permute-done.left, ...), custom_call_target="tpu_custom_call" | custom-call | tf_op jit(solution)/shard_map/outer_first/pallas_call | solution.py:356
  19.3 0.2 collective-permute-done.4.rho_other
  19.5 0.3 force_first.1
  19.8 1.0 %collective-permute-start.5 = (f32[72,128]{1,0:T(8,128)S(1)}, f32[72,128]{1,0:T(8,128)S(1)}, u32[]{:S(2)}, u32[]{:S(2)}) collective-permute-start(f32[72,128]{1,0:T(8,128)S(1)} %get-tuple-element.41), channel_id=1, source_target_pairs={{0,7},{1,0},{2,1},{3,2},{4,3},{5,4},{6,5},{7,6},{8,15},{9,8},{10,9... | collective-permute-start | bytes 110600 | tf_op jit(solution)/shard_map/ppermute | solution.py:427
  20.8 1.2 %collective-permute-start.6 = (f32[24,128]{1,0:T(8,128)S(1)}, f32[24,128]{1,0:T(8,128)S(1)}, u32[]{:S(2)}, u32[]{:S(2)}) collective-permute-start(f32[24,128]{1,0:T(8,128)S(1)} %get-tuple-element.42), channel_id=1, source_target_pairs={{0,15},{1,8},{2,9},{3,10},{4,11},{5,12},{6,13},{7,14},{8,7},{9,0},... | collective-permute-start | bytes 36872 | tf_op jit(solution)/shard_map/ppermute | solution.py:428
  22.0 0.0 collective-permute-start.7
  22.0 2.1 %collective-permute-done.6 = f32[24,128]{1,0:T(8,128)S(1)} collective-permute-done((f32[24,128]{1,0:T(8,128)S(1)}, f32[24,128]{1,0:T(8,128)S(1)}, u32[]{:S(2)}, u32[]{:S(2)}) %collective-permute-start.6) | collective-permute-done | bytes 12320 | tf_op jit(solution)/shard_map/ppermute | solution.py:428
  24.1 0.0 collective-permute-done.5.right
  24.1 0.0 collective-permute-done.7
  24.1 4.2 %collective-permute-start.8 = (f32[64,128]{1,0:T(8,128)S(1)}, f32[64,128]{1,0:T(8,128)S(1)}, u32[]{:S(2)}, u32[]{:S(2)}) collective-permute-start(f32[64,128]{1,0:T(8,128)S(1)} %pad_maximum_fusion), channel_id=1, source_target_pairs={{8,16},{16,8},{24,32},{32,24},{40,48},{48,40},{56,64},{64,56},{72,... | collective-permute-start | bytes 98312 | tf_op jit(solution)/shard_map/ppermute | solution.py:433
  28.4 0.5 early_second.1.gathered
  28.9 1.1 %collective-permute-done.8.outer = f32[64,128]{1,0:T(8,128)S(1)} collective-permute-done((f32[64,128]{1,0:T(8,128)S(1)}, f32[64,128]{1,0:T(8,128)S(1)}, u32[]{:S(2)}, u32[]{:S(2)}) %collective-permute-start.8) | collective-permute-done | bytes 32800 | tf_op jit(solution)/shard_map/ppermute | solution.py:433
  30.0 0.3 middle_second.1
  30.3 0.1 collective-permute-start.9
  30.4 0.9 %outer_second.1 = (f32[8,128]{1,0:T(8,128)S(1)}, f32[96,128]{1,0:T(8,128)S(1)}) custom-call(s32[1]{0:T(128)} %bitcast.parity, f32[48,128]{1,0:T(8,128)S(1)} %fusion.1.frame, f32[48,128]{1,0:T(8,128)S(1)} %fusion.other, f32[64,128]{1,0:T(8,128)S(1)} %collective-permute-done.8.outer, f32[72,128]{1,0:T(8,128)S(1)} %collective-permute-done.5.right, ...), custom_call_target="tpu_custom_call" | custom-call | tf_op jit(solution)/shard_map/outer_second/pallas_call | solution.py:356
  31.3 0.2 collective-permute-done.9.rho_other
  31.6 0.6 %force_second.1 = (f32[8,128]{1,0:T(8,128)S(1)}, f32[8,128]{1,0:T(8,128)S(1)}, f32[4,128]{1,0:T(4,128)S(1)}, f32[128,128]{1,0:T(8,128)S(1)}) custom-call(s32[1]{0:T(128)} %bitcast.parity, s32[8,128]{1,0:T(8,128)S(1)} %get-tuple-element.31.home, f32[48,128]{1,0:T(8,128)S(1)} %fusion.1.frame, f32[8,128]{1,0:T(8,128)S(1)} %get-tuple-element.47.rho_outer, ...), custom_call_target="tpu_custom_call" | custom-call | tf_op jit(solution)/shard_map/force_second/pallas_call | solution.py:356
  32.2 19.9 %all_to_all.11 = f32[128,1,128]{2,1,0:T(1,128)S(1)} all-to-all(f32[128,1,128]{2,1,0:T(1,128)S(1)} %bitcast.47), channel_id=1, replica_groups=mesh['depth'=16,'azim'=8] {'depth','azim'}, dimensions={0} | all-to-all | bytes 131072 | tf_op jit(solution)/shard_map/all_to_all | solution.py:454
  52.1 0.8 %soil.1 = (f32[4,16,128]{2,1,0:T(8,128)}, f32[8,128]{1,0:T(8,128)}, f32[8,128]{1,0:T(8,128)}, f32[4,128]{1,0:T(4,128)}) custom-call(f32[128,128]{1,0:T(8,128)S(1)} %bitcast.46, f32[10,16,128]{2,1,0:T(8,128)S(1)} %get-tuple-element.50.soil, f32[8,128]{1,0:T(8,128)S(1)} %get-tuple-element.51.pos, f32[8,128]{1,0:T(8,128)S(1)} %get-tuple-element.52.vel, ...), custom_call_target="tpu_custom_call" | custom-call | tf_op jit(solution)/shard_map/soil/pallas_call | solution.py:455
  (16 shorter events, 0.1 us)
Async XLA Ops:
  1.5 9.5 %collective-permute-start = (f32[96,128]{1,0:T(8,128)S(1)}, f32[96,128]{1,0:T(8,128)S(1)}, u32[]{:S(2)}, u32[]{:S(2)}) collective-permute-start(f32[96,128]{1,0:T(8,128)S(1)} %get-tuple-element.32.send), channel_id=1, source_target_pairs={{0,1},{1,2},{2,3},{3,4},{4,5},{5,6},{6,7},{7,0},{8,9},{9,10},{10,1... | collective-permute-start | bytes 147464 | tf_op jit(solution)/shard_map/ppermute | solution.py:400
  3.7 7.3 %collective-permute-start.1 = (f32[24,128]{1,0:T(8,128)S(1)}, f32[24,128]{1,0:T(8,128)S(1)}, u32[]{:S(2)}, u32[]{:S(2)}) collective-permute-start(f32[24,128]{1,0:T(8,128)S(1)} %get-tuple-element.33), channel_id=1, source_target_pairs={{0,9},{1,10},{2,11},{3,12},{4,13},{5,14},{6,15},{7,8},{8,1},{9,2},... | collective-permute-start | bytes 36872 | tf_op jit(solution)/shard_map/ppermute | solution.py:401
  5.7 5.3 %collective-permute-start.2 = (f32[24,128]{1,0:T(8,128)S(1)}, f32[24,128]{1,0:T(8,128)S(1)}, u32[]{:S(2)}, u32[]{:S(2)}) collective-permute-start(f32[24,128]{1,0:T(8,128)S(1)} %get-tuple-element.33), channel_id=1, source_target_pairs={{0,8},{8,0},{16,24},{24,16},{32,40},{40,32},{48,56},{56,48},{64,72... | collective-permute-start | bytes 36872 | tf_op jit(solution)/shard_map/ppermute | solution.py:374
  11.1 6.8 %collective-permute-start.3 = (f32[232,128]{1,0:T(8,128)S(1)}, f32[232,128]{1,0:T(8,128)S(1)}, u32[]{:S(2)}, u32[]{:S(2)}) collective-permute-start(f32[232,128]{1,0:T(8,128)S(1)} %slice_dynamic-update-slice_fusion), channel_id=1, source_target_pairs={{8,16},{16,8},{24,32},{32,24},{40,48},{48,40},{56,64},{64,56},{72,... | collective-permute-start | bytes 356360 | tf_op jit(solution)/shard_map/ppermute | solution.py:406
  18.2 1.2 %collective-permute-start.4 = (f32[8,128]{1,0:T(8,128)S(1)}, f32[8,128]{1,0:T(8,128)S(1)}, u32[]{:S(2)}, u32[]{:S(2)}) collective-permute-start(f32[8,128]{1,0:T(8,128)S(1)} %get-tuple-element.38.after.rho_own), channel_id=1, source_target_pairs={{0,8},{8,0},{16,24},{24,16},{32,40},{40,32},{48,56},{56,48},{64,72... | collective-permute-start | bytes 12296 | tf_op jit(solution)/shard_map/ppermute | solution.py:374
  19.8 4.3 %collective-permute-start.5 = (f32[72,128]{1,0:T(8,128)S(1)}, f32[72,128]{1,0:T(8,128)S(1)}, u32[]{:S(2)}, u32[]{:S(2)}) collective-permute-start(f32[72,128]{1,0:T(8,128)S(1)} %get-tuple-element.41), channel_id=1, source_target_pairs={{0,7},{1,0},{2,1},{3,2},{4,3},{5,4},{6,5},{7,6},{8,15},{9,8},{10,9... | collective-permute-start | bytes 110600 | tf_op jit(solution)/shard_map/ppermute | solution.py:427
  20.8 3.3 %collective-permute-start.6 = (f32[24,128]{1,0:T(8,128)S(1)}, f32[24,128]{1,0:T(8,128)S(1)}, u32[]{:S(2)}, u32[]{:S(2)}) collective-permute-start(f32[24,128]{1,0:T(8,128)S(1)} %get-tuple-element.42), channel_id=1, source_target_pairs={{0,15},{1,8},{2,9},{3,10},{4,11},{5,12},{6,13},{7,14},{8,7},{9,0},... | collective-permute-start | bytes 36872 | tf_op jit(solution)/shard_map/ppermute | solution.py:428
  22.0 2.1 %collective-permute-start.7 = (f32[24,128]{1,0:T(8,128)S(1)}, f32[24,128]{1,0:T(8,128)S(1)}, u32[]{:S(2)}, u32[]{:S(2)}) collective-permute-start(f32[24,128]{1,0:T(8,128)S(1)} %get-tuple-element.42), channel_id=1, source_target_pairs={{0,8},{8,0},{16,24},{24,16},{32,40},{40,32},{48,56},{56,48},{64,72... | collective-permute-start | bytes 36872 | tf_op jit(solution)/shard_map/ppermute | solution.py:374
  24.1 5.8 %collective-permute-start.8 = (f32[64,128]{1,0:T(8,128)S(1)}, f32[64,128]{1,0:T(8,128)S(1)}, u32[]{:S(2)}, u32[]{:S(2)}) collective-permute-start(f32[64,128]{1,0:T(8,128)S(1)} %pad_maximum_fusion), channel_id=1, source_target_pairs={{8,16},{16,8},{24,32},{32,24},{40,48},{48,40},{56,64},{64,56},{72,... | collective-permute-start | bytes 98312 | tf_op jit(solution)/shard_map/ppermute | solution.py:433
  30.3 1.2 %collective-permute-start.9 = (f32[8,128]{1,0:T(8,128)S(1)}, f32[8,128]{1,0:T(8,128)S(1)}, u32[]{:S(2)}, u32[]{:S(2)}) collective-permute-start(f32[8,128]{1,0:T(8,128)S(1)} %get-tuple-element.46.after.rho_own), channel_id=1, source_target_pairs={{0,8},{8,0},{16,24},{24,16},{32,40},{40,32},{48,56},{56,48},{64,72... | collective-permute-start | bytes 12296 | tf_op jit(solution)/shard_map/ppermute | solution.py:374

commit v9 on v8

--- a/solution.py
+++ b/solution.py
@@ -30,12 +30,7 @@
 NEAR = [(dr, dc) for dr in (-1, 0, 1) for dc in (-1, 0, 1)]
 
 
-def pack_kernel(count, pos, vel, mass, nb, dest, shell, stress, rate, couple, out, half, first, home, soil):
-    soil[0:4] = stress[...]
-    soil[4:7] = rate[...]
-    soil[7:10] = couple[...]
-    home[0:CELLS, :] = dest[...]
-    home[CELLS : 2 * CELLS, :] = shell[...]
+def pack_kernel(count, pos, vel, mass, nb, out, half, first):
     lane = lax.broadcasted_iota(jnp.int32, (1, S), 1)
     out[0 : 2 * CELLS, :] = pos[...]
     out[PVX * CELLS : (PVX + 2) * CELLS, :] = vel[...]
@@ -197,7 +192,12 @@
     return [(left, HALF + NB * c) for c in range(3)] + [(first, 0), (send, HALF), (send, HALF + NB)]
 
 
-def early_first_kernel(parity, frame, other, left, first, send, out):
+def early_first_kernel(parity, frame, other, left, first, send, dest, shell, stress, rate, couple, out, home, soil):
+    home[0:CELLS, :] = dest[...]
+    home[CELLS : 2 * CELLS, :] = shell[...]
+    soil[0:4] = stress[...]
+    soil[4:7] = rate[...]
+    soil[7:10] = couple[...]
     early(parity, {0: frame, 1: other}, lists_first(left, first, send), out)
 
 
@@ -373,17 +373,15 @@
     def swapped(a):
         return lax.ppermute(a, "depth", pairs)
 
-    send, half, first, home, soil = pl.pallas_call(
+    send, half, first = pl.pallas_call(
         pack_kernel,
         out_shape=(
             kept(HALF + 3 * NB),
             kept(HALF),
             kept(NB),
-            pltpu.VMEM((2 * CELLS, S), jnp.int32),
-            pltpu.VMEM((10,) + soil_stress.shape[1:], jnp.float32),
         ),
-        in_specs=[SM] + [VM] * 9,
-        out_specs=(VM,) * 5,
+        in_specs=[SM] + [VM] * 4,
+        out_specs=(VM,) * 3,
         name="pack",
     )(
         cell_count,
@@ -391,11 +389,6 @@
         fluid_vel.reshape(2 * CELLS, S),
         fluid_mass.reshape(CELLS, S),
         nb_list.reshape(NB * CELLS, S),
-        iface_dest.reshape(CELLS, S),
-        iface_shell.reshape(CELLS, S),
-        soil_stress,
-        soil_rate,
-        soil_couple,
     )
     left = lax.ppermute(send, "azim", toward_right)
     across = lax.ppermute(half, ("depth", "azim"), crossing(1))
@@ -407,9 +400,18 @@
         jnp.concatenate([frame[:SENT], other[:PLACE], left[HALF:], first, send[HALF:]], axis=0), "depth", facing
     )
     tiles = CELLS * NT
-    (gathered,) = call(
-        early_first_kernel, "early_first", (RING * NT * EARLY,), frame, other, left, first, send
-    )
+    later = (iface_dest.reshape(CELLS, S), iface_shell.reshape(CELLS, S), soil_stress, soil_rate, soil_couple)
+    gathered, home, soil = pl.pallas_call(
+        early_first_kernel,
+        out_shape=(
+            kept(RING * NT * EARLY),
+            pltpu.VMEM((2 * CELLS, S), jnp.int32),
+            pltpu.VMEM((10,) + soil_stress.shape[1:], jnp.float32),
+        ),
+        in_specs=[SM] + [VM] * 10,
+        out_specs=(VM,) * 3,
+        name="early_first",
+    )(parity, *[held(a) for a in (frame, other, left, first, send)], *later)
     rho_own, pair = call(
         middle_first_kernel, "middle_first", (WIDE, tiles * PAIR), frame, outer, left, first, send, gathered
     )

time: 53.1 us -> 53.1 us (level)
  waiting for transfers between devices: 11.4 us -> 10.6 us
  Pallas kernels: 5.99 us -> 6.77 us
    pallas_call x0 -> x1, Pallas kernels: none -> 1.28 us  [local(): pl.pallas_call(early_first_kernel, out_shape=(kept(RING * NT * EARLY), pl...]
    ppermute x1, waiting for transfers between devices: 2.52 us -> 1.7 us  [local(): lax.ppermute(jnp.concatenate([frame[:SENT], other[:PLACE], left[HALF:], f...]
    pallas_call x8 -> x7, Pallas kernels: 4.33 us -> 3.86 us  [call(): pl.pallas_call(kernel, out_shape=tuple((kept(n) for n in shapes)), in_spe...]
  transfers between devices with their start and end apart: 10 -> 10, of which waited for: 6 -> 6; matrix products, arithmetic and copies ran while one was open for 0% -> 0% of each run, Pallas kernels for 5% -> 7%
where the time goes in v9:
time: 53.1 us; the launch traced here: 52.8 us
  blocking collectives  19.9 us (37%)
  starting transfers between devices  14.6 us (27%)
  waiting for transfers between devices  10.6 us (20%)
  Pallas kernels  6.77 us (13%)
  between operations  0.82 us (2%)
    all_to_all x1, blocking collectives, local(): lax.all_to_all(part, ('depth', 'azim'), split_axis=0, concat_axis=0, tile...  19.9 us
    ppermute x1, waiting for transfers between devices, local(): across = lax.ppermute(half, ('depth', 'azim'), crossing(1))  5.29 us
    ppermute x1, starting transfers between devices, local(): lax.ppermute(jnp.concatenate([frame[:SENT], other[:PLACE]], axis=0), 'dep...  4.25 us
    pallas_call x7, Pallas kernels, call(): pl.pallas_call(kernel, out_shape=tuple((kept(n) for n in shapes)), in_spe...  3.86 us
    ppermute x1, starting transfers between devices, local(): lax.ppermute(jnp.concatenate([frame[:SENT], other[:PLACE], left[HALF:], f...  3.77 us
    ppermute x1, starting transfers between devices, local(): left = lax.ppermute(send, 'azim', toward_right)  2.11 us
    ppermute x1, waiting for transfers between devices, local(): across = lax.ppermute(half, ('depth', 'azim'), crossing(-1))  2.07 us
    ppermute x1, starting transfers between devices, local(): across = lax.ppermute(half, ('depth', 'azim'), crossing(1))  2.05 us
  transfers between devices with their start and end apart: 10, of which 6 were waited for; matrix products, arithmetic and copies ran while one was open for 0% of the time, Pallas kernels for 7%

profile of v9, /device:TPU:1, one launch (start us, length us, event | category | flops | bytes accessed | tf_op | source)
XLA Modules:
  0.0 52.8 jit_solution(16014752804300293254)
XLA Ops:
  0.6 0.9 %pack.1 = (f32[96,128]{1,0:T(8,128)S(1)}, f32[24,128]{1,0:T(8,128)S(1)}, f32[24,128]{1,0:T(8,128)S(1)}) custom-call(s32[1,4]{1,0:T(1,128)} %count.1, f32[8,128]{1,0:T(8,128)} %bitcast.65, f32[8,128]{1,0:T(8,128)} %bitcast.66, f32[4,128]{1,0:T(4,128)} %bitcast.69, s32[96,128]{1,0:T(8,128)} %bitcast.56), custom_call_target="tpu_custom_call" | custom-call | tf_op jit(solution)/shard_map/pack/pallas_call | solution.py:376
  1.5 2.1 %collective-permute-start = (f32[96,128]{1,0:T(8,128)S(1)}, f32[96,128]{1,0:T(8,128)S(1)}, u32[]{:S(2)}, u32[]{:S(2)}) collective-permute-start(f32[96,128]{1,0:T(8,128)S(1)} %get-tuple-element.32.send), channel_id=1, source_target_pairs={{0,1},{1,2},{2,3},{3,4},{4,5},{5,6},{6,7},{7,0},{8,9},{9,10},{10,1... | collective-permute-start | bytes 147464 | tf_op jit(solution)/shard_map/ppermute | solution.py:393
  3.6 2.1 %collective-permute-start.1 = (f32[24,128]{1,0:T(8,128)S(1)}, f32[24,128]{1,0:T(8,128)S(1)}, u32[]{:S(2)}, u32[]{:S(2)}) collective-permute-start(f32[24,128]{1,0:T(8,128)S(1)} %get-tuple-element.33), channel_id=1, source_target_pairs={{0,9},{1,10},{2,11},{3,12},{4,13},{5,14},{6,15},{7,8},{8,1},{9,2},... | collective-permute-start | bytes 36872 | tf_op jit(solution)/shard_map/ppermute | solution.py:394
  5.7 0.0 collective-permute-start.2
  5.7 5.3 %collective-permute-done.1 = f32[24,128]{1,0:T(8,128)S(1)} collective-permute-done((f32[24,128]{1,0:T(8,128)S(1)}, f32[24,128]{1,0:T(8,128)S(1)}, u32[]{:S(2)}, u32[]{:S(2)}) %collective-permute-start.1) | collective-permute-done | bytes 12320 | tf_op jit(solution)/shard_map/ppermute | solution.py:394
  11.0 0.0 collective-permute-done.left
  11.0 0.0 collective-permute-done.2
  11.0 3.8 %collective-permute-start.3 = (f32[232,128]{1,0:T(8,128)S(1)}, f32[232,128]{1,0:T(8,128)S(1)}, u32[]{:S(2)}, u32[]{:S(2)}) collective-permute-start(f32[232,128]{1,0:T(8,128)S(1)} %slice_dynamic-update-slice_fusion), channel_id=1, source_target_pairs={{8,16},{16,8},{24,32},{32,24},{40,48},{48,40},{56,64},{64,56},{72,... | collective-permute-start | bytes 356360 | tf_op jit(solution)/shard_map/ppermute | solution.py:399
  14.9 1.3 %early_first.1 = (f32[432,128]{1,0:T(8,128)S(1)}, s32[8,128]{1,0:T(8,128)S(1)}, f32[10,16,128]{2,1,0:T(8,128)S(1)}) custom-call(s32[1]{0:T(128)} %bitcast.parity, f32[48,128]{1,0:T(8,128)S(1)} %fusion.3.frame, f32[48,128]{1,0:T(8,128)S(1)} %fusion.2.other, f32[96,128]{1,0:T(8,128)S(1)} %collective-permute-done.left, f32[24,128]{1,0:T(8,128)S(1)} %get-tuple-element.36.first, ...), custom_call_target="tpu_custom_call" | custom-call | tf_op jit(solution)/shard_map/early_first/pallas_call | solution.py:404
  16.2 1.7 %collective-permute-done.3.outer.before = f32[232,128]{1,0:T(8,128)S(1)} collective-permute-done((f32[232,128]{1,0:T(8,128)S(1)}, f32[232,128]{1,0:T(8,128)S(1)}, u32[]{:S(2)}, u32[]{:S(2)}) %collective-permute-start.3) | collective-permute-done | bytes 118816 | tf_op jit(solution)/shard_map/ppermute | solution.py:399
  17.9 0.3 middle_first.1
  18.2 0.1 collective-permute-start.4
  18.3 0.9 %outer_first.1 = (f32[8,128]{1,0:T(8,128)S(1)}, f32[96,128]{1,0:T(8,128)S(1)}) custom-call(s32[1]{0:T(128)} %bitcast.parity, f32[48,128]{1,0:T(8,128)S(1)} %fusion.3.frame, f32[48,128]{1,0:T(8,128)S(1)} %fusion.2.other, f32[232,128]{1,0:T(8,128)S(1)} %collective-permute-done.3.outer.before, f32[96,128]{1,0:T(8,128)S(1)} %collective-permute-done.left, ...), custom_call_target="tpu_custom_call" | custom-call | tf_op jit(solution)/shard_map/outer_first/pallas_call | solution.py:356
  19.2 0.2 collective-permute-done.4.rho_other
  19.4 0.3 force_first.1
  19.7 1.0 %collective-permute-start.5 = (f32[72,128]{1,0:T(8,128)S(1)}, f32[72,128]{1,0:T(8,128)S(1)}, u32[]{:S(2)}, u32[]{:S(2)}) collective-permute-start(f32[72,128]{1,0:T(8,128)S(1)} %get-tuple-element.43), channel_id=1, source_target_pairs={{0,7},{1,0},{2,1},{3,2},{4,3},{5,4},{6,5},{7,6},{8,15},{9,8},{10,9... | collective-permute-start | bytes 110600 | tf_op jit(solution)/shard_map/ppermute | solution.py:429
  20.7 1.2 %collective-permute-start.6 = (f32[24,128]{1,0:T(8,128)S(1)}, f32[24,128]{1,0:T(8,128)S(1)}, u32[]{:S(2)}, u32[]{:S(2)}) collective-permute-start(f32[24,128]{1,0:T(8,128)S(1)} %get-tuple-element.44), channel_id=1, source_target_pairs={{0,15},{1,8},{2,9},{3,10},{4,11},{5,12},{6,13},{7,14},{8,7},{9,0},... | collective-permute-start | bytes 36872 | tf_op jit(solution)/shard_map/ppermute | solution.py:430
  22.0 0.0 collective-permute-start.7
  22.0 2.1 %collective-permute-done.6 = f32[24,128]{1,0:T(8,128)S(1)} collective-permute-done((f32[24,128]{1,0:T(8,128)S(1)}, f32[24,128]{1,0:T(8,128)S(1)}, u32[]{:S(2)}, u32[]{:S(2)}) %collective-permute-start.6) | collective-permute-done | bytes 12320 | tf_op jit(solution)/shard_map/ppermute | solution.py:430
  24.0 0.0 collective-permute-done.5.right
  24.0 0.0 collective-permute-done.7
  24.1 4.2 %collective-permute-start.8 = (f32[64,128]{1,0:T(8,128)S(1)}, f32[64,128]{1,0:T(8,128)S(1)}, u32[]{:S(2)}, u32[]{:S(2)}) collective-permute-start(f32[64,128]{1,0:T(8,128)S(1)} %pad_maximum_fusion), channel_id=1, source_target_pairs={{8,16},{16,8},{24,32},{32,24},{40,48},{48,40},{56,64},{64,56},{72,... | collective-permute-start | bytes 98312 | tf_op jit(solution)/shard_map/ppermute | solution.py:435
  28.4 0.5 early_second.1.gathered
  28.9 1.1 %collective-permute-done.8.outer = f32[64,128]{1,0:T(8,128)S(1)} collective-permute-done((f32[64,128]{1,0:T(8,128)S(1)}, f32[64,128]{1,0:T(8,128)S(1)}, u32[]{:S(2)}, u32[]{:S(2)}) %collective-permute-start.8) | collective-permute-done | bytes 32800 | tf_op jit(solution)/shard_map/ppermute | solution.py:435
  29.9 0.3 middle_second.1
  30.3 0.1 collective-permute-start.9
  30.4 0.9 %outer_second.1 = (f32[8,128]{1,0:T(8,128)S(1)}, f32[96,128]{1,0:T(8,128)S(1)}) custom-call(s32[1]{0:T(128)} %bitcast.parity, f32[48,128]{1,0:T(8,128)S(1)} %fusion.1.frame, f32[48,128]{1,0:T(8,128)S(1)} %fusion.other, f32[64,128]{1,0:T(8,128)S(1)} %collective-permute-done.8.outer, f32[72,128]{1,0:T(8,128)S(1)} %collective-permute-done.5.right, ...), custom_call_target="tpu_custom_call" | custom-call | tf_op jit(solution)/shard_map/outer_second/pallas_call | solution.py:356
  31.3 0.2 collective-permute-done.9.rho_other
  31.5 0.6 %force_second.1 = (f32[8,128]{1,0:T(8,128)S(1)}, f32[8,128]{1,0:T(8,128)S(1)}, f32[4,128]{1,0:T(4,128)S(1)}, f32[128,128]{1,0:T(8,128)S(1)}) custom-call(s32[1]{0:T(128)} %bitcast.parity, s32[8,128]{1,0:T(8,128)S(1)} %get-tuple-element.37.home, f32[48,128]{1,0:T(8,128)S(1)} %fusion.1.frame, f32[8,128]{1,0:T(8,128)S(1)} %get-tuple-element.49.rho_outer, ...), custom_call_target="tpu_custom_call" | custom-call | tf_op jit(solution)/shard_map/force_second/pallas_call | solution.py:356
  32.1 19.9 %all_to_all.11 = f32[128,1,128]{2,1,0:T(1,128)S(1)} all-to-all(f32[128,1,128]{2,1,0:T(1,128)S(1)} %bitcast.47), channel_id=1, replica_groups=mesh['depth'=16,'azim'=8] {'depth','azim'}, dimensions={0} | all-to-all | bytes 131072 | tf_op jit(solution)/shard_map/all_to_all | solution.py:456
  52.1 0.8 %soil.1 = (f32[4,16,128]{2,1,0:T(8,128)}, f32[8,128]{1,0:T(8,128)}, f32[8,128]{1,0:T(8,128)}, f32[4,128]{1,0:T(4,128)}) custom-call(f32[128,128]{1,0:T(8,128)S(1)} %bitcast.46, f32[10,16,128]{2,1,0:T(8,128)S(1)} %get-tuple-element.52.soil, f32[8,128]{1,0:T(8,128)S(1)} %get-tuple-element.53.pos, f32[8,128]{1,0:T(8,128)S(1)} %get-tuple-element.54.vel, ...), custom_call_target="tpu_custom_call" | custom-call | tf_op jit(solution)/shard_map/soil/pallas_call | solution.py:457
  (16 shorter events, 0.1 us)
Async XLA Ops:
  1.5 9.5 %collective-permute-start = (f32[96,128]{1,0:T(8,128)S(1)}, f32[96,128]{1,0:T(8,128)S(1)}, u32[]{:S(2)}, u32[]{:S(2)}) collective-permute-start(f32[96,128]{1,0:T(8,128)S(1)} %get-tuple-element.32.send), channel_id=1, source_target_pairs={{0,1},{1,2},{2,3},{3,4},{4,5},{5,6},{6,7},{7,0},{8,9},{9,10},{10,1... | collective-permute-start | bytes 147464 | tf_op jit(solution)/shard_map/ppermute | solution.py:393
  3.6 7.3 %collective-permute-start.1 = (f32[24,128]{1,0:T(8,128)S(1)}, f32[24,128]{1,0:T(8,128)S(1)}, u32[]{:S(2)}, u32[]{:S(2)}) collective-permute-start(f32[24,128]{1,0:T(8,128)S(1)} %get-tuple-element.33), channel_id=1, source_target_pairs={{0,9},{1,10},{2,11},{3,12},{4,13},{5,14},{6,15},{7,8},{8,1},{9,2},... | collective-permute-start | bytes 36872 | tf_op jit(solution)/shard_map/ppermute | solution.py:394
  5.7 5.3 %collective-permute-start.2 = (f32[24,128]{1,0:T(8,128)S(1)}, f32[24,128]{1,0:T(8,128)S(1)}, u32[]{:S(2)}, u32[]{:S(2)}) collective-permute-start(f32[24,128]{1,0:T(8,128)S(1)} %get-tuple-element.33), channel_id=1, source_target_pairs={{0,8},{8,0},{16,24},{24,16},{32,40},{40,32},{48,56},{56,48},{64,72... | collective-permute-start | bytes 36872 | tf_op jit(solution)/shard_map/ppermute | solution.py:374
  11.0 6.8 %collective-permute-start.3 = (f32[232,128]{1,0:T(8,128)S(1)}, f32[232,128]{1,0:T(8,128)S(1)}, u32[]{:S(2)}, u32[]{:S(2)}) collective-permute-start(f32[232,128]{1,0:T(8,128)S(1)} %slice_dynamic-update-slice_fusion), channel_id=1, source_target_pairs={{8,16},{16,8},{24,32},{32,24},{40,48},{48,40},{56,64},{64,56},{72,... | collective-permute-start | bytes 356360 | tf_op jit(solution)/shard_map/ppermute | solution.py:399
  18.2 1.2 %collective-permute-start.4 = (f32[8,128]{1,0:T(8,128)S(1)}, f32[8,128]{1,0:T(8,128)S(1)}, u32[]{:S(2)}, u32[]{:S(2)}) collective-permute-start(f32[8,128]{1,0:T(8,128)S(1)} %get-tuple-element.40.after.rho_own), channel_id=1, source_target_pairs={{0,8},{8,0},{16,24},{24,16},{32,40},{40,32},{48,56},{56,48},{64,72... | collective-permute-start | bytes 12296 | tf_op jit(solution)/shard_map/ppermute | solution.py:374
  19.7 4.3 %collective-permute-start.5 = (f32[72,128]{1,0:T(8,128)S(1)}, f32[72,128]{1,0:T(8,128)S(1)}, u32[]{:S(2)}, u32[]{:S(2)}) collective-permute-start(f32[72,128]{1,0:T(8,128)S(1)} %get-tuple-element.43), channel_id=1, source_target_pairs={{0,7},{1,0},{2,1},{3,2},{4,3},{5,4},{6,5},{7,6},{8,15},{9,8},{10,9... | collective-permute-start | bytes 110600 | tf_op jit(solution)/shard_map/ppermute | solution.py:429
  20.7 3.3 %collective-permute-start.6 = (f32[24,128]{1,0:T(8,128)S(1)}, f32[24,128]{1,0:T(8,128)S(1)}, u32[]{:S(2)}, u32[]{:S(2)}) collective-permute-start(f32[24,128]{1,0:T(8,128)S(1)} %get-tuple-element.44), channel_id=1, source_target_pairs={{0,15},{1,8},{2,9},{3,10},{4,11},{5,12},{6,13},{7,14},{8,7},{9,0},... | collective-permute-start | bytes 36872 | tf_op jit(solution)/shard_map/ppermute | solution.py:430
  22.0 2.1 %collective-permute-start.7 = (f32[24,128]{1,0:T(8,128)S(1)}, f32[24,128]{1,0:T(8,128)S(1)}, u32[]{:S(2)}, u32[]{:S(2)}) collective-permute-start(f32[24,128]{1,0:T(8,128)S(1)} %get-tuple-element.44), channel_id=1, source_target_pairs={{0,8},{8,0},{16,24},{24,16},{32,40},{40,32},{48,56},{56,48},{64,72... | collective-permute-start | bytes 36872 | tf_op jit(solution)/shard_map/ppermute | solution.py:374
  24.1 5.8 %collective-permute-start.8 = (f32[64,128]{1,0:T(8,128)S(1)}, f32[64,128]{1,0:T(8,128)S(1)}, u32[]{:S(2)}, u32[]{:S(2)}) collective-permute-start(f32[64,128]{1,0:T(8,128)S(1)} %pad_maximum_fusion), channel_id=1, source_target_pairs={{8,16},{16,8},{24,32},{32,24},{40,48},{48,40},{56,64},{64,56},{72,... | collective-permute-start | bytes 98312 | tf_op jit(solution)/shard_map/ppermute | solution.py:435
  30.3 1.2 %collective-permute-start.9 = (f32[8,128]{1,0:T(8,128)S(1)}, f32[8,128]{1,0:T(8,128)S(1)}, u32[]{:S(2)}, u32[]{:S(2)}) collective-permute-start(f32[8,128]{1,0:T(8,128)S(1)} %get-tuple-element.48.after.rho_own), channel_id=1, source_target_pairs={{0,8},{8,0},{16,24},{24,16},{32,40},{40,32},{48,56},{56,48},{64,72... | collective-permute-start | bytes 12296 | tf_op jit(solution)/shard_map/ppermute | solution.py:374

commit v10 on v8

--- a/solution.py
+++ b/solution.py
@@ -229,8 +229,11 @@
     return [(left, HALF + 2 * NB), (first, 0)] + [(send, HALF + NB * c) for c in range(3)] + [(right, HALF + NB)]
 
 
-def early_second_kernel(parity, frame, other, right, left, first, send, out):
+def early_second_kernel(parity, frame, other, right, left, first, send, home, out, owners):
     early(parity, {0: frame, 1: other}, lists_second(right, left, first, send), out)
+    devices = lax.broadcasted_iota(jnp.int32, (S, S), 0)
+    for c in range(CELLS):
+        owners[:, S * c : S * (c + 1)] = (devices == home[c : c + 1, :]).astype(jnp.bfloat16)
 
 
 def middle_second_kernel(parity, frame, outer, right, left, first, send, gathered, rho, pair):
@@ -245,13 +248,12 @@
 
 
 def force_second_kernel(
-    parity, home, frame, rho_outer, rho_own, rho_other, first, send, pair, dragged, pos_out, vel_out, rho_out, part
+    parity, home, frame, rho_outer, rho_own, rho_other, first, send, pair, dragged, owners, pos_out, vel_out, rho_out, part
 ):
     numbers = numbers_of(parity)
     lists = [(first, 0), (send, HALF), (send, HALF + NB), (send, HALF + 2 * NB)]
-    devices = lax.broadcasted_iota(jnp.int32, (S, S), 0)
     shells = lax.broadcasted_iota(jnp.int32, (16, S), 0)
-    owners, shares = [], []
+    shares = [[], [], []]
     for c in range(CELLS):
         (x, y, m, vx, vy, live), rho = force(
             c, numbers, frame, {-1: rho_outer, 0: rho_own, 1: rho_other}, lists[c], pair, dragged
@@ -262,21 +264,22 @@
         vel_out[CELLS + c : CELLS + c + 1, :] = vy
         rho_out[c : c + 1, :] = rho
         loads = (m * vx, m * vy, m * (sound_sq * (rho - 1.0)), 0.5 * m * (vx * vx + vy * vy))
-        owner = (devices == home[c : c + 1, :]).astype(jnp.bfloat16)
         member = shells == home[CELLS + c : CELLS + c + 1, :]
         rest = jnp.concatenate([jnp.where(member, load, 0.0) for load in loads], axis=0)
-        for _ in range(3):
-            some = rest.astype(jnp.bfloat16)
-            owners.append(owner)
-            shares.append(some)
-            rest = rest - some.astype(jnp.float32)
+        for share in shares:
+            share.append(rest.astype(jnp.bfloat16))
+            rest = rest - share[-1].astype(jnp.float32)
+    high, middle, low = [jnp.concatenate(share, axis=1) for share in shares]
+    none = jnp.zeros_like(low)
     total = lax.dot_general(
-        jnp.concatenate(owners, axis=1),
-        jnp.concatenate(shares, axis=1),
+        jnp.concatenate([owners[...], owners[...]], axis=1),
+        jnp.concatenate(
+            [jnp.concatenate(pair_of, axis=1) for pair_of in ((high, low), (none, none), (middle, none), (none, none))], axis=0
+        ),
         (((1,), (1,)), ((), ())),
         preferred_element_type=jnp.float32,
     )
-    part[...] = jnp.concatenate([total, jnp.zeros((S, S - 64), jnp.float32)], axis=1)
+    part[...] = total[:, :S] + total[:, S:]
 
 
 def soil_kernel(arrived, soil, pos, vel, rho, stress_out, pos_out, vel_out, rho_out):
@@ -355,7 +358,7 @@
     def call(kernel, name, shapes, *args):
         return pl.pallas_call(
             kernel,
-            out_shape=tuple(kept(n) for n in shapes),
+            out_shape=tuple(kept(n) if isinstance(n, int) else n for n in shapes),
             in_specs=[SM] + [VM] * len(args),
             out_specs=(VM,) * len(shapes),
             name=name,
@@ -431,8 +434,11 @@
     frame = merged(mid, right)
     other = merged(beside, across)
     beyond = lax.ppermute(jnp.concatenate([frame[:SENT], other[:PLACE]], axis=0), "depth", facing)
-    (gathered,) = call(
-        early_second_kernel, "early_second", (RING * NT * EARLY,), frame, other, right, left, first, send
+    gathered, owners = call(
+        early_second_kernel,
+        "early_second",
+        (RING * NT * EARLY, pltpu.VMEM((S, CELLS * S), jnp.bfloat16)),
+        frame, other, right, left, first, send, home,
     )
     rho_own, pair = call(
         middle_second_kernel, "middle_second", (WIDE, tiles * PAIR), frame, beyond, right, left, first, send, gathered
@@ -448,7 +454,7 @@
         force_second_kernel,
         "force_second",
         (2 * CELLS, 2 * CELLS, CELLS, S),
-        home, frame, rho_outer, rho_own, rho_other, first, send, pair, dragged,
+        home, frame, rho_outer, rho_own, rho_other, first, send, pair, dragged, owners,
     )
 
     arrived = lax.all_to_all(part, ("depth", "azim"), split_axis=0, concat_axis=0, tiled=True)

time: 53.1 us -> 53.1 us (level)
  no operation moved by 1% of the time
where the time goes in v10:
time: 53.1 us; the launch traced here: 52.9 us
  blocking collectives  19.9 us (37%)
  starting transfers between devices  14.6 us (27%)
  waiting for transfers between devices  11.4 us (21%)
  Pallas kernels  6.01 us (11%)
  between operations  0.82 us (2%)
    all_to_all x1, blocking collectives, local(): lax.all_to_all(part, ('depth', 'azim'), split_axis=0, concat_axis=0, tile...  19.9 us
    ppermute x1, waiting for transfers between devices, local(): across = lax.ppermute(half, ('depth', 'azim'), crossing(1))  5.29 us
    pallas_call x8, Pallas kernels, call(): pl.pallas_call(kernel, out_shape=tuple((kept(n) if isinstance(n, int) els...  4.35 us
    ppermute x1, starting transfers between devices, local(): lax.ppermute(jnp.concatenate([frame[:SENT], other[:PLACE]], axis=0), 'dep...  4.25 us
    ppermute x1, starting transfers between devices, local(): lax.ppermute(jnp.concatenate([frame[:SENT], other[:PLACE], left[HALF:], f...  3.77 us
    ppermute x1, waiting for transfers between devices, local(): lax.ppermute(jnp.concatenate([frame[:SENT], other[:PLACE], left[HALF:], f...  2.52 us
    ppermute x1, starting transfers between devices, local(): left = lax.ppermute(send, 'azim', toward_right)  2.11 us
    ppermute x1, waiting for transfers between devices, local(): across = lax.ppermute(half, ('depth', 'azim'), crossing(-1))  2.07 us
  transfers between devices with their start and end apart: 10, of which 6 were waited for; matrix products, arithmetic and copies ran while one was open for 0% of the time, Pallas kernels for 5%

profile of v10, /device:TPU:1, one launch (start us, length us, event | category | flops | bytes accessed | tf_op | source)
XLA Modules:
  0.0 52.9 jit_solution(9874192557132544547)
XLA Ops:
  0.6 0.9 %pack.1 = (f32[96,128]{1,0:T(8,128)S(1)}, f32[24,128]{1,0:T(8,128)S(1)}, f32[24,128]{1,0:T(8,128)S(1)}, s32[8,128]{1,0:T(8,128)S(1)}, f32[10,16,128]{2,1,0:T(8,128)S(1)}) custom-call(s32[1,4]{1,0:T(1,128)} %count.1, f32[8,128]{1,0:T(8,128)} %bitcast.65, f32[8,128]{1,0:T(8,128)} %bitcast.66, f32[4,128]{1,0:T(4,128)} %bitcast.67, s32[96,128]{1,0:T(8,128)} %bitcast.56, ...), custom_call_target="tpu_custom_call" | custom-call | tf_op jit(solution)/shard_map/pack/pallas_call | solution.py:379
  1.5 2.1 %collective-permute-start = (f32[96,128]{1,0:T(8,128)S(1)}, f32[96,128]{1,0:T(8,128)S(1)}, u32[]{:S(2)}, u32[]{:S(2)}) collective-permute-start(f32[96,128]{1,0:T(8,128)S(1)} %get-tuple-element.34.send), channel_id=1, source_target_pairs={{0,1},{1,2},{2,3},{3,4},{4,5},{5,6},{6,7},{7,0},{8,9},{9,10},{10,1... | collective-permute-start | bytes 147464 | tf_op jit(solution)/shard_map/ppermute | solution.py:403
  3.7 2.1 %collective-permute-start.1 = (f32[24,128]{1,0:T(8,128)S(1)}, f32[24,128]{1,0:T(8,128)S(1)}, u32[]{:S(2)}, u32[]{:S(2)}) collective-permute-start(f32[24,128]{1,0:T(8,128)S(1)} %get-tuple-element.35), channel_id=1, source_target_pairs={{0,9},{1,10},{2,11},{3,12},{4,13},{5,14},{6,15},{7,8},{8,1},{9,2},... | collective-permute-start | bytes 36872 | tf_op jit(solution)/shard_map/ppermute | solution.py:404
  5.7 0.0 collective-permute-start.2
  5.7 5.3 %collective-permute-done.1 = f32[24,128]{1,0:T(8,128)S(1)} collective-permute-done((f32[24,128]{1,0:T(8,128)S(1)}, f32[24,128]{1,0:T(8,128)S(1)}, u32[]{:S(2)}, u32[]{:S(2)}) %collective-permute-start.1) | collective-permute-done | bytes 12320 | tf_op jit(solution)/shard_map/ppermute | solution.py:404
  11.0 0.0 collective-permute-done.left
  11.0 0.0 collective-permute-done.2
  11.1 3.8 %collective-permute-start.3 = (f32[232,128]{1,0:T(8,128)S(1)}, f32[232,128]{1,0:T(8,128)S(1)}, u32[]{:S(2)}, u32[]{:S(2)}) collective-permute-start(f32[232,128]{1,0:T(8,128)S(1)} %slice_dynamic-update-slice_fusion), channel_id=1, source_target_pairs={{8,16},{16,8},{24,32},{32,24},{40,48},{48,40},{56,64},{64,56},{72,... | collective-permute-start | bytes 356360 | tf_op jit(solution)/shard_map/ppermute | solution.py:409
  14.9 0.5 early_first.1.gathered
  15.4 2.5 %collective-permute-done.3.outer.before = f32[232,128]{1,0:T(8,128)S(1)} collective-permute-done((f32[232,128]{1,0:T(8,128)S(1)}, f32[232,128]{1,0:T(8,128)S(1)}, u32[]{:S(2)}, u32[]{:S(2)}) %collective-permute-start.3) | collective-permute-done | bytes 118816 | tf_op jit(solution)/shard_map/ppermute | solution.py:409
  17.9 0.3 middle_first.1
  18.2 0.1 collective-permute-start.4
  18.3 0.9 %outer_first.1 = (f32[8,128]{1,0:T(8,128)S(1)}, f32[96,128]{1,0:T(8,128)S(1)}) custom-call(s32[1]{0:T(128)} %bitcast.parity, f32[48,128]{1,0:T(8,128)S(1)} %fusion.3.frame, f32[48,128]{1,0:T(8,128)S(1)} %fusion.2.other, f32[232,128]{1,0:T(8,128)S(1)} %collective-permute-done.3.outer.before, f32[96,128]{1,0:T(8,128)S(1)} %collective-permute-done.left, ...), custom_call_target="tpu_custom_call" | custom-call | tf_op jit(solution)/shard_map/outer_first/pallas_call | solution.py:359
  19.3 0.2 collective-permute-done.4.rho_other
  19.5 0.3 force_first.1
  19.8 1.0 %collective-permute-start.5 = (f32[72,128]{1,0:T(8,128)S(1)}, f32[72,128]{1,0:T(8,128)S(1)}, u32[]{:S(2)}, u32[]{:S(2)}) collective-permute-start(f32[72,128]{1,0:T(8,128)S(1)} %get-tuple-element.43), channel_id=1, source_target_pairs={{0,7},{1,0},{2,1},{3,2},{4,3},{5,4},{6,5},{7,6},{8,15},{9,8},{10,9... | collective-permute-start | bytes 110600 | tf_op jit(solution)/shard_map/ppermute | solution.py:430
  20.8 1.2 %collective-permute-start.6 = (f32[24,128]{1,0:T(8,128)S(1)}, f32[24,128]{1,0:T(8,128)S(1)}, u32[]{:S(2)}, u32[]{:S(2)}) collective-permute-start(f32[24,128]{1,0:T(8,128)S(1)} %get-tuple-element.44), channel_id=1, source_target_pairs={{0,15},{1,8},{2,9},{3,10},{4,11},{5,12},{6,13},{7,14},{8,7},{9,0},... | collective-permute-start | bytes 36872 | tf_op jit(solution)/shard_map/ppermute | solution.py:431
  22.0 0.0 collective-permute-start.7
  22.0 2.1 %collective-permute-done.6 = f32[24,128]{1,0:T(8,128)S(1)} collective-permute-done((f32[24,128]{1,0:T(8,128)S(1)}, f32[24,128]{1,0:T(8,128)S(1)}, u32[]{:S(2)}, u32[]{:S(2)}) %collective-permute-start.6) | collective-permute-done | bytes 12320 | tf_op jit(solution)/shard_map/ppermute | solution.py:431
  24.1 0.0 collective-permute-done.5.right
  24.1 0.0 collective-permute-done.7
  24.1 4.2 %collective-permute-start.8 = (f32[64,128]{1,0:T(8,128)S(1)}, f32[64,128]{1,0:T(8,128)S(1)}, u32[]{:S(2)}, u32[]{:S(2)}) collective-permute-start(f32[64,128]{1,0:T(8,128)S(1)} %pad_maximum_fusion), channel_id=1, source_target_pairs={{8,16},{16,8},{24,32},{32,24},{40,48},{48,40},{56,64},{64,56},{72,... | collective-permute-start | bytes 98312 | tf_op jit(solution)/shard_map/ppermute | solution.py:436
  28.4 0.5 early_second.1
  28.9 1.1 %collective-permute-done.8.outer = f32[64,128]{1,0:T(8,128)S(1)} collective-permute-done((f32[64,128]{1,0:T(8,128)S(1)}, f32[64,128]{1,0:T(8,128)S(1)}, u32[]{:S(2)}, u32[]{:S(2)}) %collective-permute-start.8) | collective-permute-done | bytes 32800 | tf_op jit(solution)/shard_map/ppermute | solution.py:436
  30.0 0.3 middle_second.1
  30.3 0.1 collective-permute-start.9
  30.4 0.9 %outer_second.1 = (f32[8,128]{1,0:T(8,128)S(1)}, f32[96,128]{1,0:T(8,128)S(1)}) custom-call(s32[1]{0:T(128)} %bitcast.parity, f32[48,128]{1,0:T(8,128)S(1)} %fusion.1.frame, f32[48,128]{1,0:T(8,128)S(1)} %fusion.other, f32[64,128]{1,0:T(8,128)S(1)} %collective-permute-done.8.outer, f32[72,128]{1,0:T(8,128)S(1)} %collective-permute-done.5.right, ...), custom_call_target="tpu_custom_call" | custom-call | tf_op jit(solution)/shard_map/outer_second/pallas_call | solution.py:359
  31.3 0.2 collective-permute-done.9.rho_other
  31.6 0.6 %force_second.1 = (f32[8,128]{1,0:T(8,128)S(1)}, f32[8,128]{1,0:T(8,128)S(1)}, f32[4,128]{1,0:T(4,128)S(1)}, f32[128,128]{1,0:T(8,128)S(1)}) custom-call(s32[1]{0:T(128)} %bitcast.parity, s32[8,128]{1,0:T(8,128)S(1)} %get-tuple-element.33.home, f32[48,128]{1,0:T(8,128)S(1)} %fusion.1.frame, f32[8,128]{1,0:T(8,128)S(1)} %get-tuple-element.50.rho_outer, ...), custom_call_target="tpu_custom_call" | custom-call | tf_op jit(solution)/shard_map/force_second/pallas_call | solution.py:359
  32.2 19.9 %all_to_all.11 = f32[128,1,128]{2,1,0:T(1,128)S(1)} all-to-all(f32[128,1,128]{2,1,0:T(1,128)S(1)} %bitcast.47), channel_id=1, replica_groups=mesh['depth'=16,'azim'=8] {'depth','azim'}, dimensions={0} | all-to-all | bytes 131072 | tf_op jit(solution)/shard_map/all_to_all | solution.py:460
  52.1 0.8 %soil.1 = (f32[4,16,128]{2,1,0:T(8,128)}, f32[8,128]{1,0:T(8,128)}, f32[8,128]{1,0:T(8,128)}, f32[4,128]{1,0:T(4,128)}) custom-call(f32[128,128]{1,0:T(8,128)S(1)} %bitcast.46, f32[10,16,128]{2,1,0:T(8,128)S(1)} %get-tuple-element.54.soil, f32[8,128]{1,0:T(8,128)S(1)} %get-tuple-element.55.pos, f32[8,128]{1,0:T(8,128)S(1)} %get-tuple-element.56.vel, ...), custom_call_target="tpu_custom_call" | custom-call | tf_op jit(solution)/shard_map/soil/pallas_call | solution.py:461
  (16 shorter events, 0.1 us)
Async XLA Ops:
  1.5 9.5 %collective-permute-start = (f32[96,128]{1,0:T(8,128)S(1)}, f32[96,128]{1,0:T(8,128)S(1)}, u32[]{:S(2)}, u32[]{:S(2)}) collective-permute-start(f32[96,128]{1,0:T(8,128)S(1)} %get-tuple-element.34.send), channel_id=1, source_target_pairs={{0,1},{1,2},{2,3},{3,4},{4,5},{5,6},{6,7},{7,0},{8,9},{9,10},{10,1... | collective-permute-start | bytes 147464 | tf_op jit(solution)/shard_map/ppermute | solution.py:403
  3.7 7.3 %collective-permute-start.1 = (f32[24,128]{1,0:T(8,128)S(1)}, f32[24,128]{1,0:T(8,128)S(1)}, u32[]{:S(2)}, u32[]{:S(2)}) collective-permute-start(f32[24,128]{1,0:T(8,128)S(1)} %get-tuple-element.35), channel_id=1, source_target_pairs={{0,9},{1,10},{2,11},{3,12},{4,13},{5,14},{6,15},{7,8},{8,1},{9,2},... | collective-permute-start | bytes 36872 | tf_op jit(solution)/shard_map/ppermute | solution.py:404
  5.7 5.3 %collective-permute-start.2 = (f32[24,128]{1,0:T(8,128)S(1)}, f32[24,128]{1,0:T(8,128)S(1)}, u32[]{:S(2)}, u32[]{:S(2)}) collective-permute-start(f32[24,128]{1,0:T(8,128)S(1)} %get-tuple-element.35), channel_id=1, source_target_pairs={{0,8},{8,0},{16,24},{24,16},{32,40},{40,32},{48,56},{56,48},{64,72... | collective-permute-start | bytes 36872 | tf_op jit(solution)/shard_map/ppermute | solution.py:377
  11.1 6.8 %collective-permute-start.3 = (f32[232,128]{1,0:T(8,128)S(1)}, f32[232,128]{1,0:T(8,128)S(1)}, u32[]{:S(2)}, u32[]{:S(2)}) collective-permute-start(f32[232,128]{1,0:T(8,128)S(1)} %slice_dynamic-update-slice_fusion), channel_id=1, source_target_pairs={{8,16},{16,8},{24,32},{32,24},{40,48},{48,40},{56,64},{64,56},{72,... | collective-permute-start | bytes 356360 | tf_op jit(solution)/shard_map/ppermute | solution.py:409
  18.2 1.2 %collective-permute-start.4 = (f32[8,128]{1,0:T(8,128)S(1)}, f32[8,128]{1,0:T(8,128)S(1)}, u32[]{:S(2)}, u32[]{:S(2)}) collective-permute-start(f32[8,128]{1,0:T(8,128)S(1)} %get-tuple-element.40.after.rho_own), channel_id=1, source_target_pairs={{0,8},{8,0},{16,24},{24,16},{32,40},{40,32},{48,56},{56,48},{64,72... | collective-permute-start | bytes 12296 | tf_op jit(solution)/shard_map/ppermute | solution.py:377
  19.8 4.3 %collective-permute-start.5 = (f32[72,128]{1,0:T(8,128)S(1)}, f32[72,128]{1,0:T(8,128)S(1)}, u32[]{:S(2)}, u32[]{:S(2)}) collective-permute-start(f32[72,128]{1,0:T(8,128)S(1)} %get-tuple-element.43), channel_id=1, source_target_pairs={{0,7},{1,0},{2,1},{3,2},{4,3},{5,4},{6,5},{7,6},{8,15},{9,8},{10,9... | collective-permute-start | bytes 110600 | tf_op jit(solution)/shard_map/ppermute | solution.py:430
  20.8 3.3 %collective-permute-start.6 = (f32[24,128]{1,0:T(8,128)S(1)}, f32[24,128]{1,0:T(8,128)S(1)}, u32[]{:S(2)}, u32[]{:S(2)}) collective-permute-start(f32[24,128]{1,0:T(8,128)S(1)} %get-tuple-element.44), channel_id=1, source_target_pairs={{0,15},{1,8},{2,9},{3,10},{4,11},{5,12},{6,13},{7,14},{8,7},{9,0},... | collective-permute-start | bytes 36872 | tf_op jit(solution)/shard_map/ppermute | solution.py:431
  22.0 2.1 %collective-permute-start.7 = (f32[24,128]{1,0:T(8,128)S(1)}, f32[24,128]{1,0:T(8,128)S(1)}, u32[]{:S(2)}, u32[]{:S(2)}) collective-permute-start(f32[24,128]{1,0:T(8,128)S(1)} %get-tuple-element.44), channel_id=1, source_target_pairs={{0,8},{8,0},{16,24},{24,16},{32,40},{40,32},{48,56},{56,48},{64,72... | collective-permute-start | bytes 36872 | tf_op jit(solution)/shard_map/ppermute | solution.py:377
  24.1 5.8 %collective-permute-start.8 = (f32[64,128]{1,0:T(8,128)S(1)}, f32[64,128]{1,0:T(8,128)S(1)}, u32[]{:S(2)}, u32[]{:S(2)}) collective-permute-start(f32[64,128]{1,0:T(8,128)S(1)} %pad_maximum_fusion), channel_id=1, source_target_pairs={{8,16},{16,8},{24,32},{32,24},{40,48},{48,40},{56,64},{64,56},{72,... | collective-permute-start | bytes 98312 | tf_op jit(solution)/shard_map/ppermute | solution.py:436
  30.3 1.2 %collective-permute-start.9 = (f32[8,128]{1,0:T(8,128)S(1)}, f32[8,128]{1,0:T(8,128)S(1)}, u32[]{:S(2)}, u32[]{:S(2)}) collective-permute-start(f32[8,128]{1,0:T(8,128)S(1)} %get-tuple-element.49.after.rho_own), channel_id=1, source_target_pairs={{0,8},{8,0},{16,24},{24,16},{32,40},{40,32},{48,56},{56,48},{64,72... | collective-permute-start | bytes 12296 | tf_op jit(solution)/shard_map/ppermute | solution.py:377

commit v11 on v9

--- a/solution.py
+++ b/solution.py
@@ -229,8 +229,11 @@
     return [(left, HALF + 2 * NB), (first, 0)] + [(send, HALF + NB * c) for c in range(3)] + [(right, HALF + NB)]
 
 
-def early_second_kernel(parity, frame, other, right, left, first, send, out):
+def early_second_kernel(parity, frame, other, right, left, first, send, home, out, owners):
     early(parity, {0: frame, 1: other}, lists_second(right, left, first, send), out)
+    devices = lax.broadcasted_iota(jnp.int32, (S, S), 0)
+    for c in range(CELLS):
+        owners[:, S * c : S * (c + 1)] = (devices == home[c : c + 1, :]).astype(jnp.bfloat16)
 
 
 def middle_second_kernel(parity, frame, outer, right, left, first, send, gathered, rho, pair):
@@ -245,13 +248,12 @@
 
 
 def force_second_kernel(
-    parity, home, frame, rho_outer, rho_own, rho_other, first, send, pair, dragged, pos_out, vel_out, rho_out, part
+    parity, home, frame, rho_outer, rho_own, rho_other, first, send, pair, dragged, owners, pos_out, vel_out, rho_out, part
 ):
     numbers = numbers_of(parity)
     lists = [(first, 0), (send, HALF), (send, HALF + NB), (send, HALF + 2 * NB)]
-    devices = lax.broadcasted_iota(jnp.int32, (S, S), 0)
     shells = lax.broadcasted_iota(jnp.int32, (16, S), 0)
-    owners, shares = [], []
+    shares = [[], [], []]
     for c in range(CELLS):
         (x, y, m, vx, vy, live), rho = force(
             c, numbers, frame, {-1: rho_outer, 0: rho_own, 1: rho_other}, lists[c], pair, dragged
@@ -262,21 +264,22 @@
         vel_out[CELLS + c : CELLS + c + 1, :] = vy
         rho_out[c : c + 1, :] = rho
         loads = (m * vx, m * vy, m * (sound_sq * (rho - 1.0)), 0.5 * m * (vx * vx + vy * vy))
-        owner = (devices == home[c : c + 1, :]).astype(jnp.bfloat16)
         member = shells == home[CELLS + c : CELLS + c + 1, :]
         rest = jnp.concatenate([jnp.where(member, load, 0.0) for load in loads], axis=0)
-        for _ in range(3):
-            some = rest.astype(jnp.bfloat16)
-            owners.append(owner)
-            shares.append(some)
-            rest = rest - some.astype(jnp.float32)
+        for share in shares:
+            share.append(rest.astype(jnp.bfloat16))
+            rest = rest - share[-1].astype(jnp.float32)
+    high, middle, low = [jnp.concatenate(share, axis=1) for share in shares]
+    none = jnp.zeros_like(low)
     total = lax.dot_general(
-        jnp.concatenate(owners, axis=1),
-        jnp.concatenate(shares, axis=1),
+        jnp.concatenate([owners[...], owners[...]], axis=1),
+        jnp.concatenate(
+            [jnp.concatenate(pair_of, axis=1) for pair_of in ((high, low), (none, none), (middle, none), (none, none))], axis=0
+        ),
         (((1,), (1,)), ((), ())),
         preferred_element_type=jnp.float32,
     )
-    part[...] = jnp.concatenate([total, jnp.zeros((S, S - 64), jnp.float32)], axis=1)
+    part[...] = total[:, :S] + total[:, S:]
 
 
 def soil_kernel(arrived, soil, pos, vel, rho, stress_out, pos_out, vel_out, rho_out):
@@ -355,7 +358,7 @@
     def call(kernel, name, shapes, *args):
         return pl.pallas_call(
             kernel,
-            out_shape=tuple(kept(n) for n in shapes),
+            out_shape=tuple(kept(n) if isinstance(n, int) else n for n in shapes),
             in_specs=[SM] + [VM] * len(args),
             out_specs=(VM,) * len(shapes),
             name=name,
@@ -433,8 +436,11 @@
     frame = merged(mid, right)
     other = merged(beside, across)
     beyond = lax.ppermute(jnp.concatenate([frame[:SENT], other[:PLACE]], axis=0), "depth", facing)
-    (gathered,) = call(
-        early_second_kernel, "early_second", (RING * NT * EARLY,), frame, other, right, left, first, send
+    gathered, owners = call(
+        early_second_kernel,
+        "early_second",
+        (RING * NT * EARLY, pltpu.VMEM((S, CELLS * S), jnp.bfloat16)),
+        frame, other, right, left, first, send, home,
     )
     rho_own, pair = call(
         middle_second_kernel, "middle_second", (WIDE, tiles * PAIR), frame, beyond, right, left, first, send, gathered
@@ -450,7 +456,7 @@
         force_second_kernel,
         "force_second",
         (2 * CELLS, 2 * CELLS, CELLS, S),
-        home, frame, rho_outer, rho_own, rho_other, first, send, pair, dragged,
+        home, frame, rho_outer, rho_own, rho_other, first, send, pair, dragged, owners,
     )
 
     arrived = lax.all_to_all(part, ("depth", "azim"), split_axis=0, concat_axis=0, tiled=True)

time: 53.1 us -> 53.1 us (level)
  no operation moved by 1% of the time
where the time goes in v11:
time: 53.1 us; the launch traced here: 52.9 us
  blocking collectives  19.9 us (37%)
  starting transfers between devices  14.6 us (27%)
  waiting for transfers between devices  10.6 us (20%)
  Pallas kernels  6.79 us (13%)
  between operations  0.82 us (2%)
    all_to_all x1, blocking collectives, local(): lax.all_to_all(part, ('depth', 'azim'), split_axis=0, concat_axis=0, tile...  19.9 us
    ppermute x1, waiting for transfers between devices, local(): across = lax.ppermute(half, ('depth', 'azim'), crossing(1))  5.29 us
    ppermute x1, starting transfers between devices, local(): lax.ppermute(jnp.concatenate([frame[:SENT], other[:PLACE]], axis=0), 'dep...  4.25 us
    pallas_call x7, Pallas kernels, call(): pl.pallas_call(kernel, out_shape=tuple((kept(n) if isinstance(n, int) els...  3.88 us
    ppermute x1, starting transfers between devices, local(): lax.ppermute(jnp.concatenate([frame[:SENT], other[:PLACE], left[HALF:], f...  3.77 us
    ppermute x1, starting transfers between devices, local(): left = lax.ppermute(send, 'azim', toward_right)  2.11 us
    ppermute x1, waiting for transfers between devices, local(): across = lax.ppermute(half, ('depth', 'azim'), crossing(-1))  2.07 us
    ppermute x1, starting transfers between devices, local(): across = lax.ppermute(half, ('depth', 'azim'), crossing(1))  2.05 us
  transfers between devices with their start and end apart: 10, of which 6 were waited for; matrix products, arithmetic and copies ran while one was open for 0% of the time, Pallas kernels for 7%

profile of v11, /device:TPU:1, one launch (start us, length us, event | category | flops | bytes accessed | tf_op | source)
XLA Modules:
  0.0 52.9 jit_solution(17895161636773356372)
XLA Ops:
  0.6 0.9 %pack.1 = (f32[96,128]{1,0:T(8,128)S(1)}, f32[24,128]{1,0:T(8,128)S(1)}, f32[24,128]{1,0:T(8,128)S(1)}) custom-call(s32[1,4]{1,0:T(1,128)} %count.1, f32[8,128]{1,0:T(8,128)} %bitcast.65, f32[8,128]{1,0:T(8,128)} %bitcast.66, f32[4,128]{1,0:T(4,128)} %bitcast.69, s32[96,128]{1,0:T(8,128)} %bitcast.56), custom_call_target="tpu_custom_call" | custom-call | tf_op jit(solution)/shard_map/pack/pallas_call | solution.py:379
  1.5 2.1 %collective-permute-start = (f32[96,128]{1,0:T(8,128)S(1)}, f32[96,128]{1,0:T(8,128)S(1)}, u32[]{:S(2)}, u32[]{:S(2)}) collective-permute-start(f32[96,128]{1,0:T(8,128)S(1)} %get-tuple-element.34.send), channel_id=1, source_target_pairs={{0,1},{1,2},{2,3},{3,4},{4,5},{5,6},{6,7},{7,0},{8,9},{9,10},{10,1... | collective-permute-start | bytes 147464 | tf_op jit(solution)/shard_map/ppermute | solution.py:396
  3.6 2.1 %collective-permute-start.1 = (f32[24,128]{1,0:T(8,128)S(1)}, f32[24,128]{1,0:T(8,128)S(1)}, u32[]{:S(2)}, u32[]{:S(2)}) collective-permute-start(f32[24,128]{1,0:T(8,128)S(1)} %get-tuple-element.35), channel_id=1, source_target_pairs={{0,9},{1,10},{2,11},{3,12},{4,13},{5,14},{6,15},{7,8},{8,1},{9,2},... | collective-permute-start | bytes 36872 | tf_op jit(solution)/shard_map/ppermute | solution.py:397
  5.7 0.0 collective-permute-start.2
  5.7 5.3 %collective-permute-done.1 = f32[24,128]{1,0:T(8,128)S(1)} collective-permute-done((f32[24,128]{1,0:T(8,128)S(1)}, f32[24,128]{1,0:T(8,128)S(1)}, u32[]{:S(2)}, u32[]{:S(2)}) %collective-permute-start.1) | collective-permute-done | bytes 12320 | tf_op jit(solution)/shard_map/ppermute | solution.py:397
  11.0 0.0 collective-permute-done.left
  11.0 0.0 collective-permute-done.2
  11.0 3.8 %collective-permute-start.3 = (f32[232,128]{1,0:T(8,128)S(1)}, f32[232,128]{1,0:T(8,128)S(1)}, u32[]{:S(2)}, u32[]{:S(2)}) collective-permute-start(f32[232,128]{1,0:T(8,128)S(1)} %slice_dynamic-update-slice_fusion), channel_id=1, source_target_pairs={{8,16},{16,8},{24,32},{32,24},{40,48},{48,40},{56,64},{64,56},{72,... | collective-permute-start | bytes 356360 | tf_op jit(solution)/shard_map/ppermute | solution.py:402
  14.9 1.3 %early_first.1 = (f32[432,128]{1,0:T(8,128)S(1)}, s32[8,128]{1,0:T(8,128)S(1)}, f32[10,16,128]{2,1,0:T(8,128)S(1)}) custom-call(s32[1]{0:T(128)} %bitcast.parity, f32[48,128]{1,0:T(8,128)S(1)} %fusion.3.frame, f32[48,128]{1,0:T(8,128)S(1)} %fusion.2.other, f32[96,128]{1,0:T(8,128)S(1)} %collective-permute-done.left, f32[24,128]{1,0:T(8,128)S(1)} %get-tuple-element.38.first, ...), custom_call_target="tpu_custom_call" | custom-call | tf_op jit(solution)/shard_map/early_first/pallas_call | solution.py:407
  16.2 1.7 %collective-permute-done.3.outer.before = f32[232,128]{1,0:T(8,128)S(1)} collective-permute-done((f32[232,128]{1,0:T(8,128)S(1)}, f32[232,128]{1,0:T(8,128)S(1)}, u32[]{:S(2)}, u32[]{:S(2)}) %collective-permute-start.3) | collective-permute-done | bytes 118816 | tf_op jit(solution)/shard_map/ppermute | solution.py:402
  17.9 0.3 middle_first.1
  18.2 0.1 collective-permute-start.4
  18.3 0.9 %outer_first.1 = (f32[8,128]{1,0:T(8,128)S(1)}, f32[96,128]{1,0:T(8,128)S(1)}) custom-call(s32[1]{0:T(128)} %bitcast.parity, f32[48,128]{1,0:T(8,128)S(1)} %fusion.3.frame, f32[48,128]{1,0:T(8,128)S(1)} %fusion.2.other, f32[232,128]{1,0:T(8,128)S(1)} %collective-permute-done.3.outer.before, f32[96,128]{1,0:T(8,128)S(1)} %collective-permute-done.left, ...), custom_call_target="tpu_custom_call" | custom-call | tf_op jit(solution)/shard_map/outer_first/pallas_call | solution.py:359
  19.2 0.2 collective-permute-done.4.rho_other
  19.4 0.3 force_first.1
  19.7 1.0 %collective-permute-start.5 = (f32[72,128]{1,0:T(8,128)S(1)}, f32[72,128]{1,0:T(8,128)S(1)}, u32[]{:S(2)}, u32[]{:S(2)}) collective-permute-start(f32[72,128]{1,0:T(8,128)S(1)} %get-tuple-element.45), channel_id=1, source_target_pairs={{0,7},{1,0},{2,1},{3,2},{4,3},{5,4},{6,5},{7,6},{8,15},{9,8},{10,9... | collective-permute-start | bytes 110600 | tf_op jit(solution)/shard_map/ppermute | solution.py:432
  20.7 1.2 %collective-permute-start.6 = (f32[24,128]{1,0:T(8,128)S(1)}, f32[24,128]{1,0:T(8,128)S(1)}, u32[]{:S(2)}, u32[]{:S(2)}) collective-permute-start(f32[24,128]{1,0:T(8,128)S(1)} %get-tuple-element.46), channel_id=1, source_target_pairs={{0,15},{1,8},{2,9},{3,10},{4,11},{5,12},{6,13},{7,14},{8,7},{9,0},... | collective-permute-start | bytes 36872 | tf_op jit(solution)/shard_map/ppermute | solution.py:433
  22.0 0.0 collective-permute-start.7
  22.0 2.1 %collective-permute-done.6 = f32[24,128]{1,0:T(8,128)S(1)} collective-permute-done((f32[24,128]{1,0:T(8,128)S(1)}, f32[24,128]{1,0:T(8,128)S(1)}, u32[]{:S(2)}, u32[]{:S(2)}) %collective-permute-start.6) | collective-permute-done | bytes 12320 | tf_op jit(solution)/shard_map/ppermute | solution.py:433
  24.0 0.0 collective-permute-done.5.right
  24.0 0.0 collective-permute-done.7
  24.1 4.2 %collective-permute-start.8 = (f32[64,128]{1,0:T(8,128)S(1)}, f32[64,128]{1,0:T(8,128)S(1)}, u32[]{:S(2)}, u32[]{:S(2)}) collective-permute-start(f32[64,128]{1,0:T(8,128)S(1)} %pad_maximum_fusion), channel_id=1, source_target_pairs={{8,16},{16,8},{24,32},{32,24},{40,48},{48,40},{56,64},{64,56},{72,... | collective-permute-start | bytes 98312 | tf_op jit(solution)/shard_map/ppermute | solution.py:438
  28.4 0.5 early_second.1
  28.9 1.1 %collective-permute-done.8.outer = f32[64,128]{1,0:T(8,128)S(1)} collective-permute-done((f32[64,128]{1,0:T(8,128)S(1)}, f32[64,128]{1,0:T(8,128)S(1)}, u32[]{:S(2)}, u32[]{:S(2)}) %collective-permute-start.8) | collective-permute-done | bytes 32800 | tf_op jit(solution)/shard_map/ppermute | solution.py:438
  29.9 0.3 middle_second.1
  30.3 0.1 collective-permute-start.9
  30.4 0.9 %outer_second.1 = (f32[8,128]{1,0:T(8,128)S(1)}, f32[96,128]{1,0:T(8,128)S(1)}) custom-call(s32[1]{0:T(128)} %bitcast.parity, f32[48,128]{1,0:T(8,128)S(1)} %fusion.1.frame, f32[48,128]{1,0:T(8,128)S(1)} %fusion.other, f32[64,128]{1,0:T(8,128)S(1)} %collective-permute-done.8.outer, f32[72,128]{1,0:T(8,128)S(1)} %collective-permute-done.5.right, ...), custom_call_target="tpu_custom_call" | custom-call | tf_op jit(solution)/shard_map/outer_second/pallas_call | solution.py:359
  31.3 0.2 collective-permute-done.9.rho_other
  31.5 0.6 %force_second.1 = (f32[8,128]{1,0:T(8,128)S(1)}, f32[8,128]{1,0:T(8,128)S(1)}, f32[4,128]{1,0:T(4,128)S(1)}, f32[128,128]{1,0:T(8,128)S(1)}) custom-call(s32[1]{0:T(128)} %bitcast.parity, s32[8,128]{1,0:T(8,128)S(1)} %get-tuple-element.39.home, f32[48,128]{1,0:T(8,128)S(1)} %fusion.1.frame, f32[8,128]{1,0:T(8,128)S(1)} %get-tuple-element.52.rho_outer, ...), custom_call_target="tpu_custom_call" | custom-call | tf_op jit(solution)/shard_map/force_second/pallas_call | solution.py:359
  32.2 19.9 %all_to_all.11 = f32[128,1,128]{2,1,0:T(1,128)S(1)} all-to-all(f32[128,1,128]{2,1,0:T(1,128)S(1)} %bitcast.47), channel_id=1, replica_groups=mesh['depth'=16,'azim'=8] {'depth','azim'}, dimensions={0} | all-to-all | bytes 131072 | tf_op jit(solution)/shard_map/all_to_all | solution.py:462
  52.1 0.8 %soil.1 = (f32[4,16,128]{2,1,0:T(8,128)}, f32[8,128]{1,0:T(8,128)}, f32[8,128]{1,0:T(8,128)}, f32[4,128]{1,0:T(4,128)}) custom-call(f32[128,128]{1,0:T(8,128)S(1)} %bitcast.46, f32[10,16,128]{2,1,0:T(8,128)S(1)} %get-tuple-element.56.soil, f32[8,128]{1,0:T(8,128)S(1)} %get-tuple-element.57.pos, f32[8,128]{1,0:T(8,128)S(1)} %get-tuple-element.58.vel, ...), custom_call_target="tpu_custom_call" | custom-call | tf_op jit(solution)/shard_map/soil/pallas_call | solution.py:463
  (16 shorter events, 0.1 us)
Async XLA Ops:
  1.5 9.5 %collective-permute-start = (f32[96,128]{1,0:T(8,128)S(1)}, f32[96,128]{1,0:T(8,128)S(1)}, u32[]{:S(2)}, u32[]{:S(2)}) collective-permute-start(f32[96,128]{1,0:T(8,128)S(1)} %get-tuple-element.34.send), channel_id=1, source_target_pairs={{0,1},{1,2},{2,3},{3,4},{4,5},{5,6},{6,7},{7,0},{8,9},{9,10},{10,1... | collective-permute-start | bytes 147464 | tf_op jit(solution)/shard_map/ppermute | solution.py:396
  3.6 7.3 %collective-permute-start.1 = (f32[24,128]{1,0:T(8,128)S(1)}, f32[24,128]{1,0:T(8,128)S(1)}, u32[]{:S(2)}, u32[]{:S(2)}) collective-permute-start(f32[24,128]{1,0:T(8,128)S(1)} %get-tuple-element.35), channel_id=1, source_target_pairs={{0,9},{1,10},{2,11},{3,12},{4,13},{5,14},{6,15},{7,8},{8,1},{9,2},... | collective-permute-start | bytes 36872 | tf_op jit(solution)/shard_map/ppermute | solution.py:397
  5.7 5.3 %collective-permute-start.2 = (f32[24,128]{1,0:T(8,128)S(1)}, f32[24,128]{1,0:T(8,128)S(1)}, u32[]{:S(2)}, u32[]{:S(2)}) collective-permute-start(f32[24,128]{1,0:T(8,128)S(1)} %get-tuple-element.35), channel_id=1, source_target_pairs={{0,8},{8,0},{16,24},{24,16},{32,40},{40,32},{48,56},{56,48},{64,72... | collective-permute-start | bytes 36872 | tf_op jit(solution)/shard_map/ppermute | solution.py:377
  11.0 6.8 %collective-permute-start.3 = (f32[232,128]{1,0:T(8,128)S(1)}, f32[232,128]{1,0:T(8,128)S(1)}, u32[]{:S(2)}, u32[]{:S(2)}) collective-permute-start(f32[232,128]{1,0:T(8,128)S(1)} %slice_dynamic-update-slice_fusion), channel_id=1, source_target_pairs={{8,16},{16,8},{24,32},{32,24},{40,48},{48,40},{56,64},{64,56},{72,... | collective-permute-start | bytes 356360 | tf_op jit(solution)/shard_map/ppermute | solution.py:402
  18.2 1.2 %collective-permute-start.4 = (f32[8,128]{1,0:T(8,128)S(1)}, f32[8,128]{1,0:T(8,128)S(1)}, u32[]{:S(2)}, u32[]{:S(2)}) collective-permute-start(f32[8,128]{1,0:T(8,128)S(1)} %get-tuple-element.42.after.rho_own), channel_id=1, source_target_pairs={{0,8},{8,0},{16,24},{24,16},{32,40},{40,32},{48,56},{56,48},{64,72... | collective-permute-start | bytes 12296 | tf_op jit(solution)/shard_map/ppermute | solution.py:377
  19.7 4.3 %collective-permute-start.5 = (f32[72,128]{1,0:T(8,128)S(1)}, f32[72,128]{1,0:T(8,128)S(1)}, u32[]{:S(2)}, u32[]{:S(2)}) collective-permute-start(f32[72,128]{1,0:T(8,128)S(1)} %get-tuple-element.45), channel_id=1, source_target_pairs={{0,7},{1,0},{2,1},{3,2},{4,3},{5,4},{6,5},{7,6},{8,15},{9,8},{10,9... | collective-permute-start | bytes 110600 | tf_op jit(solution)/shard_map/ppermute | solution.py:432
  20.7 3.3 %collective-permute-start.6 = (f32[24,128]{1,0:T(8,128)S(1)}, f32[24,128]{1,0:T(8,128)S(1)}, u32[]{:S(2)}, u32[]{:S(2)}) collective-permute-start(f32[24,128]{1,0:T(8,128)S(1)} %get-tuple-element.46), channel_id=1, source_target_pairs={{0,15},{1,8},{2,9},{3,10},{4,11},{5,12},{6,13},{7,14},{8,7},{9,0},... | collective-permute-start | bytes 36872 | tf_op jit(solution)/shard_map/ppermute | solution.py:433
  22.0 2.1 %collective-permute-start.7 = (f32[24,128]{1,0:T(8,128)S(1)}, f32[24,128]{1,0:T(8,128)S(1)}, u32[]{:S(2)}, u32[]{:S(2)}) collective-permute-start(f32[24,128]{1,0:T(8,128)S(1)} %get-tuple-element.46), channel_id=1, source_target_pairs={{0,8},{8,0},{16,24},{24,16},{32,40},{40,32},{48,56},{56,48},{64,72... | collective-permute-start | bytes 36872 | tf_op jit(solution)/shard_map/ppermute | solution.py:377
  24.1 5.8 %collective-permute-start.8 = (f32[64,128]{1,0:T(8,128)S(1)}, f32[64,128]{1,0:T(8,128)S(1)}, u32[]{:S(2)}, u32[]{:S(2)}) collective-permute-start(f32[64,128]{1,0:T(8,128)S(1)} %pad_maximum_fusion), channel_id=1, source_target_pairs={{8,16},{16,8},{24,32},{32,24},{40,48},{48,40},{56,64},{64,56},{72,... | collective-permute-start | bytes 98312 | tf_op jit(solution)/shard_map/ppermute | solution.py:438
  30.3 1.2 %collective-permute-start.9 = (f32[8,128]{1,0:T(8,128)S(1)}, f32[8,128]{1,0:T(8,128)S(1)}, u32[]{:S(2)}, u32[]{:S(2)}) collective-permute-start(f32[8,128]{1,0:T(8,128)S(1)} %get-tuple-element.51.after.rho_own), channel_id=1, source_target_pairs={{0,8},{8,0},{16,24},{24,16},{32,40},{40,32},{48,56},{56,48},{64,72... | collective-permute-start | bytes 12296 | tf_op jit(solution)/shard_map/ppermute | solution.py:377
